TPU v7x, 32 devices: a whole 2x2x4 slice. The times are simulated.
32 devices in a mesh: dp: 4 (over z), seq: 2 (over core), mp: 4 (over y, x).
Axes of the slice: x: 2, y: 2, z: 4, core: 2. Of those that a mesh axis runs over, the one named last changes fastest.
Arguments:
- frames: bfloat16 [16, 768, 768], P('dp', 'seq'), may hold values from -6 to 6
- cotangent: bfloat16 [16, 768, 768], P('dp', 'seq'), may hold values from -6 to 6
- lengths: int32 [16], P('dp'), may hold values from 256 to 768, as said below
- attn_master: float32 [4, 768, 768], P(None, ('dp', 'seq'), 'mp'), may hold values from -2 to 2
- attn_moment: float32 [4, 768, 768], P(None, ('dp', 'seq'), 'mp'), may hold values from -0.0546875 to 0.0546875
- attn_average: float32 [4, 768, 768], P(None, ('dp', 'seq'), 'mp'), may hold values from -0.21875 to 0.21875
- ffn_master: float32 [2, 768, 3072], P(None, ('dp', 'seq'), 'mp'), may hold values from -2 to 2
- ffn_moment: float32 [2, 768, 3072], P(None, ('dp', 'seq'), 'mp'), may hold values from -0.0546875 to 0.0546875
- ffn_average: float32 [2, 768, 3072], P(None, ('dp', 'seq'), 'mp'), may hold values from -0.21875 to 0.21875
- norm_vecs: float32 [6, 768], replicated, may hold values from -2 to 2
- norm_moment: float32 [6, 768], replicated, may hold values from -0.0546875 to 0.0546875
- norm_average: float32 [6, 768], replicated, may hold values from -3 to 3
- col_bias: float32 [4608], P('mp'), may hold values from -1.5 to 1.5
- col_moment: float32 [4608], P('mp'), may hold values from -0.0546875 to 0.0546875
- col_average: float32 [4608], P('mp'), may hold values from -1.5 to 1.5
- rel_table: float32 [320, 12], P(None, 'mp'), may hold values from -2.5 to 2.5
- rel_moment: float32 [320, 12], P(None, 'mp'), may hold values from -0.0546875 to 0.0546875
- rel_average: float32 [320, 12], P(None, 'mp'), may hold values from -2.5 to 2.5
- dec_frames: bfloat16 [16, 256, 768], P('dp', 'seq'), may hold values from -6 to 6
- dec_cotangent: bfloat16 [16, 256, 768], P('dp', 'seq'), may hold values from -6 to 6
- text_lengths: int32 [16], P('dp'), may hold values from 64 to 256, as said below
- dec_attn_master: float32 [8, 768, 768], P(None, ('dp', 'seq'), 'mp'), may hold values from -2 to 2
- dec_attn_moment: float32 [8, 768, 768], P(None, ('dp', 'seq'), 'mp'), may hold values from -0.0546875 to 0.0546875
- dec_attn_average: float32 [8, 768, 768], P(None, ('dp', 'seq'), 'mp'), may hold values from -0.21875 to 0.21875
- dec_ffn_master: float32 [2, 768, 3072], P(None, ('dp', 'seq'), 'mp'), may hold values from -2 to 2
- dec_ffn_moment: float32 [2, 768, 3072], P(None, ('dp', 'seq'), 'mp'), may hold values from -0.0546875 to 0.0546875
- dec_ffn_average: float32 [2, 768, 3072], P(None, ('dp', 'seq'), 'mp'), may hold values from -0.21875 to 0.21875
- dec_norm_vecs: float32 [9, 768], replicated, may hold values from -2 to 2
- dec_norm_moment: float32 [9, 768], replicated, may hold values from -0.0546875 to 0.0546875
- dec_norm_average: float32 [9, 768], replicated, may hold values from -3 to 3
- dec_col_bias: float32 [6144], P('mp'), may hold values from -1.5 to 1.5
- dec_col_moment: float32 [6144], P('mp'), may hold values from -0.0546875 to 0.0546875
- dec_col_average: float32 [6144], P('mp'), may hold values from -1.5 to 1.5
Outputs:
- output: bfloat16 [16, 768, 768], P('dp', 'seq')
- input_grad: bfloat16 [16, 768, 768], P('dp', 'seq')
- attn_grad: float32 [4, 768, 768], P(None, ('dp', 'seq'), 'mp')
- ffn_grad: float32 [2, 768, 3072], P(None, ('dp', 'seq'), 'mp')
- attn_master_new: float32 [4, 768, 768], P(None, ('dp', 'seq'), 'mp')
- attn_moment_new: float32 [4, 768, 768], P(None, ('dp', 'seq'), 'mp')
- attn_average_new: float32 [4, 768, 768], P(None, ('dp', 'seq'), 'mp')
- attn_copy: bfloat16 [4, 768, 768], P(None, ('dp', 'seq'), 'mp')
- ffn_master_new: float32 [2, 768, 3072], P(None, ('dp', 'seq'), 'mp')
- ffn_moment_new: float32 [2, 768, 3072], P(None, ('dp', 'seq'), 'mp')
- ffn_average_new: float32 [2, 768, 3072], P(None, ('dp', 'seq'), 'mp')
- ffn_copy: bfloat16 [2, 768, 3072], P(None, ('dp', 'seq'), 'mp')
- norm_vecs_new: float32 [6, 768], replicated
- norm_moment_new: float32 [6, 768], replicated
- norm_average_new: float32 [6, 768], replicated
- col_bias_new: float32 [4608], P('mp')
- col_moment_new: float32 [4608], P('mp')
- col_average_new: float32 [4608], P('mp')
- rel_table_new: float32 [320, 12], P(None, 'mp')
- rel_moment_new: float32 [320, 12], P(None, 'mp')
- rel_average_new: float32 [320, 12], P(None, 'mp')
- dec_output: bfloat16 [16, 256, 768], P('dp', 'seq')
- dec_input_grad: bfloat16 [16, 256, 768], P('dp', 'seq')
- dec_attn_grad: float32 [8, 768, 768], P(None, ('dp', 'seq'), 'mp')
- dec_ffn_grad: float32 [2, 768, 3072], P(None, ('dp', 'seq'), 'mp')
- dec_attn_master_new: float32 [8, 768, 768], P(None, ('dp', 'seq'), 'mp')
- dec_attn_moment_new: float32 [8, 768, 768], P(None, ('dp', 'seq'), 'mp')
- dec_attn_average_new: float32 [8, 768, 768], P(None, ('dp', 'seq'), 'mp')
- dec_attn_copy: bfloat16 [8, 768, 768], P(None, ('dp', 'seq'), 'mp')
- dec_ffn_master_new: float32 [2, 768, 3072], P(None, ('dp', 'seq'), 'mp')
- dec_ffn_moment_new: float32 [2, 768, 3072], P(None, ('dp', 'seq'), 'mp')
- dec_ffn_average_new: float32 [2, 768, 3072], P(None, ('dp', 'seq'), 'mp')
- dec_ffn_copy: bfloat16 [2, 768, 3072], P(None, ('dp', 'seq'), 'mp')
- dec_norm_vecs_new: float32 [9, 768], replicated
- dec_norm_moment_new: float32 [9, 768], replicated
- dec_norm_average_new: float32 [9, 768], replicated
- dec_col_bias_new: float32 [6144], P('mp')
- dec_col_moment_new: float32 [6144], P('mp')
- dec_col_average_new: float32 [6144], P('mp')
Inputs may be any that keep to these rules, and one draw needn't show every extreme that they name: `lengths`: each utterance has 256, 512 or 768 valid frames; the first has 768. `text_lengths`: the first utterance's transcript fills all 256 slots.
All inputs are finite; a program needn't handle non-finite values.
Results may differ from a plain program's by a relative error of at most 0.025.
Values may be sent and summed in bfloat16 or wider, within the bound.
No kernel may reach another device: no remote copies, remote signals or barrier semaphores. Data moves between devices by JAX's collectives and lax.ppermute only.
A program may use at most 320 MiB of HBM per device.

v0:
```python
import jax
import jax.numpy as jnp
from jax import lax
from jax.sharding import PartitionSpec as P

EPSILON = 1e-05
MOMENTUM = 0.9
AVERAGING = 0.75
MATRIX_RATE = 0.02
VECTOR_RATE = 0.2
MASK_VALUE = -1e30
ROOT_HALF = 0.7071067811865476
INV_ROOT_TAU = 0.3989422804014327
HIGHEST_PRECISION = lax.Precision.HIGHEST


def for_sending(x):
    return jax.tree.map(lambda a: a.astype(jnp.bfloat16) if a.dtype == jnp.float32 else a, x)


def contract_rows(left_mat, right_mat):
    return lax.dot_general(
        left_mat, right_mat, (((0,), (0,)), ((), ())), preferred_element_type=jnp.float32
    )


def contract_cols(left_mat, right_mat):
    return lax.dot_general(
        left_mat, right_mat, (((1,), (1,)), ((), ())), preferred_element_type=jnp.float32
    )


def project(rows, matrix):
    return jnp.dot(rows, matrix, preferred_element_type=jnp.float32)


def gelu_slope(gate_in):
    return (
        0.5 * (1.0 + lax.erf(gate_in * ROOT_HALF))
        + gate_in * jnp.exp(-0.5 * gate_in * gate_in) * INV_ROOT_TAU
    )


def norm_forward(values, gain_vec, offset):
    center = values - jnp.mean(values, axis=-1, keepdims=True)
    inv_std = lax.rsqrt(jnp.mean(center * center, axis=-1, keepdims=True) + EPSILON)
    normed = center * inv_std
    return (normed * gain_vec + offset, normed, inv_std)


def norm_backward(upstream, normed, inv_std, gain_vec):
    scaled = upstream * gain_vec
    inner_term = (
        scaled
        - jnp.mean(scaled, axis=-1, keepdims=True)
        - normed * jnp.mean(scaled * normed, axis=-1, keepdims=True)
    )
    return (inv_std * inner_term, jnp.sum(upstream * normed, axis=0), jnp.sum(upstream, axis=0))


def spread_diagonals(diag_vals, row_total, col_total):
    lead = diag_vals.shape[0]
    width = row_total + col_total - 1
    tiled = jnp.broadcast_to(diag_vals[:, None, :], (lead, row_total, width)).reshape(
        lead, row_total * width
    )
    padded = jnp.pad(tiled, ((0, 0), (0, row_total)))
    shaped = padded.reshape(lead, row_total, width + 1)[:, :, :col_total]
    return shaped[:, ::-1, :]


def collect_diagonals(grid):
    lead, row_total, col_total = grid.shape
    width = row_total + col_total - 1
    flipped = grid[:, ::-1, :]
    padded = jnp.pad(flipped, ((0, 0), (0, 0), (0, row_total))).reshape(
        lead, row_total * (width + 1)
    )
    return jnp.sum(padded[:, : row_total * width].reshape(lead, row_total, width), axis=1)


def update(master, moment, average, gradient, step_rate, frame_total):
    mean_grad = gradient / frame_total
    new_moment = MOMENTUM * moment + mean_grad
    new_master = master - step_rate * (mean_grad + MOMENTUM * new_moment)
    new_average = AVERAGING * average + (1.0 - AVERAGING) * new_master
    return (mean_grad, new_master, new_moment, new_average)


def run_blocks(block_fn, pieces, batched):
    if batched:
        return jax.vmap(block_fn)(pieces)
    return lax.map(block_fn, pieces)


def other_half(key_rows, value_rows, piece_shape):
    return (
        lax.all_gather(key_rows.reshape(piece_shape), "seq", axis=1, tiled=True),
        lax.all_gather(value_rows.reshape(piece_shape), "seq", axis=1, tiled=True),
    )


def back_half(key_part, value_part):
    return (
        lax.psum_scatter(
            key_part.astype(jnp.bfloat16), "seq", scatter_dimension=1, tiled=True
        ).astype(jnp.float32),
        lax.psum_scatter(
            value_part.astype(jnp.bfloat16), "seq", scatter_dimension=1, tiled=True
        ).astype(jnp.float32),
    )


def head_sum(partial_value):
    return lax.psum(partial_value.astype(jnp.bfloat16), "mp").astype(jnp.float32)


def unit_sum(partial_value):
    return lax.psum(partial_value.astype(jnp.bfloat16), "mp").astype(jnp.float32)


def unit_back(partial_value):
    return lax.psum(partial_value.astype(jnp.bfloat16), "mp").astype(jnp.float32)


def head_back(partial_value):
    return jax.tree.map(
        lambda part: part.astype(jnp.float32), lax.psum(for_sending(partial_value), "mp")
    )


def local(
    frames,
    cotangent,
    lengths,
    attn_master,
    attn_moment,
    attn_average,
    ffn_master,
    ffn_moment,
    ffn_average,
    norm_vecs,
    norm_moment,
    norm_average,
    col_bias,
    col_moment,
    col_average,
    rel_table,
    rel_moment,
    rel_average,
    dec_frames,
    dec_cotangent,
    text_lengths,
    dec_attn_master,
    dec_attn_moment,
    dec_attn_average,
    dec_ffn_master,
    dec_ffn_moment,
    dec_ffn_average,
    dec_norm_vecs,
    dec_norm_moment,
    dec_norm_average,
    dec_col_bias,
    dec_col_moment,
    dec_col_average,
):
    attn_w, ffn_w, dec_attn_w, dec_ffn_w = (
        lax.all_gather(attn_master.astype(jnp.bfloat16), ("dp", "seq"), axis=1, tiled=True),
        lax.all_gather(ffn_master.astype(jnp.bfloat16), ("dp", "seq"), axis=1, tiled=True),
        lax.all_gather(dec_attn_master.astype(jnp.bfloat16), ("dp", "seq"), axis=1, tiled=True),
        lax.all_gather(dec_ffn_master.astype(jnp.bfloat16), ("dp", "seq"), axis=1, tiled=True),
    )
    utt_count, half_len, model_width = frames.shape
    text_half = dec_frames.shape[1]
    head_cols = attn_w.shape[2]
    bucket_count, head_count = rel_table.shape
    head_size = head_cols // head_count
    max_dist = bucket_count // 2
    full_len = half_len * lax.axis_size("seq")
    text_full = text_half * lax.axis_size("seq")
    row_count = utt_count * half_len
    text_count = utt_count * text_half
    score_scale = head_size ** (-0.5)
    root_frames = float(row_count * lax.axis_size("dp") * lax.axis_size("seq")) ** 0.5
    query_start = lax.axis_index("seq") * half_len
    query_pos = query_start + jnp.arange(half_len, dtype=jnp.int32)
    text_pos = lax.axis_index("seq") * text_half + jnp.arange(text_half, dtype=jnp.int32)
    diag_width = half_len + full_len - 1
    diag_dist = jnp.arange(diag_width, dtype=jnp.int32) - (half_len - 1) - query_start
    diag_bucket = jnp.clip(diag_dist, -max_dist, max_dist - 1) + max_dist
    bucket_onehot = (
        diag_bucket[:, None] == jnp.arange(bucket_count, dtype=jnp.int32)[None, :]
    ).astype(jnp.float32)
    diag_bias = lax.dot_general(
        rel_table,
        bucket_onehot,
        (((0,), (1,)), ((), ())),
        precision=HIGHEST_PRECISION,
        preferred_element_type=jnp.float32,
    )
    rel_bias = spread_diagonals(diag_bias, half_len, full_len)
    piece_shape = (utt_count, half_len, head_cols)
    text_piece = (utt_count, text_half, head_cols)

    def scorer(query_len, key_len, query_places, extra_bias, causal):
        key_places = jnp.arange(key_len, dtype=jnp.int32)

        def scores_of(query_block, key_block, limit_len):
            query_heads = query_block.reshape(query_len, head_count, head_size)
            key_heads = key_block.reshape(key_len, head_count, head_size)
            raw_scores = (
                jnp.einsum(
                    "qhe,khe->hqk", query_heads, key_heads, preferred_element_type=jnp.float32
                )
                * score_scale
            )
            if extra_bias is not None:
                raw_scores = raw_scores + extra_bias
            key_valid = jnp.broadcast_to((key_places < limit_len)[None, :], (query_len, key_len))
            if causal:
                key_valid = key_valid & (key_places[None, :] <= query_places[:, None])
            return jnp.where(key_valid[None], raw_scores, MASK_VALUE)

        return scores_of

    def forward_fn(scores_of, query_len, key_len):

        def attend(pieces):
            query_block, key_block, value_block, limit_len = pieces
            scores = scores_of(query_block, key_block, limit_len)
            row_max = jnp.max(scores, axis=-1, keepdims=True)
            exp_scores = jnp.exp(scores - row_max)
            exp_total = jnp.sum(exp_scores, axis=-1, keepdims=True)
            prob_rows = (exp_scores / exp_total).astype(jnp.bfloat16)
            value_heads = value_block.reshape(key_len, head_count, head_size)
            context = jnp.einsum(
                "hqk,khe->qhe", prob_rows, value_heads, preferred_element_type=jnp.float32
            )
            return (
                context.reshape(query_len, head_cols).astype(jnp.bfloat16),
                (row_max + jnp.log(exp_total))[..., 0],
            )

        return attend

    def backward_fn(scores_of, query_len, key_len, table_fn):

        def attend_back(pieces):
            query_block, key_block, value_block, limit_len, log_row, grad_block = pieces
            scores = scores_of(query_block, key_block, limit_len)
            prob_rows = jnp.exp(scores - log_row[..., None])
            query_heads = query_block.reshape(query_len, head_count, head_size)
            key_heads = key_block.reshape(key_len, head_count, head_size)
            value_heads = value_block.reshape(key_len, head_count, head_size)
            grad_heads = grad_block.reshape(query_len, head_count, head_size)
            prob_grad = jnp.einsum(
                "qhe,khe->hqk", grad_heads, value_heads, preferred_element_type=jnp.float32
            )
            score_grad = (
                prob_rows * (prob_grad - jnp.sum(prob_rows * prob_grad, axis=-1, keepdims=True))
            ).astype(jnp.bfloat16)
            query_grad = (
                (
                    jnp.einsum(
                        "hqk,khe->qhe", score_grad, key_heads, preferred_element_type=jnp.float32
                    )
                    * score_scale
                )
                .reshape(query_len, head_cols)
                .astype(jnp.bfloat16)
            )
            key_grad = (
                jnp.einsum(
                    "hqk,qhe->khe", score_grad, query_heads, preferred_element_type=jnp.float32
                )
                * score_scale
            ).reshape(key_len, head_cols)
            value_grad = jnp.einsum(
                "hqk,qhe->khe",
                prob_rows.astype(jnp.bfloat16),
                grad_heads,
                preferred_element_type=jnp.float32,
            ).reshape(key_len, head_cols)
            results = (query_grad, key_grad, value_grad)
            if table_fn is not None:
                results = results + (table_fn(score_grad),)
            return results

        return attend_back

    def table_grad_of(score_grad):
        diag_sums = collect_diagonals(score_grad.astype(jnp.float32))
        return lax.dot_general(
            bucket_onehot,
            diag_sums,
            (((0,), (1,)), ((), ())),
            precision=HIGHEST_PRECISION,
            preferred_element_type=jnp.float32,
        )

    query_bias = col_bias[:head_cols]
    value_bias = col_bias[head_cols : 2 * head_cols]
    hidden_bias = col_bias[2 * head_cols :]
    inputs = frames.reshape(row_count, model_width)
    queries = (project(inputs, attn_w[0]) + query_bias).astype(jnp.bfloat16)
    keys_local = project(inputs, attn_w[1]).astype(jnp.bfloat16)
    values_local = (project(inputs, attn_w[2]) + value_bias).astype(jnp.bfloat16)
    keys_all, values_all = other_half(keys_local, values_local, piece_shape)
    query_blocks = queries.reshape(piece_shape)
    enc_scores = scorer(half_len, full_len, query_pos, rel_bias, False)
    context, log_total = run_blocks(
        forward_fn(enc_scores, half_len, full_len),
        (query_blocks, keys_all, values_all, lengths),
        False,
    )
    context_rows = context.reshape(row_count, head_cols)
    attn_sum = head_sum(contract_cols(context_rows, attn_w[3]))
    frame_rows = inputs.astype(jnp.float32)
    hidden_one, normed_one, inv_one = norm_forward(
        frame_rows + attn_sum + norm_vecs[4], norm_vecs[0], norm_vecs[1]
    )
    hidden_low = hidden_one.astype(jnp.bfloat16)
    gate_in = project(hidden_low, ffn_w[0]) + hidden_bias
    activated = jax.nn.gelu(gate_in, approximate=False).astype(jnp.bfloat16)
    ffn_sum = unit_sum(contract_cols(activated, ffn_w[1]))
    result, normed_two, inv_two = norm_forward(
        hidden_one + ffn_sum + norm_vecs[5], norm_vecs[2], norm_vecs[3]
    )
    enc_low = result.astype(jnp.bfloat16)
    text_in = dec_frames.reshape(text_count, model_width)
    self_q = (project(text_in, dec_attn_w[0]) + dec_col_bias[:head_cols]).astype(jnp.bfloat16)
    self_k = project(text_in, dec_attn_w[1]).astype(jnp.bfloat16)
    self_v = (project(text_in, dec_attn_w[2]) + dec_col_bias[head_cols : 2 * head_cols]).astype(
        jnp.bfloat16
    )
    self_keys, self_values = other_half(self_k, self_v, text_piece)
    self_scores = scorer(text_half, text_full, text_pos, None, True)
    self_context, self_log = run_blocks(
        forward_fn(self_scores, text_half, text_full),
        (self_q.reshape(text_piece), self_keys, self_values, text_lengths),
        True,
    )
    self_rows = self_context.reshape(text_count, head_cols)
    self_sum = head_sum(contract_cols(self_rows, dec_attn_w[3]))
    text_rows = text_in.astype(jnp.float32)
    dec_one, normed_d1, inv_d1 = norm_forward(
        text_rows + self_sum + dec_norm_vecs[6], dec_norm_vecs[0], dec_norm_vecs[1]
    )
    dec_one_low = dec_one.astype(jnp.bfloat16)
    cross_q = (
        project(dec_one_low, dec_attn_w[4]) + dec_col_bias[2 * head_cols : 3 * head_cols]
    ).astype(jnp.bfloat16)
    cross_k = project(enc_low, dec_attn_w[5]).astype(jnp.bfloat16)
    cross_v = (
        project(enc_low, dec_attn_w[6]) + dec_col_bias[3 * head_cols : 4 * head_cols]
    ).astype(jnp.bfloat16)
    cross_keys, cross_values = other_half(cross_k, cross_v, piece_shape)
    cross_scores = scorer(text_half, full_len, text_pos, None, False)
    cross_context, cross_log = run_blocks(
        forward_fn(cross_scores, text_half, full_len),
        (cross_q.reshape(text_piece), cross_keys, cross_values, lengths),
        True,
    )
    cross_rows = cross_context.reshape(text_count, head_cols)
    cross_sum = head_sum(contract_cols(cross_rows, dec_attn_w[7]))
    dec_two, normed_d2, inv_d2 = norm_forward(
        dec_one + cross_sum + dec_norm_vecs[7], dec_norm_vecs[2], dec_norm_vecs[3]
    )
    dec_two_low = dec_two.astype(jnp.bfloat16)
    dec_gate = project(dec_two_low, dec_ffn_w[0]) + dec_col_bias[4 * head_cols :]
    dec_act = jax.nn.gelu(dec_gate, approximate=False).astype(jnp.bfloat16)
    dec_ffn_sum = unit_sum(contract_cols(dec_act, dec_ffn_w[1]))
    dec_result, normed_d3, inv_d3 = norm_forward(
        dec_two + dec_ffn_sum + dec_norm_vecs[8], dec_norm_vecs[4], dec_norm_vecs[5]
    )
    text_valid = (
        (text_pos[None, :] < text_lengths[:, None]).astype(jnp.float32).reshape(text_count, 1)
    )
    dec_up = dec_cotangent.reshape(text_count, model_width).astype(jnp.float32) * text_valid
    grad_d3, gain_d3, shift_d3 = norm_backward(dec_up, normed_d3, inv_d3, dec_norm_vecs[4])
    dec_ffn_back = grad_d3.astype(jnp.bfloat16)
    dec_gate_grad = (project(dec_ffn_back, dec_ffn_w[1]) * gelu_slope(dec_gate)).astype(
        jnp.bfloat16
    )
    grad_h2 = grad_d3 + unit_back(contract_cols(dec_gate_grad, dec_ffn_w[0]))
    grad_d2, gain_d2, shift_d2 = norm_backward(grad_h2, normed_d2, inv_d2, dec_norm_vecs[2])
    cross_back = grad_d2.astype(jnp.bfloat16)
    cross_ctx_grad = project(cross_back, dec_attn_w[7]).astype(jnp.bfloat16).reshape(text_piece)
    cross_keys_b, cross_values_b = (cross_keys, cross_values)
    cross_qg, cross_kp, cross_vp = run_blocks(
        backward_fn(cross_scores, text_half, full_len, None),
        (
            cross_q.reshape(text_piece),
            cross_keys_b,
            cross_values_b,
            lengths,
            cross_log,
            cross_ctx_grad,
        ),
        True,
    )
    cross_kg, cross_vg = back_half(cross_kp, cross_vp)
    cross_q_rows = cross_qg.reshape(text_count, head_cols)
    cross_k_rows = cross_kg.reshape(row_count, head_cols).astype(jnp.bfloat16)
    cross_v_rows = cross_vg.reshape(row_count, head_cols).astype(jnp.bfloat16)
    query_back, memory_back = head_back(
        (
            contract_cols(cross_q_rows, dec_attn_w[4]),
            contract_cols(cross_k_rows, dec_attn_w[5]) + contract_cols(cross_v_rows, dec_attn_w[6]),
        )
    )
    grad_h1 = grad_d2 + query_back
    grad_d1, gain_d1, shift_d1 = norm_backward(grad_h1, normed_d1, inv_d1, dec_norm_vecs[0])
    self_back = grad_d1.astype(jnp.bfloat16)
    self_ctx_grad = project(self_back, dec_attn_w[3]).astype(jnp.bfloat16).reshape(text_piece)
    self_keys_b, self_values_b = (self_keys, self_values)
    self_qg, self_kp, self_vp = run_blocks(
        backward_fn(self_scores, text_half, text_full, None),
        (
            self_q.reshape(text_piece),
            self_keys_b,
            self_values_b,
            text_lengths,
            self_log,
            self_ctx_grad,
        ),
        True,
    )
    self_kg, self_vg = back_half(self_kp, self_vp)
    self_q_rows = self_qg.reshape(text_count, head_cols)
    self_k_rows = self_kg.reshape(text_count, head_cols).astype(jnp.bfloat16)
    self_v_rows = self_vg.reshape(text_count, head_cols).astype(jnp.bfloat16)
    text_grad = grad_d1 + head_back(
        contract_cols(self_q_rows, dec_attn_w[0])
        + contract_cols(self_k_rows, dec_attn_w[1])
        + contract_cols(self_v_rows, dec_attn_w[2])
    )
    valid_rows = (query_pos[None, :] < lengths[:, None]).astype(jnp.float32).reshape(row_count, 1)
    upstream = (
        cotangent.reshape(row_count, model_width).astype(jnp.float32) * valid_rows + memory_back
    )
    grad_two, gain_two, shift_two = norm_backward(upstream, normed_two, inv_two, norm_vecs[2])
    ffn_back = grad_two.astype(jnp.bfloat16)
    gate_grad = (project(ffn_back, ffn_w[1]) * gelu_slope(gate_in)).astype(jnp.bfloat16)
    hidden_grad = grad_two + unit_back(contract_cols(gate_grad, ffn_w[0]))
    grad_one, gain_one, shift_one = norm_backward(hidden_grad, normed_one, inv_one, norm_vecs[0])
    attn_back = grad_one.astype(jnp.bfloat16)
    context_grad = project(attn_back, attn_w[3]).astype(jnp.bfloat16).reshape(piece_shape)
    keys_back, values_back = (keys_all, values_all)
    query_grad, key_part, value_part, table_parts = run_blocks(
        backward_fn(enc_scores, half_len, full_len, table_grad_of),
        (query_blocks, keys_back, values_back, lengths, log_total, context_grad),
        False,
    )
    key_grad, value_grad = back_half(key_part, value_part)
    query_rows = query_grad.reshape(row_count, head_cols)
    key_rows = key_grad.reshape(row_count, head_cols).astype(jnp.bfloat16)
    value_rows = value_grad.reshape(row_count, head_cols).astype(jnp.bfloat16)
    input_grad = grad_one + head_back(
        contract_cols(query_rows, attn_w[0])
        + contract_cols(key_rows, attn_w[1])
        + contract_cols(value_rows, attn_w[2])
    )
    attn_local = jnp.stack(
        [
            contract_rows(inputs, query_rows),
            contract_rows(inputs, key_rows),
            contract_rows(inputs, value_rows),
            contract_rows(attn_back, context_rows),
        ]
    )
    ffn_local = jnp.stack(
        [contract_rows(hidden_low, gate_grad), contract_rows(ffn_back, activated)]
    )
    dec_attn_local = jnp.stack(
        [
            contract_rows(text_in, self_q_rows),
            contract_rows(text_in, self_k_rows),
            contract_rows(text_in, self_v_rows),
            contract_rows(self_back, self_rows),
            contract_rows(dec_one_low, cross_q_rows),
            contract_rows(enc_low, cross_k_rows),
            contract_rows(enc_low, cross_v_rows),
            contract_rows(cross_back, cross_rows),
        ]
    )
    dec_ffn_local = jnp.stack(
        [contract_rows(dec_two_low, dec_gate_grad), contract_rows(dec_ffn_back, dec_act)]
    )
    parts_data = (
        lax.psum_scatter(
            attn_local.astype(jnp.bfloat16), "dp", scatter_dimension=1, tiled=True
        ).astype(jnp.float32),
        lax.psum_scatter(
            ffn_local.astype(jnp.bfloat16), "dp", scatter_dimension=1, tiled=True
        ).astype(jnp.float32),
        lax.psum_scatter(
            dec_attn_local.astype(jnp.bfloat16), "dp", scatter_dimension=1, tiled=True
        ).astype(jnp.float32),
        lax.psum_scatter(
            dec_ffn_local.astype(jnp.bfloat16), "dp", scatter_dimension=1, tiled=True
        ).astype(jnp.float32),
    )
    attn_total, ffn_total, dec_attn_total, dec_ffn_total = (
        lax.psum_scatter(
            parts_data[0].astype(jnp.bfloat16), "seq", scatter_dimension=1, tiled=True
        ).astype(jnp.float32),
        lax.psum_scatter(
            parts_data[1].astype(jnp.bfloat16), "seq", scatter_dimension=1, tiled=True
        ).astype(jnp.float32),
        lax.psum_scatter(
            parts_data[2].astype(jnp.bfloat16), "seq", scatter_dimension=1, tiled=True
        ).astype(jnp.float32),
        lax.psum_scatter(
            parts_data[3].astype(jnp.bfloat16), "seq", scatter_dimension=1, tiled=True
        ).astype(jnp.float32),
    )
    norm_local = jnp.stack(
        [
            gain_one,
            shift_one,
            gain_two,
            shift_two,
            jnp.sum(grad_one, axis=0),
            jnp.sum(grad_two, axis=0),
        ]
    )
    col_local = jnp.concatenate(
        [
            jnp.sum(query_rows, axis=0, dtype=jnp.float32),
            jnp.sum(value_rows, axis=0, dtype=jnp.float32),
            jnp.sum(gate_grad, axis=0, dtype=jnp.float32),
        ]
    )
    dec_norm_local = jnp.stack(
        [
            gain_d1,
            shift_d1,
            gain_d2,
            shift_d2,
            gain_d3,
            shift_d3,
            jnp.sum(grad_d1, axis=0),
            jnp.sum(grad_d2, axis=0),
            jnp.sum(grad_d3, axis=0),
        ]
    )
    dec_col_local = jnp.concatenate(
        [
            jnp.sum(self_q_rows, axis=0, dtype=jnp.float32),
            jnp.sum(self_v_rows, axis=0, dtype=jnp.float32),
            jnp.sum(cross_q_rows, axis=0, dtype=jnp.float32),
            jnp.sum(cross_v_rows, axis=0, dtype=jnp.float32),
            jnp.sum(dec_gate_grad, axis=0, dtype=jnp.float32),
        ]
    )
    valid_local = jnp.sum(valid_rows)
    norm_total, col_total, table_total, frame_total, dec_norm_total, dec_col_total = lax.psum(
        (
            norm_local,
            col_local,
            jnp.sum(table_parts, axis=0),
            valid_local,
            dec_norm_local,
            dec_col_local,
        ),
        ("dp", "seq"),
    )
    matrix_rate = MATRIX_RATE * root_frames
    vector_rate = VECTOR_RATE * root_frames
    attn_new = update(attn_master, attn_moment, attn_average, attn_total, matrix_rate, frame_total)
    ffn_new = update(ffn_master, ffn_moment, ffn_average, ffn_total, matrix_rate, frame_total)
    norm_new = update(norm_vecs, norm_moment, norm_average, norm_total, vector_rate, frame_total)
    col_new = update(col_bias, col_moment, col_average, col_total, vector_rate, frame_total)
    rel_new = update(rel_table, rel_moment, rel_average, table_total, vector_rate, frame_total)
    dattn_new = update(
        dec_attn_master, dec_attn_moment, dec_attn_average, dec_attn_total, matrix_rate, frame_total
    )
    dffn_new = update(
        dec_ffn_master, dec_ffn_moment, dec_ffn_average, dec_ffn_total, matrix_rate, frame_total
    )
    dnorm_new = update(
        dec_norm_vecs, dec_norm_moment, dec_norm_average, dec_norm_total, vector_rate, frame_total
    )
    dcol_new = update(
        dec_col_bias, dec_col_moment, dec_col_average, dec_col_total, vector_rate, frame_total
    )
    out_shape = (utt_count, half_len, model_width)
    text_shape = (utt_count, text_half, model_width)
    return (
        enc_low.reshape(out_shape),
        input_grad.astype(jnp.bfloat16).reshape(out_shape),
        attn_new[0],
        ffn_new[0],
        attn_new[1],
        attn_new[2],
        attn_new[3],
        attn_new[1].astype(jnp.bfloat16),
        ffn_new[1],
        ffn_new[2],
        ffn_new[3],
        ffn_new[1].astype(jnp.bfloat16),
        norm_new[1],
        norm_new[2],
        norm_new[3],
        col_new[1],
        col_new[2],
        col_new[3],
        rel_new[1],
        rel_new[2],
        rel_new[3],
        dec_result.astype(jnp.bfloat16).reshape(text_shape),
        text_grad.astype(jnp.bfloat16).reshape(text_shape),
        dattn_new[0],
        dffn_new[0],
        dattn_new[1],
        dattn_new[2],
        dattn_new[3],
        dattn_new[1].astype(jnp.bfloat16),
        dffn_new[1],
        dffn_new[2],
        dffn_new[3],
        dffn_new[1].astype(jnp.bfloat16),
        dnorm_new[1],
        dnorm_new[2],
        dnorm_new[3],
        dcol_new[1],
        dcol_new[2],
        dcol_new[3],
    )


def solution(mesh):
    in_specs = (
        P("dp", "seq", None),
        P("dp", "seq", None),
        P("dp"),
        P(None, ("dp", "seq"), "mp"),
        P(None, ("dp", "seq"), "mp"),
        P(None, ("dp", "seq"), "mp"),
        P(None, ("dp", "seq"), "mp"),
        P(None, ("dp", "seq"), "mp"),
        P(None, ("dp", "seq"), "mp"),
        P(),
        P(),
        P(),
        P("mp"),
        P("mp"),
        P("mp"),
        P(None, "mp"),
        P(None, "mp"),
        P(None, "mp"),
        P("dp", "seq", None),
        P("dp", "seq", None),
        P("dp"),
        P(None, ("dp", "seq"), "mp"),
        P(None, ("dp", "seq"), "mp"),
        P(None, ("dp", "seq"), "mp"),
        P(None, ("dp", "seq"), "mp"),
        P(None, ("dp", "seq"), "mp"),
        P(None, ("dp", "seq"), "mp"),
        P(),
        P(),
        P(),
        P("mp"),
        P("mp"),
        P("mp"),
    )
    out_specs = (
        P("dp", "seq", None),
        P("dp", "seq", None),
        P(None, ("dp", "seq"), "mp"),
        P(None, ("dp", "seq"), "mp"),
        P(None, ("dp", "seq"), "mp"),
        P(None, ("dp", "seq"), "mp"),
        P(None, ("dp", "seq"), "mp"),
        P(None, ("dp", "seq"), "mp"),
        P(None, ("dp", "seq"), "mp"),
        P(None, ("dp", "seq"), "mp"),
        P(None, ("dp", "seq"), "mp"),
        P(None, ("dp", "seq"), "mp"),
        P(),
        P(),
        P(),
        P("mp"),
        P("mp"),
        P("mp"),
        P(None, "mp"),
        P(None, "mp"),
        P(None, "mp"),
        P("dp", "seq", None),
        P("dp", "seq", None),
        P(None, ("dp", "seq"), "mp"),
        P(None, ("dp", "seq"), "mp"),
        P(None, ("dp", "seq"), "mp"),
        P(None, ("dp", "seq"), "mp"),
        P(None, ("dp", "seq"), "mp"),
        P(None, ("dp", "seq"), "mp"),
        P(None, ("dp", "seq"), "mp"),
        P(None, ("dp", "seq"), "mp"),
        P(None, ("dp", "seq"), "mp"),
        P(None, ("dp", "seq"), "mp"),
        P(),
        P(),
        P(),
        P("mp"),
        P("mp"),
        P("mp"),
    )
    return jax.shard_map(local, mesh=mesh, in_specs=in_specs, out_specs=out_specs, check_vma=False)
```

profile of v0, /device:TPU:0, one launch (start us, length us, event | category | flops | bytes accessed | tf_op | source)
XLA Modules:
  0.0 1784.2 jit_solution(11123355338248223518)
XLA Ops:
  9.9 28.2 %all-gather.9.cloned.1.call-done = bf16[4,768,192]{2,1,0:T(8,128)(2,1)} async-done(((bf16[4,96,192]{2,1,0:T(8,128)(2,1)}), bf16[4,768,192]{2,1,0:T(8,128)(2,1)}) %all-gather.9.cloned.1.call-update) | async-done | bytes 1179664 | tf_op jit(solution)/shard_map/all_gather | solution.py:168
  68.7 23.1 %rev.9 = f32[3,384,768]{2,1,0:T(8,128)S(1)} reverse(f32[3,384,768]{2,1,0:T(8,128)} %slice.192), dimensions={1} | reverse | bytes 7077888 | tf_op jit(solution)/shard_map/rev | solution.py:69
  96.2 29.6 %while.32 = (s32[]{:T(128)}, bf16[4,384,192]{1,2,0:T(8,128)(2,1)}, f32[4,3,384]{2,1,0:T(4,128)}, bf16[4,768,192]{1,2,0:T(8,128)(2,1)}, s32[4]{0:T(128)S(1)}, /*i...) while((s32[]{:T(128)}, bf16[4,384,192]{1,2,0:T(8,128)(2,1)}, ...), condition=%wide.region_3.4_spmd.clone, body=%wide.region_0.3_spmd.clone.sunk | while | flops 234528384 | bytes 16851060 | solution.py:93
  149.8 55.9 %all-reduce.15.cloned.1.call-done = bf16[1536,768]{1,0:T(8,128)(2,1)} async-done(((bf16[1536,768]{1,0:T(8,128)(2,1)}), bf16[1536,768]{1,0:T(8,128)(2,1)}) %all-reduce.15.cloned.1.call-update) | async-done | bytes 2359312 | tf_op jit(solution)/shard_map/psum | solution.py:115
  213.2 26.2 %all-gather.15.cloned.1.call-done = bf16[2,768,768]{2,1,0:T(8,128)(2,1)} async-done(((bf16[2,96,768]{2,1,0:T(8,128)(2,1)}), bf16[2,768,768]{2,1,0:T(8,128)(2,1)}) %all-gather.15.cloned.1.call-update) | async-done | bytes 2359312 | tf_op jit(solution)/shard_map/all_gather | solution.py:169
  239.5 14.8 fusion.23
  259.9 86.0 %all-reduce.29.cloned.1.call-done = (bf16[1536,768]{1,0:T(8,128)(2,1)}, bf16[512,768]{1,0:T(8,128)(2,1)}) async-done(((bf16[1536,768]{1,0:T(8,128)(2,1)}, bf16[512,768]{1,0:T(8,128)(2,1)}), (bf16[1536,768]{1,0:T(8,128)(2,1)}, bf16[512,768]{1,0:T(8,128)(2,1)})) %all-reduce.29.cloned.1.call-update) | async-done | bytes 3145744 | tf_op jit(solution)/shard_map/psum | solution.py:119
  390.1 49.2 %all-reduce.17.cloned.1.call-done = bf16[512,768]{1,0:T(8,128)(2,1)} async-done(((bf16[512,768]{1,0:T(8,128)(2,1)}), bf16[512,768]{1,0:T(8,128)(2,1)}) %all-reduce.17.cloned.1.call-update) | async-done | bytes 786448 | tf_op jit(solution)/shard_map/psum | solution.py:115
  441.1 32.0 %all-gather.23.cloned.1.call-done = bf16[2,768,768]{2,1,0:T(8,128)(2,1)} async-done(((bf16[2,96,768]{2,1,0:T(8,128)(2,1)}), bf16[2,768,768]{2,1,0:T(8,128)(2,1)}) %all-gather.23.cloned.1.call-update) | async-done | bytes 2359312 | tf_op jit(solution)/shard_map/all_gather | solution.py:171
  483.0 46.5 %all-reduce.19.cloned.1.call-done = bf16[512,768]{1,0:T(8,128)(2,1)} async-done(((bf16[512,768]{1,0:T(8,128)(2,1)}), bf16[512,768]{1,0:T(8,128)(2,1)}) %all-reduce.19.cloned.1.call-update) | async-done | bytes 786448 | tf_op jit(solution)/shard_map/psum | solution.py:119
  540.9 48.8 %all-reduce.21.cloned.1.call-done = bf16[512,768]{1,0:T(8,128)(2,1)} async-done(((bf16[512,768]{1,0:T(8,128)(2,1)}), bf16[512,768]{1,0:T(8,128)(2,1)}) %all-reduce.21.cloned.1.call-update) | async-done | bytes 786448 | tf_op jit(solution)/shard_map/psum | solution.py:123
  599.0 27.1 %copy.248 = bf16[4,768,192]{0,2,1:T(8,128)(2,1)} copy(bf16[4,768,192]{1,2,0:T(8,128)(2,1)S(1)} %bitcast.582) | data formatting | bytes 2359296
  626.0 71.2 %reshape.603 = bf16[768,768]{1,0:T(8,128)(2,1)} reshape(bf16[768,192,4]{2,1,0:T(8,128)(2,1)} %bitcast.530) | data formatting | bytes 2359296
  705.0 27.1 %copy.246 = bf16[4,768,192]{0,2,1:T(8,128)(2,1)} copy(bf16[4,768,192]{1,2,0:T(8,128)(2,1)S(1)} %bitcast.581) | data formatting | bytes 2359296
  732.1 71.1 %reshape.601 = bf16[768,768]{1,0:T(8,128)(2,1)} reshape(bf16[768,192,4]{2,1,0:T(8,128)(2,1)} %bitcast.531) | data formatting | bytes 2359296
  803.3 41.4 %reshape.604 = bf16[384,192,4]{2,1,0:T(8,128)(2,1)} reshape(bf16[384,768]{1,0:T(8,128)(2,1)} %reduce-scatter.45.cloned.1.call-done) | data formatting | bytes 1179648
  844.7 17.8 copy.249
  862.7 41.4 %reshape.602 = bf16[384,192,4]{2,1,0:T(8,128)(2,1)} reshape(bf16[384,768]{1,0:T(8,128)(2,1)} %reduce-scatter.43.cloned.1.call-done) | data formatting | bytes 1179648
  904.1 17.8 copy.247
  935.7 65.5 %all-reduce.23.cloned.1.call-done = bf16[1536,768]{1,0:T(8,128)(2,1)} async-done(((bf16[1536,768]{1,0:T(8,128)(2,1)}), bf16[1536,768]{1,0:T(8,128)(2,1)}) %all-reduce.23.cloned.1.call-update) | async-done | bytes 2359312 | tf_op jit(solution)/shard_map/psum | solution.py:128
  1020.9 87.5 %all-reduce.27.cloned.1.call-done = (bf16[1536,768]{1,0:T(8,128)(2,1)}, bf16[512,768]{1,0:T(8,128)(2,1)}) async-done(((bf16[1536,768]{1,0:T(8,128)(2,1)}, bf16[512,768]{1,0:T(8,128)(2,1)}), (bf16[1536,768]{1,0:T(8,128)(2,1)}, bf16[512,768]{1,0:T(8,128)(2,1)})) %all-reduce.27.cloned.1.call-update) | async-done | bytes 3145744 | tf_op jit(solution)/shard_map/psum | solution.py:123
  1121.8 275.8 %while.33 = (s32[]{:T(128)}, bf16[4,384,192]{1,2,0:T(8,128)(2,1)}, bf16[4,768,192]{1,2,0:T(8,128)(2,1)}, bf16[4,768,192]{1,2,0:T(8,128)(2,1)}, f32[4,320,3]{1,2,...) while((s32[]{:T(128)}, bf16[4,384,192]{1,2,0:T(8,128)(2,1)}, ...), condition=%wide.region_40.41_spmd.clone, body=%wide.region_37.40_spmd.clone.sunk | while | flops 590839040 | bytes 116979096 | solution.py:93
  1131.6 26.2 %rev.12 = f32[3,384,768]{2,1,0:T(8,128)} reverse(bf16[3,384,768]{2,1,0:T(8,128)(2,1)} %multiply_convert_fusion.5), dimensions={1} | reverse | bytes 5308416 | tf_op jit(solution)/shard_map/while/body/eval_jaxpr/rev | solution.py:75
  1200.4 26.2 %rev.12 = f32[3,384,768]{2,1,0:T(8,128)} reverse(bf16[3,384,768]{2,1,0:T(8,128)(2,1)} %multiply_convert_fusion.5), dimensions={1} | reverse | bytes 5308416 | tf_op jit(solution)/shard_map/while/body/eval_jaxpr/rev | solution.py:75
  1269.2 26.2 %rev.12 = f32[3,384,768]{2,1,0:T(8,128)} reverse(bf16[3,384,768]{2,1,0:T(8,128)(2,1)} %multiply_convert_fusion.5), dimensions={1} | reverse | bytes 5308416 | tf_op jit(solution)/shard_map/while/body/eval_jaxpr/rev | solution.py:75
  1338.0 26.2 %rev.12 = f32[3,384,768]{2,1,0:T(8,128)} reverse(bf16[3,384,768]{2,1,0:T(8,128)(2,1)} %multiply_convert_fusion.5), dimensions={1} | reverse | bytes 5308416 | tf_op jit(solution)/shard_map/while/body/eval_jaxpr/rev | solution.py:75
  1443.0 24.0 %reshape.613 = bf16[256,768]{1,0:T(8,128)(2,1)} reshape(bf16[256,192,4]{2,1,0:T(8,128)(2,1)} %bitcast.545) | data formatting | bytes 786432
  1477.0 24.1 %reshape.615 = bf16[256,768]{1,0:T(8,128)(2,1)} reshape(bf16[256,192,4]{2,1,0:T(8,128)(2,1)} %bitcast.546) | data formatting | bytes 786432
  1535.7 15.5 reshape.614
  1557.7 15.3 reshape.616
  1677.9 31.2 %all-reduce.2 = (f32[]{:T(128)}, f32[6,768]{1,0:T(8,128)S(1)}, f32[1152]{0:T(1024)S(1)}, f32[320,3]{0,1:T(4,128)S(1)}, f32[9,768]{1,0:T(8,128)S(1)}, /*index=5*/f32[1536]{0:T(1024)S(1)}) all-reduce(f32[]{:T(128)} %fusion.171, f32[6,768]{1,0:T(8,128)} %stack.145, ...), channel_id=1, replica_groups=mesh['dp'=4,'seq'=2,'mp'=4] {'dp','seq'}, use_global_device_ids=true, to_apply=%region_47.48 | all-reduce | flops 15169 | bytes 121352 | tf_op jit(solution)/shard_map/psum | solution.py:558
  1738.5 16.3 all-reduce.25.cloned.1.call-done
  (844 shorter events, 656.5 us)
Async XLA Ops:
  7.2 30.8 %all-gather.9.cloned.1.call-start = ((), (), s32[]{:S(2)}) async-start(), calls=%async_computation.14 | async-start | bytes 1769472 | tf_op jit(solution)/shard_map/all_gather | solution.py:168
  9.0 86.4 %all-gather.11.cloned.1.call-start = ((), (), s32[]{:S(2)}) async-start(), calls=%async_computation.15 | async-start | bytes 1769472 | tf_op jit(solution)/shard_map/all_gather | solution.py:99
  41.7 53.6 %all-gather.13.cloned.1.call-start = ((), (), s32[]{:S(2)}) async-start(), calls=%async_computation.16 | async-start | bytes 1769472 | tf_op jit(solution)/shard_map/all_gather | solution.py:98
  44.7 90.9 %all-gather.17.cloned.1.call-start = ((), (), s32[]{:S(2)}) async-start(), calls=%async_computation.19 | async-start | bytes 3538944 | tf_op jit(solution)/shard_map/all_gather | solution.py:170
  45.6 160.1 %all-reduce.15.cloned.1.call-start = ((), (), s32[]{:S(2)}) async-start(), calls=%async_computation.17 | async-start | bytes 4718592 | tf_op jit(solution)/shard_map/psum | solution.py:115
  131.4 108.1 %all-gather.15.cloned.1.call-start = ((), (), s32[]{:S(2)}) async-start(), calls=%async_computation.18 | async-start | bytes 2654208 | tf_op jit(solution)/shard_map/all_gather | solution.py:169
  133.4 212.5 %all-reduce.29.cloned.1.call-start = ((), (), s32[]{:S(2)}) async-start(), calls=%async_computation.43 | async-start | bytes 6291456 | tf_op jit(solution)/shard_map/psum | solution.py:119
  135.5 215.1 %copy-start.109 = (f32[768]{0:T(1024)}, f32[768]{0:T(1024)S(1)}, u32[]{:S(2)}) copy-start(f32[768]{0:T(1024)S(1)} %get-tuple-element.589) | copy-start | bytes 9220
  259.2 109.1 %all-gather.19.cloned.1.call-start = ((), (), s32[]{:S(2)}) async-start(), calls=%async_computation.20 | async-start | bytes 1769472 | tf_op jit(solution)/shard_map/all_gather | solution.py:98
  358.5 21.8 %all-gather.21.cloned.1.call-start = ((), (), s32[]{:S(2)}) async-start(), calls=%async_computation.21 | async-start | bytes 1769472 | tf_op jit(solution)/shard_map/all_gather | solution.py:99
  358.7 233.7 %copy-start.113 = (f32[768]{0:T(1024)}, f32[768]{0:T(1024)S(1)}, u32[]{:S(2)}) copy-start(f32[768]{0:T(1024)S(1)} %get-tuple-element.584) | copy-start | bytes 9220
  365.9 73.4 %all-reduce.17.cloned.1.call-start = ((), (), s32[]{:S(2)}) async-start(), calls=%async_computation.22 | async-start | bytes 1572864 | tf_op jit(solution)/shard_map/psum | solution.py:115
  389.2 84.0 %all-gather.23.cloned.1.call-start = ((), (), s32[]{:S(2)}) async-start(), calls=%async_computation.23 | async-start | bytes 2654208 | tf_op jit(solution)/shard_map/all_gather | solution.py:171
  390.0 139.5 %all-reduce.19.cloned.1.call-start = ((), (), s32[]{:S(2)}) async-start(), calls=%async_computation.24 | async-start | bytes 1572864 | tf_op jit(solution)/shard_map/psum | solution.py:119
  481.5 108.2 %all-reduce.21.cloned.1.call-start = ((), (), s32[]{:S(2)}) async-start(), calls=%async_computation.25 | async-start | bytes 1572864 | tf_op jit(solution)/shard_map/psum | solution.py:123
  540.8 262.5 %reduce-scatter.45.cloned.1.call-start = ((), (), s32[]{:S(2)}) async-start(), calls=%async_computation.32 | async-start | bytes 1769472
  697.3 165.4 %reduce-scatter.43.cloned.1.call-start = ((), (), s32[]{:S(2)}) async-start(), calls=%async_computation.31 | async-start | bytes 1769472
  803.2 198.0 %all-reduce.23.cloned.1.call-start = ((), (), s32[]{:S(2)}) async-start(), calls=%async_computation.26 | async-start | bytes 4718592 | tf_op jit(solution)/shard_map/psum | solution.py:128
  927.4 181.0 %all-reduce.27.cloned.1.call-start = ((), (), s32[]{:S(2)}) async-start(), calls=%async_computation.42 | async-start | bytes 6291456 | tf_op jit(solution)/shard_map/psum | solution.py:123
  1020.8 485.6 %reduce-scatter.49.cloned.1.call-start = ((), (), s32[]{:S(2)}) async-start(), calls=%async_computation.34 | async-start | bytes 1769472
  1402.5 107.6 %reduce-scatter.47.cloned.1.call-start = ((), (), s32[]{:S(2)}) async-start(), calls=%async_computation.33 | async-start | bytes 1769472
  1405.9 116.6 %reduce-scatter.39.cloned.1.call-start = ((), (), s32[]{:S(2)}) async-start(), calls=%async_computation.29 | async-start | bytes 2949120 | tf_op jit(solution)/shard_map/reduce_scatter | solution.py:500
  1410.8 114.7 %reduce-scatter.35.cloned.1.call-start = ((), (), s32[]{:S(2)}) async-start(), calls=%async_computation.27 | async-start | bytes 2949120 | tf_op jit(solution)/shard_map/reduce_scatter | solution.py:494
  1423.2 112.5 %reduce-scatter.55.cloned.1.call-start = ((), (), s32[]{:S(2)}) async-start(), calls=%async_computation.37 | async-start | bytes 589824
  1467.0 90.7 %reduce-scatter.57.cloned.1.call-start = ((), (), s32[]{:S(2)}) async-start(), calls=%async_computation.38 | async-start | bytes 589824
  1505.0 78.9 %reduce-scatter.51.cloned.1.call-start = ((), (), s32[]{:S(2)}) async-start(), calls=%async_computation.35 | async-start | bytes 1474560
  1522.4 196.8 %reduce-scatter.41.cloned.1.call-start = ((), (), s32[]{:S(2)}) async-start(), calls=%async_computation.30 | async-start | bytes 884736 | tf_op jit(solution)/shard_map/reduce_scatter | solution.py:514
  1523.1 200.9 %reduce-scatter.37.cloned.1.call-start = ((), (), s32[]{:S(2)}) async-start(), calls=%async_computation.28 | async-start | bytes 884736 | tf_op jit(solution)/shard_map/reduce_scatter | solution.py:508
  1525.5 204.4 %reduce-scatter.53.cloned.1.call-start = ((), (), s32[]{:S(2)}) async-start(), calls=%async_computation.36 | async-start | bytes 442368
  1583.9 148.9 %reduce-scatter.59.cloned.1.call-start = ((), (), s32[]{:S(2)}) async-start(), calls=%async_computation.39 | async-start | bytes 2949120
  1602.0 152.8 %all-reduce.25.cloned.1.call-start = ((), (), s32[]{:S(2)}) async-start(), calls=%async_computation.41 | async-start | bytes 6291456 | tf_op jit(solution)/shard_map/psum | solution.py:128
  1650.3 114.6 %reduce-scatter.61.cloned.1.call-start = ((), (), s32[]{:S(2)}) async-start(), calls=%async_computation.40 | async-start | bytes 884736
  (193 other events, 2909.9 us)
Sparse Core Ops, SparseCore 0:
  10.2 27.7 all-gather.8
  41.8 8.7 all-gather.10
  52.8 10.3 all-gather.12
  65.2 39.4 all-gather.16
  131.5 74.1 all-reduce.14
  207.8 31.6 all-gather.14
  259.3 86.4 all-reduce.28
  358.6 9.1 all-gather.18
  370.0 10.3 all-gather.20
  389.3 49.9 all-reduce.16
  441.6 31.5 all-gather.22
  481.6 47.8 all-reduce.18
  541.0 48.7 all-reduce.20
  697.4 8.6 reduce-scatter.44
  803.4 8.3 reduce-scatter.42
  927.5 73.7 all-reduce.22
  1021.0 87.3 all-reduce.26
  1402.6 8.6 reduce-scatter.48
  1413.6 9.8 reduce-scatter.46
  1425.7 49.2 reduce-scatter.38
  1478.0 47.5 reduce-scatter.34
  1528.4 7.2 reduce-scatter.54
  1538.5 8.9 reduce-scatter.56
  1549.8 30.3 reduce-scatter.50
  1582.5 6.6 reduce-scatter.40
  1591.4 9.1 reduce-scatter.36
  1602.8 8.8 reduce-scatter.52
  1614.1 49.1 reduce-scatter.58
  1667.9 86.8 all-reduce.24
  1756.9 8.0 reduce-scatter.60
where the time goes:
time: 1810 us; the launch traced here: 1780 us
  local copies, waits for them, and re-layouts  850 us (47%)
  waiting for transfers between devices  563 us (31%)
  matrix products  180 us (10%)
  other arithmetic  135 us (7%)
  blocking collectives  35.4 us (2%)
    unnamed x370, local copies, waits for them, and re-layouts  514 us
    psum x2, waiting for transfers between devices, unit_back(): lax.psum(partial_value.astype(jnp.bfloat16), 'mp').astype(jnp.float32)  136 us
    psum x2, waiting for transfers between devices, unit_sum(): lax.psum(partial_value.astype(jnp.bfloat16), 'mp').astype(jnp.float32)  132 us
    psum x2, waiting for transfers between devices, head_sum(): lax.psum(partial_value.astype(jnp.bfloat16), 'mp').astype(jnp.float32)  105 us
    rev x4, local copies, waits for them, and re-layouts, collect_diagonals(): flipped = grid[:, ::-1, :]  105 us
    psum x2, waiting for transfers between devices, head_back(): lax.psum(for_sending(partial_value), 'mp')  81.8 us
    dot_general x16, matrix products, project(): return jnp.dot(rows, matrix, preferred_element_type=jnp.float32)  52.1 us
    reshape x4, local copies, waits for them, and re-layouts, collect_diagonals(): padded[:, :row_total * width].reshape(lead, row_total, width)  49.2 us
  transfers between devices with their start and end apart: 30, of which 15 were waited for; matrix products, arithmetic and copies ran while one was open for 33% of the time, Pallas kernels for 0%

commit v1 on v0

v1 whole, which is shorter than its diff:
```python
import functools

import jax
import jax.numpy as jnp
from jax import lax
from jax.experimental import pallas as pl
from jax.experimental.pallas import tpu as pltpu
from jax.sharding import PartitionSpec as P

EPSILON = 1e-05
MOMENTUM = 0.9
AVERAGING = 0.75
MATRIX_RATE = 0.02
VECTOR_RATE = 0.2
MASK_VALUE = -1e30
ROOT_HALF = 0.7071067811865476
INV_ROOT_TAU = 0.3989422804014327
BLOCK = 256
PAIR = 128
BF16 = jnp.bfloat16
F32 = jnp.float32


def bf(a):
    return a.astype(BF16)


def wide(a):
    return a.astype(F32)


def dot_nn(left, right):
    return jnp.dot(left, right, preferred_element_type=F32)


def dot_nt(left, right):
    return lax.dot_general(left, right, (((1,), (1,)), ((), ())), preferred_element_type=F32)


def dot_tn(left, right):
    return lax.dot_general(left, right, (((0,), (0,)), ((), ())), preferred_element_type=F32)


def swap_core(v):
    return lax.ppermute(v, "seq", [(0, 1), (1, 0)])


def swap_mp(v, bits):
    return lax.ppermute(v, "mp", [(m, m ^ bits) for m in range(4)])


def spread_perm(flip):
    return [
        (s * 4 + y * 2 + x, y * 4 + (s ^ flip) * 2 + x)
        for s in range(2)
        for y in range(2)
        for x in range(2)
    ]


def spread(v, flip):
    return lax.ppermute(v, ("seq", "mp"), spread_perm(flip))


def unspread(v, flip):
    return lax.ppermute(v, ("seq", "mp"), [(d, s) for s, d in spread_perm(flip)])


def shift_dp(v, k):
    n = lax.axis_size("dp")
    return lax.ppermute(v, "dp", [(i, (i + k) % n) for i in range(n)])


def sum_dp(v):
    n = lax.axis_size("dp")
    if n > 4:
        return lax.psum(v, "dp")
    return v + sum(shift_dp(v, k) for k in range(1, n))


def gather_chunk(shard):
    n = lax.axis_size("dp")
    half = shard.shape[0] // 2
    if n > 4:
        whole = lax.all_gather(shard, "dp", axis=0, tiled=False)
        za, zb = whole[:, :half], whole[:, half:]
    else:
        blocks = [shard] + [shift_dp(shard, k) for k in range(1, n)]
        za = jnp.stack([b[:half] for b in blocks])
        zb = jnp.stack([b[half:] for b in blocks])
    ax = swap_mp(za, 1)
    first = [[spread(za, a) for a in range(2)], [spread(ax, a) for a in range(2)]]
    own = [spread(zb, a) for a in range(2)]
    second = [own, [swap_mp(b, 1) for b in own]]
    return [first, second]


def scatter_chunk(pieces):
    n = lax.axis_size("dp")
    first, second = pieces
    t = [sum(wide(unspread(first[dx][a], a)) for a in range(2)) for dx in range(2)]
    ta = wide(swap_mp(bf(t[1]), 1))
    u = [bf(wide(second[0][a]) + wide(swap_mp(second[1][a], 1))) for a in range(2)]
    tb = [wide(unspread(u[a], a)) for a in range(2)]
    if n > 4:
        whole = bf(jnp.concatenate([t[0] + ta, tb[0] + tb[1]], axis=1))
        return wide(lax.psum_scatter(whole, "dp", scatter_dimension=0, tiled=False))
    total = None
    for k in range(n):
        part = jnp.concatenate([t[0][k] + ta[k], tb[0][k] + tb[1][k]], axis=0)
        part = part if k == 0 else wide(shift_dp(bf(part), n - k))
        total = part if total is None else total + part
    return total


def pack_attn(shard):
    main, rest = shard[:, :, :PAIR], shard[:, :, PAIR:]
    return jnp.concatenate([main, jnp.concatenate([rest[0::2], rest[1::2]], axis=-1)], axis=0)


def unpack_attn(tiles, count):
    main, rest = tiles[:count], tiles[count:]
    left, right = rest[:, :, : PAIR // 2], rest[:, :, PAIR // 2 :]
    rest = jnp.stack([left, right], axis=1).reshape(count, tiles.shape[1], PAIR // 2)
    return jnp.concatenate([main, rest], axis=-1)


def half_lanes(shape):
    return lax.broadcasted_iota(jnp.int32, shape, len(shape) - 1) < PAIR // 2


def half_roll(v):
    return bf(pltpu.roll(wide(v), PAIR // 2, 1))


def assemble_attn(pieces, plans, count, zidx, yidx):
    flat = [pieces[h][dx][a] for h in range(2) for dx in range(2) for a in range(2)]
    n, half, rows, _ = flat[0].shape

    def kernel(zi, yi, *refs):
        ins, outs = refs[:8], refs[8:]
        low = half_lanes((rows, PAIR))
        for a in range(2):
            side = yi[a]

            def tile(t, dx):
                return ins[(t // half) * 4 + dx * 2 + a][0, t % half]

            for out, plan in zip(outs, plans):
                for place, (mat, j) in enumerate(plan):
                    if j < 2:
                        val = tile(mat, j)
                    else:
                        t0, t1 = tile(count + mat // 2, 0), tile(count + mat // 2, 1)
                        if mat % 2 == 0:
                            val = jnp.where(low, t0, half_roll(t1))
                        else:
                            val = jnp.where(low, half_roll(t0), t1)
                    out[0, side, :, place * PAIR : (place + 1) * PAIR] = val

    outs = pl.pallas_call(
        kernel,
        grid_spec=pltpu.PrefetchScalarGridSpec(
            num_scalar_prefetch=2,
            grid=(n,),
            in_specs=[pl.BlockSpec((1, half, rows, PAIR), lambda k, zi, yi: (k, 0, 0, 0))] * 8,
            out_specs=[
                pl.BlockSpec((1, 2, rows, PAIR * len(p)), lambda k, zi, yi: (zi[k], 0, 0, 0))
                for p in plans
            ],
        ),
        out_shape=[jax.ShapeDtypeStruct((n, 2, rows, PAIR * len(p)), BF16) for p in plans],
        cost_estimate=pl.CostEstimate(
            flops=0, transcendentals=0, bytes_accessed=2 * 8 * n * half * rows * PAIR * 2
        ),
        name="assemble_attn",
    )(zidx, yidx, *flat)
    return [o.reshape(n * 2 * rows, -1) for o in outs]


def split_attn(mats, plans, count, zidx, yidx):
    half = (count + count // 2) // 2
    n = zidx.shape[0]
    rows = mats[0].shape[0] // (2 * n)
    ins = [m.reshape(n, 2, rows, -1) for m in mats]
    where = {}
    for i, plan in enumerate(plans):
        for place, key in enumerate(plan):
            where[key] = (i, place)

    def kernel(zi, yi, *refs):
        srcs, outs = refs[: len(mats)], refs[len(mats) :]
        low = half_lanes((rows, PAIR))
        for a in range(2):
            side = yi[a]

            def get(mat, j):
                i, place = where[(mat, j)]
                return srcs[i][0, side, :, place * PAIR : (place + 1) * PAIR]

            for dx in range(2):
                for t in range(2 * half):
                    if t < count:
                        val = get(t, dx)
                    else:
                        p = t - count
                        t0, t1 = get(2 * p, 2), get(2 * p + 1, 2)
                        if dx == 0:
                            val = jnp.where(low, t0, half_roll(t1))
                        else:
                            val = jnp.where(low, half_roll(t0), t1)
                    outs[(t // half) * 4 + dx * 2 + a][0, t % half] = val

    outs = pl.pallas_call(
        kernel,
        grid_spec=pltpu.PrefetchScalarGridSpec(
            num_scalar_prefetch=2,
            grid=(n,),
            in_specs=[
                pl.BlockSpec((1, 2, rows, m.shape[-1]), lambda k, zi, yi: (zi[k], 0, 0, 0))
                for m in ins
            ],
            out_specs=[pl.BlockSpec((1, half, rows, PAIR), lambda k, zi, yi: (k, 0, 0, 0))] * 8,
        ),
        out_shape=[jax.ShapeDtypeStruct((n, half, rows, PAIR), BF16)] * 8,
        cost_estimate=pl.CostEstimate(
            flops=0, transcendentals=0, bytes_accessed=2 * 8 * n * half * rows * PAIR * 2
        ),
        name="split_attn",
    )(zidx, yidx, *ins)
    return [[[outs[h * 4 + dx * 2 + a] for a in range(2)] for dx in range(2)] for h in range(2)]


def assemble_ffn(pieces, zidx, yidx):
    flat = [pieces[h][dx][a] for h in range(2) for dx in range(2) for a in range(2)]
    n, _, rows, cols = flat[0].shape

    def kernel(zi, yi, *refs):
        ins, outs = refs[:8], refs[8:]
        for a in range(2):
            for h in range(2):
                for dx in range(2):
                    outs[h][0, yi[a], :, dx * cols : (dx + 1) * cols] = ins[h * 4 + dx * 2 + a][0, 0]

    outs = pl.pallas_call(
        kernel,
        grid_spec=pltpu.PrefetchScalarGridSpec(
            num_scalar_prefetch=2,
            grid=(n,),
            in_specs=[pl.BlockSpec((1, 1, rows, cols), lambda k, zi, yi: (k, 0, 0, 0))] * 8,
            out_specs=[
                pl.BlockSpec((1, 2, rows, 2 * cols), lambda k, zi, yi: (zi[k], 0, 0, 0))
            ]
            * 2,
        ),
        out_shape=[jax.ShapeDtypeStruct((n, 2, rows, 2 * cols), BF16)] * 2,
        cost_estimate=pl.CostEstimate(
            flops=0, transcendentals=0, bytes_accessed=2 * 8 * n * rows * cols * 2
        ),
        name="assemble_ffn",
    )(zidx, yidx, *flat)
    return [o.reshape(n * 2 * rows, 2 * cols) for o in outs]


def split_ffn(mats, zidx, yidx):
    n = zidx.shape[0]
    rows = mats[0].shape[0] // (2 * n)
    cols = mats[0].shape[1] // 2
    ins = [m.reshape(n, 2, rows, 2 * cols) for m in mats]

    def kernel(zi, yi, *refs):
        srcs, outs = refs[:2], refs[2:]
        for a in range(2):
            for h in range(2):
                for dx in range(2):
                    outs[h * 4 + dx * 2 + a][0, 0] = srcs[h][
                        0, yi[a], :, dx * cols : (dx + 1) * cols
                    ]

    outs = pl.pallas_call(
        kernel,
        grid_spec=pltpu.PrefetchScalarGridSpec(
            num_scalar_prefetch=2,
            grid=(n,),
            in_specs=[pl.BlockSpec((1, 2, rows, 2 * cols), lambda k, zi, yi: (zi[k], 0, 0, 0))] * 2,
            out_specs=[pl.BlockSpec((1, 1, rows, cols), lambda k, zi, yi: (k, 0, 0, 0))] * 8,
        ),
        out_shape=[jax.ShapeDtypeStruct((n, 1, rows, cols), BF16)] * 8,
        cost_estimate=pl.CostEstimate(
            flops=0, transcendentals=0, bytes_accessed=2 * 8 * n * rows * cols * 2
        ),
        name="split_ffn",
    )(zidx, yidx, *ins)
    return [[[outs[h * 4 + dx * 2 + a] for a in range(2)] for dx in range(2)] for h in range(2)]


def bias_tiles(line, blocks):
    heads, _, length = line.shape
    spans = 2 * blocks - 1
    width = 2 * BLOCK

    def kernel(line_ref, out_ref):
        row = lax.broadcasted_iota(jnp.int32, (8, width), 0)
        for d in range(spans):
            start = (spans - 1 - d) * BLOCK
            window = line_ref[0, :, start : start + width]
            turned = jnp.concatenate([window[:, BLOCK:], window[:, :BLOCK]], axis=1)
            tile = jnp.broadcast_to(turned, (8, width))
            for bit in (1, 2, 4):
                tile = jnp.where((row & bit) != 0, pltpu.roll(tile, bit, 1), tile)
            size = 8
            while size < BLOCK:
                tile = jnp.concatenate([tile, pltpu.roll(tile, size, 1)], axis=0)
                size *= 2
            out_ref[0, d] = tile[:, :BLOCK]

    return pl.pallas_call(
        kernel,
        grid=(heads,),
        in_specs=[pl.BlockSpec((1, 1, length), lambda h: (h, 0, 0))],
        out_specs=pl.BlockSpec((1, spans, BLOCK, BLOCK), lambda h: (h, 0, 0, 0)),
        out_shape=jax.ShapeDtypeStruct((heads, spans, BLOCK, BLOCK), F32),
        cost_estimate=pl.CostEstimate(
            flops=heads * spans * BLOCK * BLOCK * 8,
            transcendentals=0,
            bytes_accessed=heads * spans * BLOCK * BLOCK * 4,
        ),
        name="bias_tiles",
    )(line)


def diagonal_sums(tile):
    width = 2 * BLOCK
    t = jnp.concatenate([tile, jnp.zeros_like(tile)], axis=1)
    size = BLOCK
    while size > 8:
        size //= 2
        t = t[:size] + pltpu.roll(t[size:], width - size, 1)
    row = lax.broadcasted_iota(jnp.int32, (8, width), 0)
    for bit in (1, 2, 4):
        t = jnp.where((row & bit) != 0, pltpu.roll(t, width - bit, 1), t)
    return jnp.sum(t, axis=0, keepdims=True)


def head_keys(keys, limit, a):
    lane = lax.broadcasted_iota(jnp.int32, keys.shape, 1)
    place = lax.broadcasted_iota(jnp.int32, keys.shape, 0)
    mine = (lane // (PAIR // 2)) == a
    flag = jnp.where(place < limit, 0.0, MASK_VALUE)
    other = jnp.where(lane == (1 - a) * (PAIR // 2), flag, 0.0)
    return bf(jnp.where(mine, wide(keys), other))


def head_queries(queries, scale, a, mark):
    lane = lax.broadcasted_iota(jnp.int32, queries.shape, 1)
    mine = (lane // (PAIR // 2)) == a
    other = jnp.where(lane == (1 - a) * (PAIR // 2), mark, 0.0)
    return bf(jnp.where(mine, wide(queries) * scale, other))


def only_head(values, a):
    lane = lax.broadcasted_iota(jnp.int32, values.shape, 1)
    return bf(jnp.where((lane // (PAIR // 2)) == a, wide(values), 0.0))


def score_blocks(key_a, query_a, bias_ref, a, qb, key_blocks, causal):
    out = []
    for kb in range(key_blocks):
        st = dot_nt(key_a[kb * BLOCK : (kb + 1) * BLOCK], query_a)
        if bias_ref is not None:
            st = st + bias_ref[a, kb - qb + key_blocks - 1]
        if causal:
            kpos = lax.broadcasted_iota(jnp.int32, st.shape, 0)
            qpos = lax.broadcasted_iota(jnp.int32, st.shape, 1)
            st = jnp.where(kpos <= qpos, st, MASK_VALUE)
        out.append(st)
    return out


def attention_forward(queries, memory, limit, bias, causal, fused):
    query_len = queries.shape[0]
    key_len = query_len if fused else memory.shape[0]
    pairs = queries.shape[1] // ((3 if fused else 1) * PAIR)
    key_blocks, query_blocks = key_len // BLOCK, query_len // BLOCK
    scale = (PAIR // 2) ** (-0.5)

    def kernel(limit_ref, q_ref, *refs):
        refs = list(refs)
        kv_ref = q_ref if fused else refs.pop(0)
        bias_ref = refs.pop(0) if bias is not None else None
        c_ref, lse_ref = refs
        k0 = PAIR if fused else 0
        keys = kv_ref[:, k0 : k0 + PAIR]
        values = kv_ref[:, k0 + PAIR : k0 + 2 * PAIR]
        key_a = [head_keys(keys, limit_ref[0], a) for a in range(2)]

        def visit(qb):
            rows = pl.ds(pl.multiple_of(qb * BLOCK, BLOCK), BLOCK)
            q = q_ref[rows, 0:PAIR]
            parts = []
            for a in range(2):
                st = score_blocks(
                    key_a[a], head_queries(q, scale, a, 1.0), bias_ref, a, qb, key_blocks, causal
                )
                top = functools.reduce(
                    jnp.maximum, [jnp.max(b, axis=0, keepdims=True) for b in st]
                )
                ex = [jnp.exp(b - top) for b in st]
                total = sum(jnp.sum(b, axis=0, keepdims=True) for b in ex)
                ct = sum(
                    dot_tn(values[kb * BLOCK : (kb + 1) * BLOCK], bf(ex[kb]))
                    for kb in range(key_blocks)
                )
                parts.append(ct[a * (PAIR // 2) : (a + 1) * (PAIR // 2)] * (1.0 / total))
                lse_ref[0, a : a + 1, rows] = top + jnp.log(total)
            c_ref[rows, :] = bf(jnp.transpose(jnp.concatenate(parts, axis=0)))

        if query_blocks == 1:
            visit(0)
        else:
            pl.loop(0, query_blocks)(visit)

    in_specs = [pl.BlockSpec((query_len, (3 if fused else 1) * PAIR), lambda j, n: (0, j))]
    args = [queries]
    if not fused:
        in_specs.append(pl.BlockSpec((key_len, 2 * PAIR), lambda j, n: (0, j)))
        args.append(memory)
    if bias is not None:
        in_specs.append(pl.BlockSpec((2,) + bias.shape[1:], lambda j, n: (j, 0, 0, 0)))
        args.append(bias)
    return pl.pallas_call(
        kernel,
        grid_spec=pltpu.PrefetchScalarGridSpec(
            num_scalar_prefetch=1,
            grid=(pairs,),
            in_specs=in_specs,
            out_specs=[
                pl.BlockSpec((query_len, PAIR), lambda j, n: (0, j)),
                pl.BlockSpec((1, 8, query_len), lambda j, n: (j, 0, 0)),
            ],
        ),
        out_shape=[
            jax.ShapeDtypeStruct((query_len, pairs * PAIR), BF16),
            jax.ShapeDtypeStruct((pairs, 8, query_len), F32),
        ],
        compiler_params=pltpu.CompilerParams(vmem_limit_bytes=40 << 20),
        cost_estimate=pl.CostEstimate(
            flops=pairs * 2 * query_len * key_len * PAIR * 4,
            transcendentals=pairs * 2 * query_len * key_len,
            bytes_accessed=pairs * PAIR * 2 * 2 * (query_len + key_len),
        ),
        name="attend_" + ("enc" if bias is not None else "dec" if fused else "cross"),
    )(limit, *args)


def attention_backward(queries, memory, limit, bias, causal, fused, context, lse, context_grad):
    query_len = queries.shape[0]
    key_len = query_len if fused else memory.shape[0]
    pairs = queries.shape[1] // ((3 if fused else 1) * PAIR)
    key_blocks, query_blocks = key_len // BLOCK, query_len // BLOCK
    spans = 2 * key_blocks - 1
    scale = (PAIR // 2) ** (-0.5)

    def kernel(limit_ref, q_ref, *refs):
        refs = list(refs)
        kv_ref = q_ref if fused else refs.pop(0)
        bias_ref = refs.pop(0) if bias is not None else None
        c_ref, lse_ref, dc_ref = refs[:3]
        refs = refs[3:]
        dq_ref = refs.pop(0)
        dkv_ref = dq_ref if fused else refs.pop(0)
        diag_ref = refs.pop(0) if bias is not None else None
        dk_acc, dv_acc = refs[:2]
        tile_acc = refs[2] if bias is not None else None
        k0 = PAIR if fused else 0
        keys = kv_ref[:, k0 : k0 + PAIR]
        values = kv_ref[:, k0 + PAIR : k0 + 2 * PAIR]
        key_a = [head_keys(keys, limit_ref[0], a) for a in range(2)]
        pure_key_a = [only_head(keys, a) for a in range(2)]
        value_a = [only_head(values, a) for a in range(2)]
        dk_acc[...] = jnp.zeros_like(dk_acc)
        dv_acc[...] = jnp.zeros_like(dv_acc)
        if bias is not None:
            tile_acc[...] = jnp.zeros_like(tile_acc)

        def visit(qb):
            rows = pl.ds(pl.multiple_of(qb * BLOCK, BLOCK), BLOCK)
            q = q_ref[rows, 0:PAIR]
            dc = dc_ref[rows, :]
            both = jnp.transpose(wide(dc) * wide(c_ref[rows, :]))
            dqt = jnp.zeros((PAIR, BLOCK), F32)
            for a in range(2):
                st = score_blocks(
                    key_a[a], head_queries(q, scale, a, 1.0), bias_ref, a, qb, key_blocks, causal
                )
                delta = jnp.sum(
                    both[a * (PAIR // 2) : (a + 1) * (PAIR // 2)], axis=0, keepdims=True
                )
                log_row = lse_ref[0, a : a + 1, rows]
                dc_a = only_head(dc, a)
                q_a = head_queries(q, scale, a, 0.0)
                for kb in range(key_blocks):
                    span = slice(kb * BLOCK, (kb + 1) * BLOCK)
                    p = jnp.exp(st[kb] - log_row)
                    dp = dot_nt(value_a[a][span], dc)
                    ds = p * (dp - delta)
                    dsb = bf(ds)
                    dv_acc[span, :] += dot_nn(bf(p), dc_a)
                    dk_acc[span, :] += dot_nn(dsb, q_a)
                    dqt = dqt + dot_tn(pure_key_a[a][span], dsb)
                    if bias is not None:
                        tile_acc[a, kb - qb + key_blocks - 1] += ds
            dq_ref[rows, 0:PAIR] = bf(jnp.transpose(dqt) * scale)

        if query_blocks == 1:
            visit(0)
        else:
            pl.loop(0, query_blocks)(visit)
        dkv_ref[:, k0 : k0 + PAIR] = bf(dk_acc[...])
        dkv_ref[:, k0 + PAIR : k0 + 2 * PAIR] = bf(dv_acc[...])
        if bias is not None:
            for a in range(2):
                for d in range(spans):
                    diag_ref[a, d : d + 1, :] = diagonal_sums(tile_acc[a, d])

    in_specs = [pl.BlockSpec((query_len, (3 if fused else 1) * PAIR), lambda j, n: (0, j))]
    args = [queries]
    if not fused:
        in_specs.append(pl.BlockSpec((key_len, 2 * PAIR), lambda j, n: (0, j)))
        args.append(memory)
    if bias is not None:
        in_specs.append(pl.BlockSpec((2,) + bias.shape[1:], lambda j, n: (j, 0, 0, 0)))
        args.append(bias)
    in_specs += [
        pl.BlockSpec((query_len, PAIR), lambda j, n: (0, j)),
        pl.BlockSpec((1, 8, query_len), lambda j, n: (j, 0, 0)),
        pl.BlockSpec((query_len, PAIR), lambda j, n: (0, j)),
    ]
    args += [context, lse, context_grad]
    out_specs = [pl.BlockSpec((query_len, (3 if fused else 1) * PAIR), lambda j, n: (0, j))]
    out_shape = [jax.ShapeDtypeStruct(queries.shape, BF16)]
    scratch = [pltpu.VMEM((key_len, PAIR), F32)] * 2
    if not fused:
        out_specs.append(pl.BlockSpec((key_len, 2 * PAIR), lambda j, n: (0, j)))
        out_shape.append(jax.ShapeDtypeStruct(memory.shape, BF16))
    if bias is not None:
        out_specs.append(pl.BlockSpec((2, 8, 2 * BLOCK), lambda j, n: (j, 0, 0)))
        out_shape.append(jax.ShapeDtypeStruct((2 * pairs, 8, 2 * BLOCK), F32))
        scratch.append(pltpu.VMEM((2, spans, BLOCK, BLOCK), F32))
    return pl.pallas_call(
        kernel,
        grid_spec=pltpu.PrefetchScalarGridSpec(
            num_scalar_prefetch=1,
            grid=(pairs,),
            in_specs=in_specs,
            out_specs=out_specs,
            scratch_shapes=scratch,
        ),
        out_shape=out_shape,
        compiler_params=pltpu.CompilerParams(vmem_limit_bytes=40 << 20),
        cost_estimate=pl.CostEstimate(
            flops=pairs * 2 * query_len * key_len * PAIR * 10,
            transcendentals=pairs * 2 * query_len * key_len,
            bytes_accessed=pairs * PAIR * 2 * 4 * (query_len + key_len),
        ),
        name="attend_back_" + ("enc" if bias is not None else "dec" if fused else "cross"),
    )(limit, *args)


def gelu(z):
    return z * (0.5 * (1.0 + lax.erf(z * ROOT_HALF)))


def gelu_slope(z):
    return 0.5 * (1.0 + lax.erf(z * ROOT_HALF)) + z * jnp.exp(-0.5 * z * z) * INV_ROOT_TAU


def norm_forward(values, gain, offset):
    center = values - jnp.mean(values, axis=-1, keepdims=True)
    inv = lax.rsqrt(jnp.mean(center * center, axis=-1, keepdims=True) + EPSILON)
    normed = center * inv
    return normed * gain + offset, normed, inv


def norm_backward(upstream, normed, inv, gain):
    scaled = upstream * gain
    inner = (
        scaled
        - jnp.mean(scaled, axis=-1, keepdims=True)
        - normed * jnp.mean(scaled * normed, axis=-1, keepdims=True)
    )
    return inv * inner, jnp.sum(upstream * normed, axis=0), jnp.sum(upstream, axis=0)


def update(master, moment, average, gradient, rate, frame_total):
    mean_grad = gradient / frame_total
    new_moment = MOMENTUM * moment + mean_grad
    new_master = master - rate * (mean_grad + MOMENTUM * new_moment)
    new_average = AVERAGING * average + (1.0 - AVERAGING) * new_master
    return mean_grad, new_master, new_moment, new_average


def both_cores(part):
    low = bf(part)
    return wide(low) + wide(swap_core(low))


def order_cols(v0, v1):
    return jnp.concatenate(
        [v0[..., :PAIR], v1[..., :PAIR], v0[..., PAIR:], v1[..., PAIR:]], axis=-1
    )


def group_cols(v):
    half = PAIR // 2
    return (
        jnp.concatenate([v[..., :PAIR], v[..., 2 * PAIR : 2 * PAIR + half]], axis=-1),
        jnp.concatenate([v[..., PAIR : 2 * PAIR], v[..., 2 * PAIR + half :]], axis=-1),
    )


QKV_PLAN = [(m, j) for j in range(3) for m in range(3)]
ENC_PLANS = [QKV_PLAN, [(3, j) for j in range(3)]]
DEC_PLANS = [
    QKV_PLAN,
    [(3, j) for j in range(3)],
    [(4, j) for j in range(3)],
    [(m, j) for j in range(3) for m in (5, 6)],
    [(7, j) for j in range(3)],
]


def local(
    frames,
    cotangent,
    lengths,
    attn_master,
    attn_moment,
    attn_average,
    ffn_master,
    ffn_moment,
    ffn_average,
    norm_vecs,
    norm_moment,
    norm_average,
    col_bias,
    col_moment,
    col_average,
    rel_table,
    rel_moment,
    rel_average,
    dec_frames,
    dec_cotangent,
    text_lengths,
    dec_attn_master,
    dec_attn_moment,
    dec_attn_average,
    dec_ffn_master,
    dec_ffn_moment,
    dec_ffn_average,
    dec_norm_vecs,
    dec_norm_moment,
    dec_norm_average,
    dec_col_bias,
    dec_col_moment,
    dec_col_average,
):
    n_dp = lax.axis_size("dp")
    z, s, m = lax.axis_index("dp"), lax.axis_index("seq"), lax.axis_index("mp")
    y = m // 2
    utt_count, half_len, width = frames.shape
    text_half = dec_frames.shape[1]
    full_len, text_full = 2 * half_len, 2 * text_half
    order = jnp.arange(n_dp, dtype=jnp.int32)
    zidx = order if n_dp > 4 else (z - order) % n_dp
    yidx = jnp.stack([y, 1 - y]).astype(jnp.int32)
    root_frames = float(utt_count * full_len * n_dp) ** 0.5

    attn_pieces = gather_chunk(pack_attn(bf(attn_master)))
    ffn_pieces = gather_chunk(bf(ffn_master))
    dec_attn_pieces = gather_chunk(pack_attn(bf(dec_attn_master)))
    dec_ffn_pieces = gather_chunk(bf(dec_ffn_master))
    w_qkv, w_o = assemble_attn(attn_pieces, ENC_PLANS, 4, zidx, yidx)
    w_one, w_two = assemble_ffn(ffn_pieces, zidx, yidx)
    d_qkv, d_o, c_q, c_kv, c_o = assemble_attn(dec_attn_pieces, DEC_PLANS, 8, zidx, yidx)
    dw_one, dw_two = assemble_ffn(dec_ffn_pieces, zidx, yidx)

    bucket_count, group_heads = rel_table.shape
    group_width = attn_master.shape[2]
    unit_count = ffn_master.shape[2]
    packed = jnp.concatenate([col_bias, dec_col_bias, rel_table.T.reshape(-1)])
    groups = [spread(packed, 0), None]
    groups[1] = swap_mp(groups[0], 1)
    enc_cols, dec_cols = col_bias.shape[0], dec_col_bias.shape[0]

    def cols_at(start):
        return order_cols(*[g[start : start + group_width] for g in groups])

    def units_at(start):
        return jnp.concatenate([g[start : start + unit_count] for g in groups])

    def qkv_bias(q, v):
        blank = jnp.zeros((PAIR,), F32)
        cut = [slice(j * PAIR, (j + 1) * PAIR) for j in range(3)]
        return jnp.concatenate([part for c in cut for part in (q[c], blank, v[c])])

    bias_qkv = qkv_bias(cols_at(0), cols_at(group_width))
    bias_one = units_at(2 * group_width)
    bias_dqkv = qkv_bias(cols_at(enc_cols), cols_at(enc_cols + group_width))
    bias_cq = cols_at(enc_cols + 2 * group_width)
    cv = cols_at(enc_cols + 3 * group_width)
    blank = jnp.zeros((PAIR,), F32)
    bias_ckv = jnp.concatenate(
        [part for j in range(3) for part in (blank, cv[j * PAIR : (j + 1) * PAIR])]
    )
    bias_done = units_at(enc_cols + 4 * group_width)
    tables = [
        g[enc_cols + dec_cols :].reshape(group_heads, bucket_count) for g in groups
    ]
    heads = jnp.stack(
        [tables[0][0], tables[0][1], tables[1][0], tables[1][1], tables[0][2], tables[1][2]]
    )
    max_dist = bucket_count // 2
    blocks = full_len // BLOCK
    before = blocks * BLOCK - max_dist + 1
    after = blocks * BLOCK - max_dist - 1
    line = jnp.pad(heads[:, ::-1], ((0, 0), (before, after)), mode="edge")
    bias = bias_tiles(line[:, None, :], blocks)

    def all_rows(parts):
        mine = lax.dynamic_index_in_dim(parts, m, 0, keepdims=False)
        other = swap_core(mine)
        first = jnp.where(s == 0, mine, other)
        last = jnp.where(s == 0, other, mine)
        return jnp.concatenate([first, last], axis=0)

    inputs = all_rows(frames)
    text_in = all_rows(dec_frames)
    upstream_in = all_rows(cotangent)
    text_upstream = all_rows(dec_cotangent)
    limit = lax.dynamic_slice_in_dim(lengths, m, 1)
    text_limit = lax.dynamic_slice_in_dim(text_lengths, m, 1)
    frame_total = sum_dp(jnp.broadcast_to(wide(jnp.sum(lengths)), (8, 128)))[0, 0]

    def to_owners(rows):
        count = rows.shape[0] // 2
        mine = lax.dynamic_slice_in_dim(rows, s * count, count, 0)
        cut = count // 2
        a, b = mine[:cut], mine[cut:]
        ax, by = swap_mp(a, 1), swap_mp(b, 2)
        ay, axy = swap_mp(a, 2), swap_mp(ax, 2)
        bx, byx = swap_mp(b, 1), swap_mp(by, 1)
        out = jnp.zeros((utt_count, count, width), rows.dtype)
        for bits, top, low in ((0, a, b), (1, ax, bx), (2, ay, by), (3, axy, byx)):
            out = lax.dynamic_update_slice(out, top[None], (m ^ bits, 0, 0))
            out = lax.dynamic_update_slice(out, low[None], (m ^ bits, cut, 0))
        return out

    qkv = bf(dot_nn(inputs, w_qkv) + bias_qkv)
    context, lse = attention_forward(qkv, None, limit, bias, False, True)
    attn_sum = both_cores(dot_nt(context, w_o))
    hidden_one, normed_one, inv_one = norm_forward(
        wide(inputs) + attn_sum + norm_vecs[4], norm_vecs[0], norm_vecs[1]
    )
    hidden_low = bf(hidden_one)
    gate_in = dot_nn(hidden_low, w_one) + bias_one
    activated = bf(gelu(gate_in))
    ffn_sum = both_cores(dot_nt(activated, w_two))
    result, normed_two, inv_two = norm_forward(
        hidden_one + ffn_sum + norm_vecs[5], norm_vecs[2], norm_vecs[3]
    )
    enc_low = bf(result)
    out_enc = to_owners(enc_low)

    dqkv = bf(dot_nn(text_in, d_qkv) + bias_dqkv)
    self_context, self_lse = attention_forward(dqkv, None, text_limit, None, True, True)
    self_sum = both_cores(dot_nt(self_context, d_o))
    dec_one, normed_d1, inv_d1 = norm_forward(
        wide(text_in) + self_sum + dec_norm_vecs[6], dec_norm_vecs[0], dec_norm_vecs[1]
    )
    dec_one_low = bf(dec_one)
    cross_q = bf(dot_nn(dec_one_low, c_q) + bias_cq)
    cross_kv = bf(dot_nn(enc_low, c_kv) + bias_ckv)
    cross_context, cross_lse = attention_forward(cross_q, cross_kv, limit, None, False, False)
    cross_sum = both_cores(dot_nt(cross_context, c_o))
    dec_two, normed_d2, inv_d2 = norm_forward(
        dec_one + cross_sum + dec_norm_vecs[7], dec_norm_vecs[2], dec_norm_vecs[3]
    )
    dec_two_low = bf(dec_two)
    dec_gate = dot_nn(dec_two_low, dw_one) + bias_done
    dec_act = bf(gelu(dec_gate))
    dec_ffn_sum = both_cores(dot_nt(dec_act, dw_two))
    dec_result, normed_d3, inv_d3 = norm_forward(
        dec_two + dec_ffn_sum + dec_norm_vecs[8], dec_norm_vecs[4], dec_norm_vecs[5]
    )
    out_dec = to_owners(bf(dec_result))

    text_places = lax.broadcasted_iota(jnp.int32, (text_full, 1), 0)
    dec_up = jnp.where(text_places < text_limit[0], wide(text_upstream), 0.0)
    grad_d3, gain_d3, shift_d3 = norm_backward(dec_up, normed_d3, inv_d3, dec_norm_vecs[4])
    dec_ffn_back = bf(grad_d3)
    dec_gate_grad = bf(dot_nn(dec_ffn_back, dw_two) * gelu_slope(dec_gate))
    grad_h2 = grad_d3 + both_cores(dot_nt(dec_gate_grad, dw_one))
    dec_ffn_grads = [
        bf(dot_tn(dec_two_low, dec_gate_grad)),
        bf(dot_tn(dec_ffn_back, dec_act)),
    ]
    dec_ffn_total = scatter_chunk(split_ffn(dec_ffn_grads, zidx, yidx))

    grad_d2, gain_d2, shift_d2 = norm_backward(grad_h2, normed_d2, inv_d2, dec_norm_vecs[2])
    cross_back = bf(grad_d2)
    cross_qg, cross_kvg = attention_backward(
        cross_q,
        cross_kv,
        limit,
        None,
        False,
        False,
        cross_context,
        cross_lse,
        bf(dot_nn(cross_back, c_o)),
    )
    memory_back = both_cores(dot_nt(cross_kvg, c_kv))
    grad_h1 = grad_d2 + both_cores(dot_nt(cross_qg, c_q))
    grad_d1, gain_d1, shift_d1 = norm_backward(grad_h1, normed_d1, inv_d1, dec_norm_vecs[0])
    self_back = bf(grad_d1)
    (self_g,) = attention_backward(
        dqkv,
        None,
        text_limit,
        None,
        True,
        True,
        self_context,
        self_lse,
        bf(dot_nn(self_back, d_o)),
    )
    text_grad = grad_d1 + both_cores(dot_nt(self_g, d_qkv))
    dec_attn_grads = [
        bf(dot_tn(text_in, self_g)),
        bf(dot_tn(self_back, self_context)),
        bf(dot_tn(dec_one_low, cross_qg)),
        bf(dot_tn(enc_low, cross_kvg)),
        bf(dot_tn(cross_back, cross_context)),
    ]
    dec_attn_total = unpack_attn(
        scatter_chunk(split_attn(dec_attn_grads, DEC_PLANS, 8, zidx, yidx)), 8
    )
    out_text_grad = to_owners(bf(text_grad))

    places = lax.broadcasted_iota(jnp.int32, (full_len, 1), 0)
    upstream = jnp.where(places < limit[0], wide(upstream_in), 0.0) + memory_back
    grad_two, gain_two, shift_two = norm_backward(upstream, normed_two, inv_two, norm_vecs[2])
    ffn_back = bf(grad_two)
    gate_grad = bf(dot_nn(ffn_back, w_two) * gelu_slope(gate_in))
    hidden_grad = grad_two + both_cores(dot_nt(gate_grad, w_one))
    ffn_grads = [bf(dot_tn(hidden_low, gate_grad)), bf(dot_tn(ffn_back, activated))]
    ffn_total = scatter_chunk(split_ffn(ffn_grads, zidx, yidx))
    grad_one, gain_one, shift_one = norm_backward(hidden_grad, normed_one, inv_one, norm_vecs[0])
    attn_back = bf(grad_one)
    enc_g, diag = attention_backward(
        qkv, None, limit, bias, False, True, context, lse, bf(dot_nn(attn_back, w_o))
    )
    input_grad = grad_one + both_cores(dot_nt(enc_g, w_qkv))
    attn_grads = [bf(dot_tn(inputs, enc_g)), bf(dot_tn(attn_back, context))]
    attn_total = unpack_attn(
        scatter_chunk(split_attn(attn_grads, ENC_PLANS, 4, zidx, yidx)), 4
    )
    out_input_grad = to_owners(bf(input_grad))

    def col_sum(a):
        return jnp.sum(a, axis=0, dtype=F32)

    def pick(v, stride, at):
        return jnp.concatenate(
            [v[(j * stride + at) * PAIR : (j * stride + at + 1) * PAIR] for j in range(3)]
        )

    enc_sum, dec_sum, kv_sum = col_sum(enc_g), col_sum(self_g), col_sum(cross_kvg)
    col_parts = [
        group_cols(pick(enc_sum, 3, 0)),
        group_cols(pick(enc_sum, 3, 2)),
        jnp.split(col_sum(gate_grad), 2),
        group_cols(pick(dec_sum, 3, 0)),
        group_cols(pick(dec_sum, 3, 2)),
        group_cols(col_sum(cross_qg)),
        group_cols(pick(kv_sum, 2, 1)),
        jnp.split(col_sum(dec_gate_grad), 2),
    ]
    turned = jnp.concatenate([diag[:, :, BLOCK:], diag[:, :, :BLOCK]], axis=-1)
    span_count = 2 * blocks - 1
    line_grad = sum(
        jnp.pad(
            turned[:, d],
            ((0, 0), ((span_count - 1 - d) * BLOCK, d * BLOCK)),
        )
        for d in range(span_count)
    )
    first_bucket = jnp.sum(line_grad[:, before + bucket_count :], axis=1, keepdims=True)
    last_bucket = jnp.sum(line_grad[:, :before], axis=1, keepdims=True)
    head_grad = line_grad[:, before : before + bucket_count][:, ::-1]
    head_grad = jnp.concatenate(
        [
            head_grad[:, :1] + first_bucket,
            head_grad[:, 1:-1],
            head_grad[:, -1:] + last_bucket,
        ],
        axis=1,
    )
    table_parts = (head_grad[jnp.array([0, 1, 4])], head_grad[jnp.array([2, 3, 5])])
    norm_local = jnp.stack(
        [gain_one, shift_one, gain_two, shift_two, jnp.sum(grad_one, 0), jnp.sum(grad_two, 0)]
    )
    dec_norm_local = jnp.stack(
        [
            gain_d1,
            shift_d1,
            gain_d2,
            shift_d2,
            gain_d3,
            shift_d3,
            jnp.sum(grad_d1, 0),
            jnp.sum(grad_d2, 0),
            jnp.sum(grad_d3, 0),
        ]
    )
    shared = jnp.concatenate([norm_local.reshape(-1), dec_norm_local.reshape(-1)])
    vectors = [
        jnp.concatenate([p[dx] for p in col_parts] + [table_parts[dx].reshape(-1), shared])
        for dx in range(2)
    ]
    small = unspread(vectors[0] + swap_mp(vectors[1], 1), 0)
    small = sum_dp(small + swap_core(small))
    cut = [enc_cols, dec_cols, group_heads * bucket_count, norm_vecs.size, dec_norm_vecs.size]
    ends = [sum(cut[: i + 1]) for i in range(len(cut))]
    col_total, dec_col_total, table_total, norm_total, dec_norm_total, _ = jnp.split(small, ends)
    table_total = table_total.reshape(group_heads, bucket_count).T
    norm_total = norm_total.reshape(norm_vecs.shape)
    dec_norm_total = dec_norm_total.reshape(dec_norm_vecs.shape)

    matrix_rate = MATRIX_RATE * root_frames
    vector_rate = VECTOR_RATE * root_frames
    attn_new = update(attn_master, attn_moment, attn_average, attn_total, matrix_rate, frame_total)
    ffn_new = update(ffn_master, ffn_moment, ffn_average, ffn_total, matrix_rate, frame_total)
    norm_new = update(norm_vecs, norm_moment, norm_average, norm_total, vector_rate, frame_total)
    col_new = update(col_bias, col_moment, col_average, col_total, vector_rate, frame_total)
    rel_new = update(rel_table, rel_moment, rel_average, table_total, vector_rate, frame_total)
    dattn_new = update(
        dec_attn_master, dec_attn_moment, dec_attn_average, dec_attn_total, matrix_rate, frame_total
    )
    dffn_new = update(
        dec_ffn_master, dec_ffn_moment, dec_ffn_average, dec_ffn_total, matrix_rate, frame_total
    )
    dnorm_new = update(
        dec_norm_vecs, dec_norm_moment, dec_norm_average, dec_norm_total, vector_rate, frame_total
    )
    dcol_new = update(
        dec_col_bias, dec_col_moment, dec_col_average, dec_col_total, vector_rate, frame_total
    )
    return (
        out_enc,
        out_input_grad,
        attn_new[0],
        ffn_new[0],
        *attn_new[1:],
        bf(attn_new[1]),
        *ffn_new[1:],
        bf(ffn_new[1]),
        *norm_new[1:],
        *col_new[1:],
        *rel_new[1:],
        out_dec,
        out_text_grad,
        dattn_new[0],
        dffn_new[0],
        *dattn_new[1:],
        bf(dattn_new[1]),
        *dffn_new[1:],
        bf(dffn_new[1]),
        *dnorm_new[1:],
        *dcol_new[1:],
    )


def solution(mesh):
    rows = P("dp", "seq", None)
    matrix = P(None, ("dp", "seq"), "mp")
    table = P(None, "mp")
    enc_params = [matrix] * 6 + [P()] * 3 + [P("mp")] * 3 + [table] * 3
    dec_params = [matrix] * 6 + [P()] * 3 + [P("mp")] * 3
    in_specs = (rows, rows, P("dp"), *enc_params, rows, rows, P("dp"), *dec_params)
    out_specs = (
        [rows, rows]
        + [matrix] * 10
        + [P()] * 3
        + [P("mp")] * 3
        + [table] * 3
        + [rows, rows]
        + [matrix] * 10
        + [P()] * 3
        + [P("mp")] * 3
    )
    return jax.shard_map(
        local, mesh=mesh, in_specs=in_specs, out_specs=tuple(out_specs), check_vma=False
    )
```

time: 1810 us -> 803 us (0.44)
  local copies, waits for them, and re-layouts: 850 us -> 54.2 us
  waiting for transfers between devices: 563 us -> 221 us
  starting transfers between devices: 2.44 us -> 233 us
  matrix products: 180 us -> 64.1 us
  Pallas kernels: 0 us -> 104 us
  blocking collectives: 35.4 us -> 0 us
  other arithmetic: 135 us -> 107 us
    unnamed x370 -> x353, local copies, waits for them, and re-layouts: 514 us -> 17.3 us
    psum x8 -> x0, waiting for transfers between devices: 456 us -> none  [the longest x2 136 us: unit_back(): lax.psum(partial_value.astype(jnp.bfloat16), 'mp').astype(jnp.float32)]
    ppermute x0 -> x146, starting transfers between devices: none -> 233 us  [the longest x25 58.7 us: unspread(): lax.ppermute(v, ('seq', 'mp'), [(d, s) for s, d in spread_perm(flip)])]
    ppermute x0 -> x146, waiting for transfers between devices: none -> 221 us  [the longest x50 126 us: swap_mp(): return lax.ppermute(v, 'mp', [(m, m ^ bits) for m in range(4)])]
    rev x5 -> x0, local copies, waits for them, and re-layouts: 128 us -> none  [the longest x4 105 us: collect_diagonals(): flipped = grid[:, ::-1, :]]
    dot_general x93 -> x33, matrix products: 180 us -> 64.1 us  [the longest x11 24.7 us: dot_tn(): lax.dot_general(left, right, (((0,), (0,)), ((), ())), preferred_element_...]
    pallas_call x0 -> x15, Pallas kernels: none -> 104 us  [the longest x3 31.9 us: attention_backward(): pl.pallas_call(kernel, grid_spec=pltpu.PrefetchScalarGridSpec(num_scalar_...]
    all_gather x8 -> x0, waiting for transfers between devices: 92.6 us -> none  [the longest x1 32 us: local(): lax.all_gather(dec_ffn_master.astype(jnp.bfloat16), ('dp', 'seq'), axis=1...]
  transfers between devices with their start and end apart: 30 -> 146, of which waited for: 15 -> 39; matrix products, arithmetic and copies ran while one was open for 33% -> 24% of each run, Pallas kernels for 0% -> 13%
where the time goes in v1:
time: 803 us; the launch traced here: 788 us
  starting transfers between devices  233 us (29%)
  waiting for transfers between devices  221 us (28%)
  other arithmetic  107 us (13%)
  Pallas kernels  104 us (13%)
  matrix products  64.1 us (8%)
  local copies, waits for them, and re-layouts  54.2 us (7%)
    ppermute x50, waiting for transfers between devices, swap_mp(): return lax.ppermute(v, 'mp', [(m, m ^ bits) for m in range(4)])  126 us
    ppermute x30, waiting for transfers between devices, shift_dp(): return lax.ppermute(v, 'dp', [(i, (i + k) % n) for i in range(n)])  60 us
    ppermute x25, starting transfers between devices, unspread(): lax.ppermute(v, ('seq', 'mp'), [(d, s) for s, d in spread_perm(flip)])  58.7 us
    ppermute x25, starting transfers between devices, spread(): return lax.ppermute(v, ('seq', 'mp'), spread_perm(flip))  55.7 us
    ppermute x30, starting transfers between devices, shift_dp(): return lax.ppermute(v, 'dp', [(i, (i + k) % n) for i in range(n)])  55.5 us
    ppermute x50, starting transfers between devices, swap_mp(): return lax.ppermute(v, 'mp', [(m, m ^ bits) for m in range(4)])  51.2 us
    pallas_call x3, Pallas kernels, attention_backward(): pl.pallas_call(kernel, grid_spec=pltpu.PrefetchScalarGridSpec(num_scalar_...  31.9 us
    dot_general x11, matrix products, dot_tn(): lax.dot_general(left, right, (((0,), (0,)), ((), ())), preferred_element_...  24.7 us
  transfers between devices with their start and end apart: 146, of which 39 were waited for; matrix products, arithmetic and copies ran while one was open for 24% of the time, Pallas kernels for 13%

profile of v1, /device:TPU:0, one launch (start us, length us, event | category | flops | bytes accessed | tf_op | source)
XLA Modules:
  0.0 788.4 jit_solution(13081149444046428019)
XLA Ops:
  39.9 6.6 bias_tiles.1.refs_0_
  67.0 22.7 %collective-permute-done.38 = bf16[12,96,128]{2,1,0:T(8,128)(2,1)S(1)} collective-permute-done((bf16[12,96,128]{2,1,0:T(8,128)(2,1)S(1)}, bf16[12,96,128]{2,1,0:T(8,128)(2,1)S(1)}, u32[]{:S(2)}, u32[]{:S(2)}) %collective-permute-start.38) | collective-permute-done | bytes 294944 | tf_op jit(solution)/shard_map/ppermute | solution.py:71
  92.0 10.6 %collective-permute-done.52 = bf16[2,96,768]{2,1,0:T(8,128)(2,1)S(1)} collective-permute-done((bf16[2,96,768]{2,1,0:T(8,128)(2,1)S(1)}, bf16[2,96,768]{2,1,0:T(8,128)(2,1)S(1)}, u32[]{:S(2)}, u32[]{:S(2)}) %collective-permute-start.52) | collective-permute-done | bytes 294944 | tf_op jit(solution)/shard_map/ppermute | solution.py:71
  115.5 6.1 collective-permute-start.25
  127.5 14.2 %collective-permute-done.8.refs_3_ = bf16[4,3,96,128]{3,2,1,0:T(8,128)(2,1)S(1)} collective-permute-done((bf16[4,3,96,128]{3,2,1,0:T(8,128)(2,1)S(1)}, bf16[4,3,96,128]{3,2,1,0:T(8,128)(2,1)S(1)}, u32[]{:S(2)}, u32[]{:S(2)}) %collective-permute-start.8) | collective-permute-done | bytes 294944 | tf_op jit(solution)/shard_map/ppermute | solution.py:62
  144.2 6.0 collective-permute-start.45
  163.9 6.0 collective-permute-start.22
  180.7 12.7 %attend_enc.1 = (bf16[768,384]{1,0:T(8,128)(2,1)S(1)}, f32[3,8,768]{2,1,0:T(8,128)S(1)}) custom-call(s32[1]{0:T(128)} %dynamic_slice.33.limit_ref, bf16[768,1152]{1,0:T(8,128)(2,1)S(1)} %fusion.6.q_ref, f32[6,5,256,256]{3,2,1,0:T(8,128)S(1)} %copy-done), custom_call_target="tpu_custom_call" | custom-call | flops 1811939328 | bytes 2359296 | tf_op jit(solution)/shard_map/attend_enc/pallas_call | solution.py:431
  195.4 6.0 collective-permute-start.43
  205.3 5.8 assemble_ffn.2
  211.1 6.8 collective-permute-done.47.refs_6_
  217.9 12.2 %collective-permute-done.48.refs_7_ = bf16[4,6,96,128]{3,2,1,0:T(8,128)(2,1)} collective-permute-done((bf16[4,6,96,128]{3,2,1,0:T(8,128)(2,1)}, bf16[4,6,96,128]{3,2,1,0:T(8,128)(2,1)}, u32[]{:S(2)}, u32[]{:S(2)}) %collective-permute-start.48) | collective-permute-done | bytes 589856 | tf_op jit(solution)/shard_map/ppermute | solution.py:49
  230.1 6.2 collective-permute-start.59
  237.7 6.0 assemble_attn.3
  280.7 11.3 %collective-permute-done.62.refs_7_ = bf16[4,1,96,768]{3,2,1,0:T(8,128)(2,1)} collective-permute-done((bf16[4,1,96,768]{3,2,1,0:T(8,128)(2,1)}, bf16[4,1,96,768]{3,2,1,0:T(8,128)(2,1)}, u32[]{:S(2)}, u32[]{:S(2)}) %collective-permute-start.62) | collective-permute-done | bytes 589856 | tf_op jit(solution)/shard_map/ppermute | solution.py:49
  291.9 5.7 assemble_ffn.3
  363.7 13.4 %collective-permute-done.113 = bf16[64,768]{1,0:T(8,128)(2,1)S(1)} collective-permute-done((bf16[64,768]{1,0:T(8,128)(2,1)}, bf16[64,768]{1,0:T(8,128)(2,1)S(1)}, u32[]{:S(2)}, u32[]{:S(2)}) %collective-permute-start.113) | collective-permute-done | bytes 98336 | tf_op jit(solution)/shard_map/ppermute | solution.py:49
  386.6 6.1 attend_back_cross.1
  408.9 6.0 collective-permute-start.140
  431.4 6.0 collective-permute-start.122
  437.4 6.0 collective-permute-start.124
  453.7 11.6 %collective-permute-done.116 = bf16[64,768]{1,0:T(8,128)(2,1)S(1)} collective-permute-done((bf16[64,768]{1,0:T(8,128)(2,1)S(1)}, bf16[64,768]{1,0:T(8,128)(2,1)S(1)}, u32[]{:S(2)}, u32[]{:S(2)}) %collective-permute-start.116) | collective-permute-done | bytes 98336 | tf_op jit(solution)/shard_map/ppermute | solution.py:49
  481.5 7.2 collective-permute-start.143
  509.1 6.0 collective-permute-start.128
  562.0 6.2 collective-permute-done.93
  572.9 6.7 collective-permute-done.97
  584.4 6.3 collective-permute-start.96
  612.2 22.6 %attend_back_enc.1 = (bf16[768,1152]{1,0:T(8,128)(2,1)S(1)}, f32[6,8,512]{2,1,0:T(8,128)S(1)}) custom-call(s32[1]{0:T(128)} %dynamic_slice.33.limit_ref, bf16[768,1152]{1,0:T(8,128)(2,1)S(1)} %fusion.6.q_ref, f32[6,5,256,256]{3,2,1,0:T(8,128)S(1)} %bitcast.321, bf16[768,384]{1,0:T(8,128)(2,1)S(1)} %get-tuple-element.93.refs_1_, ...), custom_call_target="tpu_custom_call" | custom-call | flops 4529848320 | bytes 4718592 | tf_op jit(solution)/shard_map/attend_back_enc/pallas_call | solution.py:550
  680.7 5.9 collective-permute-start.101
  686.6 7.5 collective-permute-done.107
  751.2 6.1 collective-permute-done.85
  773.3 6.7 collective-permute-done.72
  (965 shorter events, 508.3 us)
Async XLA Ops:
  2.0 45.2 %collective-permute-start.1 = (bf16[6,96,128]{2,1,0:T(8,128)(2,1)S(1)}, bf16[6,96,128]{2,1,0:T(8,128)(2,1)}, u32[]{:S(2)}, u32[]{:S(2)}) collective-permute-start(bf16[6,96,128]{2,1,0:T(8,128)(2,1)S(1)} %maximum_maximum_fusion.1), channel_id=1, source_target_pairs={{0,8},{8,16},{16,24},{24,0},{1,9},{9,17},{17,25},{25,1},{2,10},{10... | collective-permute-start | bytes 442376 | tf_op jit(solution)/shard_map/ppermute | solution.py:71
  5.1 44.0 %collective-permute-start.2 = (bf16[6,96,128]{2,1,0:T(8,128)(2,1)S(1)}, bf16[6,96,128]{2,1,0:T(8,128)(2,1)}, u32[]{:S(2)}, u32[]{:S(2)}) collective-permute-start(bf16[6,96,128]{2,1,0:T(8,128)(2,1)S(1)} %maximum_maximum_fusion.1), channel_id=1, source_target_pairs={{0,16},{8,24},{16,0},{24,8},{1,17},{9,25},{17,1},{25,9},{2,18},{10... | collective-permute-start | bytes 442376 | tf_op jit(solution)/shard_map/ppermute | solution.py:71
  54.3 35.4 %collective-permute-start.38 = (bf16[12,96,128]{2,1,0:T(8,128)(2,1)S(1)}, bf16[12,96,128]{2,1,0:T(8,128)(2,1)S(1)}, u32[]{:S(2)}, u32[]{:S(2)}) collective-permute-start(bf16[12,96,128]{2,1,0:T(8,128)(2,1)S(1)} %maximum_maximum_fusion), channel_id=1, source_target_pairs={{0,16},{8,24},{16,0},{24,8},{1,17},{9,25},{17,1},{25,9},{2,18},{10... | collective-permute-start | bytes 884744 | tf_op jit(solution)/shard_map/ppermute | solution.py:71
  55.4 35.0 %collective-permute-start.39 = (bf16[12,96,128]{2,1,0:T(8,128)(2,1)S(1)}, bf16[12,96,128]{2,1,0:T(8,128)(2,1)S(1)}, u32[]{:S(2)}, u32[]{:S(2)}) collective-permute-start(bf16[12,96,128]{2,1,0:T(8,128)(2,1)S(1)} %maximum_maximum_fusion), channel_id=1, source_target_pairs={{0,24},{8,0},{16,8},{24,16},{1,25},{9,1},{17,9},{25,17},{2,26},{10... | collective-permute-start | bytes 884744 | tf_op jit(solution)/shard_map/ppermute | solution.py:71
  59.4 43.2 %collective-permute-start.52 = (bf16[2,96,768]{2,1,0:T(8,128)(2,1)S(1)}, bf16[2,96,768]{2,1,0:T(8,128)(2,1)S(1)}, u32[]{:S(2)}, u32[]{:S(2)}) collective-permute-start(bf16[2,96,768]{2,1,0:T(8,128)(2,1)S(1)} %convert_element_type.511), channel_id=1, source_target_pairs={{0,16},{8,24},{16,0},{24,8},{1,17},{9,25},{17,1},{25,9},{2,18},{10... | collective-permute-start | bytes 884744 | tf_op jit(solution)/shard_map/ppermute | solution.py:71
  65.0 37.7 %collective-permute-start.53 = (bf16[2,96,768]{2,1,0:T(8,128)(2,1)S(1)}, bf16[2,96,768]{2,1,0:T(8,128)(2,1)S(1)}, u32[]{:S(2)}, u32[]{:S(2)}) collective-permute-start(bf16[2,96,768]{2,1,0:T(8,128)(2,1)S(1)} %convert_element_type.511), channel_id=1, source_target_pairs={{0,24},{8,0},{16,8},{24,16},{1,25},{9,1},{17,9},{25,17},{2,26},{10... | collective-permute-start | bytes 884744 | tf_op jit(solution)/shard_map/ppermute | solution.py:71
  114.0 36.1 %collective-permute-start.24 = (bf16[4,1,96,768]{3,2,1,0:T(8,128)(2,1)S(1)}, bf16[4,1,96,768]{3,2,1,0:T(8,128)(2,1)}, u32[]{:S(2)}, u32[]{:S(2)}) collective-permute-start(bf16[4,1,96,768]{3,2,1,0:T(8,128)(2,1)S(1)} %pad_maximum_fusion.2), channel_id=1, source_target_pairs={{0,0},{1,1},{2,4},{3,5},{4,2},{5,3},{6,6},{7,7},{8,8},{9,9},{10,12... | collective-permute-start | bytes 1769480 | tf_op jit(solution)/shard_map/ppermute | solution.py:62
  195.4 55.1 %collective-permute-start.15 = (bf16[768,768]{1,0:T(8,128)(2,1)}, bf16[768,768]{1,0:T(8,128)(2,1)}, u32[]{:S(2)}, u32[]{:S(2)}) collective-permute-start(bf16[768,768]{1,0:T(8,128)(2,1)} %convolution_convert_fusion.9), channel_id=1, source_target_pairs={{0,4},{4,0},{1,5},{5,1},{2,6},{6,2},{3,7},{7,3},{8,12},{12,8},{9,1... | collective-permute-start | bytes 3538952 | tf_op jit(solution)/shard_map/ppermute | solution.py:45
  195.4 40.9 %collective-permute-start.43 = (bf16[4,6,96,128]{3,2,1,0:T(8,128)(2,1)}, bf16[4,6,96,128]{3,2,1,0:T(8,128)(2,1)}, u32[]{:S(2)}, u32[]{:S(2)}) collective-permute-start(bf16[4,6,96,128]{3,2,1,0:T(8,128)(2,1)} %collective-permute-done.42), channel_id=1, source_target_pairs={{0,0},{1,1},{2,4},{3,5},{4,2},{5,3},{6,6},{7,7},{8,8},{9,9},{10,12... | collective-permute-start | bytes 1769480 | tf_op jit(solution)/shard_map/ppermute | solution.py:62
  201.4 35.0 %collective-permute-start.44 = (bf16[4,6,96,128]{3,2,1,0:T(8,128)(2,1)}, bf16[4,6,96,128]{3,2,1,0:T(8,128)(2,1)}, u32[]{:S(2)}, u32[]{:S(2)}) collective-permute-start(bf16[4,6,96,128]{3,2,1,0:T(8,128)(2,1)} %collective-permute-done.42), channel_id=1, source_target_pairs={{0,2},{1,3},{2,6},{3,7},{4,0},{5,1},{6,4},{7,5},{8,10},{9,11},{10,... | collective-permute-start | bytes 1769480 | tf_op jit(solution)/shard_map/ppermute | solution.py:62
  217.9 36.0 %collective-permute-start.35 = (bf16[384,768]{1,0:T(8,128)(2,1)}, bf16[384,768]{1,0:T(8,128)(2,1)}, u32[]{:S(2)}, u32[]{:S(2)}) collective-permute-start(bf16[384,768]{1,0:T(8,128)(2,1)} %dynamic-slice_bitcast_fusion), channel_id=1, source_target_pairs={{0,4},{4,0},{1,5},{5,1},{2,6},{6,2},{3,7},{7,3},{8,12},{12,8},{9,1... | collective-permute-start | bytes 1769480 | tf_op jit(solution)/shard_map/ppermute | solution.py:45
  350.5 65.3 %collective-permute-start.134 = (bf16[4,1,96,768]{3,2,1,0:T(8,128)(2,1)}, bf16[4,1,96,768]{3,2,1,0:T(8,128)(2,1)S(1)}, u32[]{:S(2)}, u32[]{:S(2)}) collective-permute-start(bf16[4,1,96,768]{3,2,1,0:T(8,128)(2,1)} %get-tuple-element.137), channel_id=1, source_target_pairs={{0,0},{1,1},{4,2},{5,3},{2,4},{3,5},{6,6},{7,7},{8,8},{9,9},{12,10... | collective-permute-start | bytes 1769480 | tf_op jit(solution)/shard_map/ppermute | solution.py:66
  353.9 48.7 %collective-permute-start.136 = (bf16[4,1,96,768]{3,2,1,0:T(8,128)(2,1)}, bf16[4,1,96,768]{3,2,1,0:T(8,128)(2,1)S(1)}, u32[]{:S(2)}, u32[]{:S(2)}) collective-permute-start(bf16[4,1,96,768]{3,2,1,0:T(8,128)(2,1)} %get-tuple-element.139), channel_id=1, source_target_pairs={{0,0},{1,1},{4,2},{5,3},{2,4},{3,5},{6,6},{7,7},{8,8},{9,9},{12,10... | collective-permute-start | bytes 1769480 | tf_op jit(solution)/shard_map/ppermute | solution.py:66
  356.5 46.1 %collective-permute-start.137 = (bf16[4,1,96,768]{3,2,1,0:T(8,128)(2,1)}, bf16[4,1,96,768]{3,2,1,0:T(8,128)(2,1)S(1)}, u32[]{:S(2)}, u32[]{:S(2)}) collective-permute-start(bf16[4,1,96,768]{3,2,1,0:T(8,128)(2,1)} %get-tuple-element.140), channel_id=1, source_target_pairs={{2,0},{3,1},{6,2},{7,3},{0,4},{1,5},{4,6},{5,7},{10,8},{11,9},{14,... | collective-permute-start | bytes 1769480 | tf_op jit(solution)/shard_map/ppermute | solution.py:66
  403.7 42.1 %collective-permute-start.138 = (bf16[4,1,96,768]{3,2,1,0:T(8,128)(2,1)}, bf16[4,1,96,768]{3,2,1,0:T(8,128)(2,1)}, u32[]{:S(2)}, u32[]{:S(2)}) collective-permute-start(bf16[4,1,96,768]{3,2,1,0:T(8,128)(2,1)} %add_convert_fusion.4), channel_id=1, source_target_pairs={{0,1},{1,0},{2,3},{3,2},{4,5},{5,4},{6,7},{7,6},{8,9},{9,8},{10,11... | collective-permute-start | bytes 1769480 | tf_op jit(solution)/shard_map/ppermute | solution.py:49
  408.9 38.2 %collective-permute-start.140 = (bf16[4,1,96,768]{3,2,1,0:T(8,128)(2,1)}, bf16[4,1,96,768]{3,2,1,0:T(8,128)(2,1)}, u32[]{:S(2)}, u32[]{:S(2)}) collective-permute-start(bf16[4,1,96,768]{3,2,1,0:T(8,128)(2,1)} %add_convert_fusion.3), channel_id=1, source_target_pairs={{0,0},{1,1},{4,2},{5,3},{2,4},{3,5},{6,6},{7,7},{8,8},{9,9},{12,10... | collective-permute-start | bytes 1769480 | tf_op jit(solution)/shard_map/ppermute | solution.py:66
  431.4 58.2 %collective-permute-start.122 = (bf16[4,6,96,128]{3,2,1,0:T(8,128)(2,1)}, bf16[4,6,96,128]{3,2,1,0:T(8,128)(2,1)}, u32[]{:S(2)}, u32[]{:S(2)}) collective-permute-start(bf16[4,6,96,128]{3,2,1,0:T(8,128)(2,1)} %get-tuple-element.129), channel_id=1, source_target_pairs={{0,0},{1,1},{4,2},{5,3},{2,4},{3,5},{6,6},{7,7},{8,8},{9,9},{12,10... | collective-permute-start | bytes 1769480 | tf_op jit(solution)/shard_map/ppermute | solution.py:66
  437.4 41.9 %collective-permute-start.124 = (bf16[4,6,96,128]{3,2,1,0:T(8,128)(2,1)}, bf16[4,6,96,128]{3,2,1,0:T(8,128)(2,1)}, u32[]{:S(2)}, u32[]{:S(2)}) collective-permute-start(bf16[4,6,96,128]{3,2,1,0:T(8,128)(2,1)} %get-tuple-element.131), channel_id=1, source_target_pairs={{0,0},{1,1},{4,2},{5,3},{2,4},{3,5},{6,6},{7,7},{8,8},{9,9},{12,10... | collective-permute-start | bytes 1769480 | tf_op jit(solution)/shard_map/ppermute | solution.py:66
  479.3 39.6 %collective-permute-start.66 = (bf16[768,768]{1,0:T(8,128)(2,1)S(1)}, bf16[768,768]{1,0:T(8,128)(2,1)S(1)}, u32[]{:S(2)}, u32[]{:S(2)}) collective-permute-start(bf16[768,768]{1,0:T(8,128)(2,1)S(1)} %copy-done.61), channel_id=1, source_target_pairs={{0,4},{4,0},{1,5},{5,1},{2,6},{6,2},{3,7},{7,3},{8,12},{12,8},{9,1... | collective-permute-start | bytes 3538952 | tf_op jit(solution)/shard_map/ppermute | solution.py:45
  508.4 38.6 %collective-permute-start.126 = (bf16[4,6,96,128]{3,2,1,0:T(8,128)(2,1)S(1)}, bf16[4,6,96,128]{3,2,1,0:T(8,128)(2,1)}, u32[]{:S(2)}, u32[]{:S(2)}) collective-permute-start(bf16[4,6,96,128]{3,2,1,0:T(8,128)(2,1)S(1)} %add_convert_fusion.7), channel_id=1, source_target_pairs={{0,1},{1,0},{2,3},{3,2},{4,5},{5,4},{6,7},{7,6},{8,9},{9,8},{10,11... | collective-permute-start | bytes 1769480 | tf_op jit(solution)/shard_map/ppermute | solution.py:49
  509.1 42.2 %collective-permute-start.128 = (bf16[4,6,96,128]{3,2,1,0:T(8,128)(2,1)}, bf16[4,6,96,128]{3,2,1,0:T(8,128)(2,1)}, u32[]{:S(2)}, u32[]{:S(2)}) collective-permute-start(bf16[4,6,96,128]{3,2,1,0:T(8,128)(2,1)} %add_convert_fusion.6), channel_id=1, source_target_pairs={{0,0},{1,1},{4,2},{5,3},{2,4},{3,5},{6,6},{7,7},{8,8},{9,9},{12,10... | collective-permute-start | bytes 1769480 | tf_op jit(solution)/shard_map/ppermute | solution.py:66
  515.8 38.3 %collective-permute-start.130 = (bf16[4,6,96,128]{3,2,1,0:T(8,128)(2,1)}, bf16[4,6,96,128]{3,2,1,0:T(8,128)(2,1)}, u32[]{:S(2)}, u32[]{:S(2)}) collective-permute-start(bf16[4,6,96,128]{3,2,1,0:T(8,128)(2,1)} %add_convert_fusion.5), channel_id=1, source_target_pairs={{2,0},{3,1},{6,2},{7,3},{0,4},{1,5},{4,6},{5,7},{10,8},{11,9},{14,... | collective-permute-start | bytes 1769480 | tf_op jit(solution)/shard_map/ppermute | solution.py:66
  542.8 39.0 %collective-permute-start.90 = (bf16[4,1,96,768]{3,2,1,0:T(8,128)(2,1)}, bf16[4,1,96,768]{3,2,1,0:T(8,128)(2,1)S(1)}, u32[]{:S(2)}, u32[]{:S(2)}) collective-permute-start(bf16[4,1,96,768]{3,2,1,0:T(8,128)(2,1)} %get-tuple-element.118), channel_id=1, source_target_pairs={{0,0},{1,1},{4,2},{5,3},{2,4},{3,5},{6,6},{7,7},{8,8},{9,9},{12,10... | collective-permute-start | bytes 1769480 | tf_op jit(solution)/shard_map/ppermute | solution.py:66
  581.8 61.4 %collective-permute-start.94 = (bf16[4,1,96,768]{3,2,1,0:T(8,128)(2,1)}, bf16[4,1,96,768]{3,2,1,0:T(8,128)(2,1)}, u32[]{:S(2)}, u32[]{:S(2)}) collective-permute-start(bf16[4,1,96,768]{3,2,1,0:T(8,128)(2,1)} %add_convert_fusion.10), channel_id=1, source_target_pairs={{0,1},{1,0},{2,3},{3,2},{4,5},{5,4},{6,7},{7,6},{8,9},{9,8},{10,11... | collective-permute-start | bytes 1769480 | tf_op jit(solution)/shard_map/ppermute | solution.py:49
  584.4 64.7 %collective-permute-start.96 = (bf16[4,1,96,768]{3,2,1,0:T(8,128)(2,1)}, bf16[4,1,96,768]{3,2,1,0:T(8,128)(2,1)}, u32[]{:S(2)}, u32[]{:S(2)}) collective-permute-start(bf16[4,1,96,768]{3,2,1,0:T(8,128)(2,1)} %add_convert_fusion.9), channel_id=1, source_target_pairs={{0,0},{1,1},{4,2},{5,3},{2,4},{3,5},{6,6},{7,7},{8,8},{9,9},{12,10... | collective-permute-start | bytes 1769480 | tf_op jit(solution)/shard_map/ppermute | solution.py:66
  596.0 58.2 %collective-permute-start.98 = (bf16[4,1,96,768]{3,2,1,0:T(8,128)(2,1)}, bf16[4,1,96,768]{3,2,1,0:T(8,128)(2,1)}, u32[]{:S(2)}, u32[]{:S(2)}) collective-permute-start(bf16[4,1,96,768]{3,2,1,0:T(8,128)(2,1)} %add_convert_fusion.8), channel_id=1, source_target_pairs={{2,0},{3,1},{6,2},{7,3},{0,4},{1,5},{4,6},{5,7},{10,8},{11,9},{14,... | collective-permute-start | bytes 1769480 | tf_op jit(solution)/shard_map/ppermute | solution.py:66
  660.1 54.2 %collective-permute-start.99 = (bf16[2,96,768]{2,1,0:T(8,128)(2,1)}, bf16[2,96,768]{2,1,0:T(8,128)(2,1)}, u32[]{:S(2)}, u32[]{:S(2)}) collective-permute-start(bf16[2,96,768]{2,1,0:T(8,128)(2,1)} %pad_maximum_fusion.14), channel_id=1, source_target_pairs={{0,24},{8,0},{16,8},{24,16},{1,25},{9,1},{17,9},{25,17},{2,26},{10... | collective-permute-start | bytes 884744 | tf_op jit(solution)/shard_map/ppermute | solution.py:71
  666.5 49.4 %collective-permute-start.100 = (bf16[2,96,768]{2,1,0:T(8,128)(2,1)}, bf16[2,96,768]{2,1,0:T(8,128)(2,1)}, u32[]{:S(2)}, u32[]{:S(2)}) collective-permute-start(bf16[2,96,768]{2,1,0:T(8,128)(2,1)} %pad_maximum_fusion.15), channel_id=1, source_target_pairs={{0,16},{8,24},{16,0},{24,8},{1,17},{9,25},{17,1},{25,9},{2,18},{10... | collective-permute-start | bytes 884744 | tf_op jit(solution)/shard_map/ppermute | solution.py:71
  680.7 37.7 %collective-permute-start.101 = (bf16[2,96,768]{2,1,0:T(8,128)(2,1)}, bf16[2,96,768]{2,1,0:T(8,128)(2,1)}, u32[]{:S(2)}, u32[]{:S(2)}) collective-permute-start(bf16[2,96,768]{2,1,0:T(8,128)(2,1)} %pad_maximum_fusion.16), channel_id=1, source_target_pairs={{0,8},{8,16},{16,24},{24,0},{1,9},{9,17},{17,25},{25,1},{2,10},{10... | collective-permute-start | bytes 884744 | tf_op jit(solution)/shard_map/ppermute | solution.py:71
  694.2 41.4 %collective-permute-start.75 = (bf16[4,3,96,128]{3,2,1,0:T(8,128)(2,1)}, bf16[4,3,96,128]{3,2,1,0:T(8,128)(2,1)}, u32[]{:S(2)}, u32[]{:S(2)}) collective-permute-start(bf16[4,3,96,128]{3,2,1,0:T(8,128)(2,1)} %get-tuple-element.110), channel_id=1, source_target_pairs={{0,0},{1,1},{4,2},{5,3},{2,4},{3,5},{6,6},{7,7},{8,8},{9,9},{12,10... | collective-permute-start | bytes 884744 | tf_op jit(solution)/shard_map/ppermute | solution.py:66
  697.9 39.0 %collective-permute-start.76 = (bf16[4,3,96,128]{3,2,1,0:T(8,128)(2,1)}, bf16[4,3,96,128]{3,2,1,0:T(8,128)(2,1)}, u32[]{:S(2)}, u32[]{:S(2)}) collective-permute-start(bf16[4,3,96,128]{3,2,1,0:T(8,128)(2,1)} %get-tuple-element.111), channel_id=1, source_target_pairs={{2,0},{3,1},{6,2},{7,3},{0,4},{1,5},{4,6},{5,7},{10,8},{11,9},{14,... | collective-permute-start | bytes 884744 | tf_op jit(solution)/shard_map/ppermute | solution.py:66
  726.3 35.0 %collective-permute-start.68 = (bf16[768,768]{1,0:T(8,128)(2,1)}, bf16[768,768]{1,0:T(8,128)(2,1)}, u32[]{:S(2)}, u32[]{:S(2)}) collective-permute-start(bf16[768,768]{1,0:T(8,128)(2,1)} %convolution_convert_fusion.7), channel_id=1, source_target_pairs={{0,4},{4,0},{1,5},{5,1},{2,6},{6,2},{3,7},{7,3},{8,12},{12,8},{9,1... | collective-permute-start | bytes 3538952 | tf_op jit(solution)/shard_map/ppermute | solution.py:45
  (286 other events, 4151.1 us)

commit v2 on v1

--- a/solution.py
+++ b/solution.py
@@ -49,68 +49,63 @@
     return lax.ppermute(v, "mp", [(m, m ^ bits) for m in range(4)])
 
 
-def spread_perm(flip):
-    return [
-        (s * 4 + y * 2 + x, y * 4 + (s ^ flip) * 2 + x)
+def spread_perm(dx, flip):
+    pairs = [
+        (s * 4 + y * 2 + x, y * 4 + (s ^ flip) * 2 + (x ^ dx))
         for s in range(2)
         for y in range(2)
         for x in range(2)
     ]
-
-
-def spread(v, flip):
-    return lax.ppermute(v, ("seq", "mp"), spread_perm(flip))
-
-
-def unspread(v, flip):
-    return lax.ppermute(v, ("seq", "mp"), [(d, s) for s, d in spread_perm(flip)])
-
-
-def shift_dp(v, k):
-    n = lax.axis_size("dp")
-    return lax.ppermute(v, "dp", [(i, (i + k) % n) for i in range(n)])
+    return [(a, b) for a, b in pairs if a != b]
+
+
+ROUTES = [(dx, flip) for dx in range(2) for flip in range(2)]
+
+
+def spread(v, dx, flip):
+    return lax.ppermute(v, ("seq", "mp"), spread_perm(dx, flip))
+
+
+def unspread(v, dx, flip):
+    return lax.ppermute(v, ("seq", "mp"), [(d, s) for s, d in spread_perm(dx, flip)])
 
 
 def sum_dp(v):
     n = lax.axis_size("dp")
-    if n > 4:
+    if n != 4:
         return lax.psum(v, "dp")
-    return v + sum(shift_dp(v, k) for k in range(1, n))
-
-
-def gather_chunk(shard):
-    n = lax.axis_size("dp")
-    half = shard.shape[0] // 2
-    if n > 4:
-        whole = lax.all_gather(shard, "dp", axis=0, tiled=False)
-        za, zb = whole[:, :half], whole[:, half:]
-    else:
-        blocks = [shard] + [shift_dp(shard, k) for k in range(1, n)]
-        za = jnp.stack([b[:half] for b in blocks])
-        zb = jnp.stack([b[half:] for b in blocks])
-    ax = swap_mp(za, 1)
-    first = [[spread(za, a) for a in range(2)], [spread(ax, a) for a in range(2)]]
-    own = [spread(zb, a) for a in range(2)]
-    second = [own, [swap_mp(b, 1) for b in own]]
-    return [first, second]
-
-
-def scatter_chunk(pieces):
-    n = lax.axis_size("dp")
-    first, second = pieces
-    t = [sum(wide(unspread(first[dx][a], a)) for a in range(2)) for dx in range(2)]
-    ta = wide(swap_mp(bf(t[1]), 1))
-    u = [bf(wide(second[0][a]) + wide(swap_mp(second[1][a], 1))) for a in range(2)]
-    tb = [wide(unspread(u[a], a)) for a in range(2)]
-    if n > 4:
-        whole = bf(jnp.concatenate([t[0] + ta, tb[0] + tb[1]], axis=1))
-        return wide(lax.psum_scatter(whole, "dp", scatter_dimension=0, tiled=False))
-    total = None
-    for k in range(n):
-        part = jnp.concatenate([t[0][k] + ta[k], tb[0][k] + tb[1][k]], axis=0)
-        part = part if k == 0 else wide(shift_dp(bf(part), n - k))
-        total = part if total is None else total + part
-    return total
+    for bits in (1, 2):
+        v = v + lax.ppermute(v, "dp", [(i, i ^ bits) for i in range(n)])
+    return v
+
+
+def stage(*values):
+    return lax.optimization_barrier(values)
+
+
+def after(values, *others):
+    return lax.optimization_barrier((values, others))[0]
+
+
+def gather_dp(shard):
+    return lax.all_gather(shard, "dp", axis=0, tiled=False)
+
+
+def scatter_dp(whole):
+    return lax.psum_scatter(whole, "dp", scatter_dimension=0, tiled=False)
+
+
+def gather_plane(v):
+    return [v] + [spread(v, dx, flip) for dx, flip in ROUTES]
+
+
+def scatter_plane(pieces):
+    return [unspread(p, dx, flip) for p, (dx, flip) in zip(pieces, ROUTES)]
+
+
+def sum_plane(pieces, back, own):
+    first = jnp.where(own, wide(pieces[0]), wide(back[0]))
+    return bf(first + sum(wide(b) for b in back[1:]))
 
 
 def pack_attn(shard):
@@ -118,13 +113,6 @@
     return jnp.concatenate([main, jnp.concatenate([rest[0::2], rest[1::2]], axis=-1)], axis=0)
 
 
-def unpack_attn(tiles, count):
-    main, rest = tiles[:count], tiles[count:]
-    left, right = rest[:, :, : PAIR // 2], rest[:, :, PAIR // 2 :]
-    rest = jnp.stack([left, right], axis=1).reshape(count, tiles.shape[1], PAIR // 2)
-    return jnp.concatenate([main, rest], axis=-1)
-
-
 def half_lanes(shape):
     return lax.broadcasted_iota(jnp.int32, shape, len(shape) - 1) < PAIR // 2
 
@@ -133,18 +121,18 @@
     return bf(pltpu.roll(wide(v), PAIR // 2, 1))
 
 
-def assemble_attn(pieces, plans, count, zidx, yidx):
-    flat = [pieces[h][dx][a] for h in range(2) for dx in range(2) for a in range(2)]
-    n, half, rows, _ = flat[0].shape
-
-    def kernel(zi, yi, *refs):
-        ins, outs = refs[:8], refs[8:]
+def assemble_attn(pieces, plans, count, yidx):
+    n, tiles, rows, _ = pieces[0].shape
+
+    def kernel(yi, *refs):
+        ins, outs = refs[:5], refs[5:]
         low = half_lanes((rows, PAIR))
         for a in range(2):
             side = yi[a]
 
             def tile(t, dx):
-                return ins[(t // half) * 4 + dx * 2 + a][0, t % half]
+                val = ins[1 + dx * 2 + a][0, t]
+                return jnp.where(yi[2] == 1, ins[0][0, t], val) if dx + a == 0 else val
 
             for out, plan in zip(outs, plans):
                 for place, (mat, j) in enumerate(plan):
@@ -161,26 +149,25 @@
     outs = pl.pallas_call(
         kernel,
         grid_spec=pltpu.PrefetchScalarGridSpec(
-            num_scalar_prefetch=2,
+            num_scalar_prefetch=1,
             grid=(n,),
-            in_specs=[pl.BlockSpec((1, half, rows, PAIR), lambda k, zi, yi: (k, 0, 0, 0))] * 8,
+            in_specs=[pl.BlockSpec((1, tiles, rows, PAIR), lambda k, yi: (k, 0, 0, 0))] * 5,
             out_specs=[
-                pl.BlockSpec((1, 2, rows, PAIR * len(p)), lambda k, zi, yi: (zi[k], 0, 0, 0))
+                pl.BlockSpec((1, 2, rows, PAIR * len(p)), lambda k, yi: (k, 0, 0, 0))
                 for p in plans
             ],
         ),
         out_shape=[jax.ShapeDtypeStruct((n, 2, rows, PAIR * len(p)), BF16) for p in plans],
         cost_estimate=pl.CostEstimate(
-            flops=0, transcendentals=0, bytes_accessed=2 * 8 * n * half * rows * PAIR * 2
+            flops=0, transcendentals=0, bytes_accessed=9 * n * tiles * rows * PAIR * 2
         ),
         name="assemble_attn",
-    )(zidx, yidx, *flat)
+    )(yidx, *pieces)
     return [o.reshape(n * 2 * rows, -1) for o in outs]
 
 
-def split_attn(mats, plans, count, zidx, yidx):
-    half = (count + count // 2) // 2
-    n = zidx.shape[0]
+def split_attn(mats, plans, count, n, yidx):
+    tiles = count + count // 2
     rows = mats[0].shape[0] // (2 * n)
     ins = [m.reshape(n, 2, rows, -1) for m in mats]
     where = {}
@@ -188,7 +175,7 @@
         for place, key in enumerate(plan):
             where[key] = (i, place)
 
-    def kernel(zi, yi, *refs):
+    def kernel(yi, *refs):
         srcs, outs = refs[: len(mats)], refs[len(mats) :]
         low = half_lanes((rows, PAIR))
         for a in range(2):
@@ -199,7 +186,7 @@
                 return srcs[i][0, side, :, place * PAIR : (place + 1) * PAIR]
 
             for dx in range(2):
-                for t in range(2 * half):
+                for t in range(tiles):
                     if t < count:
                         val = get(t, dx)
                     else:
@@ -209,89 +196,142 @@
                             val = jnp.where(low, t0, half_roll(t1))
                         else:
                             val = jnp.where(low, half_roll(t0), t1)
-                    outs[(t // half) * 4 + dx * 2 + a][0, t % half] = val
+                    outs[dx * 2 + a][0, t] = val
 
     outs = pl.pallas_call(
         kernel,
         grid_spec=pltpu.PrefetchScalarGridSpec(
-            num_scalar_prefetch=2,
+            num_scalar_prefetch=1,
             grid=(n,),
             in_specs=[
-                pl.BlockSpec((1, 2, rows, m.shape[-1]), lambda k, zi, yi: (zi[k], 0, 0, 0))
+                pl.BlockSpec((1, 2, rows, m.shape[-1]), lambda k, yi: (k, 0, 0, 0))
                 for m in ins
             ],
-            out_specs=[pl.BlockSpec((1, half, rows, PAIR), lambda k, zi, yi: (k, 0, 0, 0))] * 8,
-        ),
-        out_shape=[jax.ShapeDtypeStruct((n, half, rows, PAIR), BF16)] * 8,
+            out_specs=[pl.BlockSpec((1, tiles, rows, PAIR), lambda k, yi: (k, 0, 0, 0))] * 4,
+        ),
+        out_shape=[jax.ShapeDtypeStruct((n, tiles, rows, PAIR), BF16)] * 4,
         cost_estimate=pl.CostEstimate(
-            flops=0, transcendentals=0, bytes_accessed=2 * 8 * n * half * rows * PAIR * 2
+            flops=0, transcendentals=0, bytes_accessed=8 * n * tiles * rows * PAIR * 2
         ),
         name="split_attn",
-    )(zidx, yidx, *ins)
-    return [[[outs[h * 4 + dx * 2 + a] for a in range(2)] for dx in range(2)] for h in range(2)]
-
-
-def assemble_ffn(pieces, zidx, yidx):
-    flat = [pieces[h][dx][a] for h in range(2) for dx in range(2) for a in range(2)]
-    n, _, rows, cols = flat[0].shape
-
-    def kernel(zi, yi, *refs):
-        ins, outs = refs[:8], refs[8:]
+    )(yidx, *ins)
+    return outs
+
+
+def assemble_ffn(pieces, yidx):
+    n, _, rows, cols = pieces[0].shape
+
+    def kernel(yi, *refs):
+        ins, outs = refs[:5], refs[5:]
         for a in range(2):
             for h in range(2):
                 for dx in range(2):
-                    outs[h][0, yi[a], :, dx * cols : (dx + 1) * cols] = ins[h * 4 + dx * 2 + a][0, 0]
+                    val = ins[1 + dx * 2 + a][0, h]
+                    val = jnp.where(yi[2] == 1, ins[0][0, h], val) if dx + a == 0 else val
+                    outs[h][0, yi[a], :, dx * cols : (dx + 1) * cols] = val
 
     outs = pl.pallas_call(
         kernel,
         grid_spec=pltpu.PrefetchScalarGridSpec(
-            num_scalar_prefetch=2,
+            num_scalar_prefetch=1,
             grid=(n,),
-            in_specs=[pl.BlockSpec((1, 1, rows, cols), lambda k, zi, yi: (k, 0, 0, 0))] * 8,
+            in_specs=[pl.BlockSpec((1, 2, rows, cols), lambda k, yi: (k, 0, 0, 0))] * 5,
             out_specs=[
-                pl.BlockSpec((1, 2, rows, 2 * cols), lambda k, zi, yi: (zi[k], 0, 0, 0))
+                pl.BlockSpec((1, 2, rows, 2 * cols), lambda k, yi: (k, 0, 0, 0))
             ]
             * 2,
         ),
         out_shape=[jax.ShapeDtypeStruct((n, 2, rows, 2 * cols), BF16)] * 2,
         cost_estimate=pl.CostEstimate(
-            flops=0, transcendentals=0, bytes_accessed=2 * 8 * n * rows * cols * 2
+            flops=0, transcendentals=0, bytes_accessed=2 * 9 * n * rows * cols * 2
         ),
         name="assemble_ffn",
-    )(zidx, yidx, *flat)
+    )(yidx, *pieces)
     return [o.reshape(n * 2 * rows, 2 * cols) for o in outs]
 
 
-def split_ffn(mats, zidx, yidx):
-    n = zidx.shape[0]
+def split_ffn(mats, n, yidx):
     rows = mats[0].shape[0] // (2 * n)
     cols = mats[0].shape[1] // 2
     ins = [m.reshape(n, 2, rows, 2 * cols) for m in mats]
 
-    def kernel(zi, yi, *refs):
+    def kernel(yi, *refs):
         srcs, outs = refs[:2], refs[2:]
         for a in range(2):
             for h in range(2):
                 for dx in range(2):
-                    outs[h * 4 + dx * 2 + a][0, 0] = srcs[h][
-                        0, yi[a], :, dx * cols : (dx + 1) * cols
-                    ]
+                    outs[dx * 2 + a][0, h] = srcs[h][0, yi[a], :, dx * cols : (dx + 1) * cols]
+
+    return pl.pallas_call(
+        kernel,
+        grid_spec=pltpu.PrefetchScalarGridSpec(
+            num_scalar_prefetch=1,
+            grid=(n,),
+            in_specs=[pl.BlockSpec((1, 2, rows, 2 * cols), lambda k, yi: (k, 0, 0, 0))] * 2,
+            out_specs=[pl.BlockSpec((1, 2, rows, cols), lambda k, yi: (k, 0, 0, 0))] * 4,
+        ),
+        out_shape=[jax.ShapeDtypeStruct((n, 2, rows, cols), BF16)] * 4,
+        cost_estimate=pl.CostEstimate(
+            flops=0, transcendentals=0, bytes_accessed=2 * 8 * n * rows * cols * 2
+        ),
+        name="split_ffn",
+    )(yidx, *ins)
+
+
+def assemble_planes(planes, yidx):
+    n = planes.shape[0]
+    rows, cols = planes.shape[4:]
+
+    def kernel(yi, src, *outs):
+        for k in range(n):
+            for a in range(2):
+                for h in range(2):
+                    outs[h][k, yi[a]] = src[k, 0, a, h]
 
     outs = pl.pallas_call(
         kernel,
         grid_spec=pltpu.PrefetchScalarGridSpec(
-            num_scalar_prefetch=2,
-            grid=(n,),
-            in_specs=[pl.BlockSpec((1, 2, rows, 2 * cols), lambda k, zi, yi: (zi[k], 0, 0, 0))] * 2,
-            out_specs=[pl.BlockSpec((1, 1, rows, cols), lambda k, zi, yi: (k, 0, 0, 0))] * 8,
-        ),
-        out_shape=[jax.ShapeDtypeStruct((n, 1, rows, cols), BF16)] * 8,
+            num_scalar_prefetch=1,
+            grid=(2,),
+            in_specs=[pl.BlockSpec((n, 1, 2, 2, rows, cols), lambda d, yi: (0, d, 0, 0, 0, 0))],
+            out_specs=[pl.BlockSpec((n, 2, rows, cols), lambda d, yi: (0, 0, 0, d))] * 2,
+        ),
+        compiler_params=pltpu.CompilerParams(vmem_limit_bytes=32 << 20),
+        out_shape=[jax.ShapeDtypeStruct((n, 2, rows, 2 * cols), BF16)] * 2,
         cost_estimate=pl.CostEstimate(
             flops=0, transcendentals=0, bytes_accessed=2 * 8 * n * rows * cols * 2
         ),
-        name="split_ffn",
-    )(zidx, yidx, *ins)
-    return [[[outs[h * 4 + dx * 2 + a] for a in range(2)] for dx in range(2)] for h in range(2)]
+        name="assemble_planes",
+    )(yidx, planes)
+    return [o.reshape(n * 2 * rows, 2 * cols) for o in outs]
+
+
+def split_planes(mats, n, yidx):
+    rows = mats[0].shape[0] // (2 * n)
+    cols = mats[0].shape[1] // 2
+    ins = [m.reshape(n, 2, rows, 2 * cols) for m in mats]
+
+    def kernel(yi, *refs):
+        for k in range(n):
+            for a in range(2):
+                for h in range(2):
+                    refs[2][k, 0, a, h] = refs[h][k, yi[a]]
+
+    return pl.pallas_call(
+        kernel,
+        grid_spec=pltpu.PrefetchScalarGridSpec(
+            num_scalar_prefetch=1,
+            grid=(2,),
+            in_specs=[pl.BlockSpec((n, 2, rows, cols), lambda d, yi: (0, 0, 0, d))] * 2,
+            out_specs=pl.BlockSpec((n, 1, 2, 2, rows, cols), lambda d, yi: (0, d, 0, 0, 0, 0)),
+        ),
+        compiler_params=pltpu.CompilerParams(vmem_limit_bytes=32 << 20),
+        out_shape=jax.ShapeDtypeStruct((n, 2, 2, 2, rows, cols), BF16),
+        cost_estimate=pl.CostEstimate(
+            flops=0, transcendentals=0, bytes_accessed=2 * 8 * n * rows * cols * 2
+        ),
+        name="split_planes",
+    )(yidx, *ins)
 
 
 def bias_tiles(line, blocks):
@@ -592,6 +632,105 @@
     return inv * inner, jnp.sum(upstream * normed, axis=0), jnp.sum(upstream, axis=0)
 
 
+def update_matrices(sums, alternative, own, state, rate, inverse, packed):
+    master = state[0]
+    count, rows, cols = master.shape
+    step = 2 if packed else 1
+    arrays = list(sums) + ([alternative] if alternative is not None else [])
+
+    def kernel(own_ref, inv_ref, *refs):
+        if packed:
+            groups = [refs[2 * i : 2 * i + 2] for i in range(len(arrays))]
+            refs = refs[2 * len(arrays) :]
+        else:
+            groups = [refs[i : i + 1] for i in range(len(arrays))]
+            refs = refs[len(arrays) :]
+        state_refs, outs = refs[:3], refs[3:]
+        inv = inv_ref[0]
+
+        def total(part, i):
+            vals = [wide(g[part][i]) for g in groups]
+            if alternative is not None:
+                vals = [jnp.where(own_ref[0] == 1, vals[-1], vals[0])] + vals[1:-1]
+            return functools.reduce(jnp.add, vals)
+
+        def advance(grad, i, span):
+            mean_grad = grad * inv
+            new_moment = MOMENTUM * state_refs[1][i, :, span] + mean_grad
+            new_master = state_refs[0][i, :, span] - rate * (mean_grad + MOMENTUM * new_moment)
+            outs[0][i, :, span] = mean_grad
+            outs[1][i, :, span] = new_master
+            outs[2][i, :, span] = new_moment
+            outs[3][i, :, span] = (
+                AVERAGING * state_refs[2][i, :, span] + (1.0 - AVERAGING) * new_master
+            )
+            outs[4][i, :, span] = bf(new_master)
+
+        if packed:
+            rest = total(1, 0)
+            turned = pltpu.roll(rest, PAIR // 2, 1)
+            for i in range(2):
+                advance(total(0, i), i, slice(0, PAIR))
+                advance((turned if i else rest)[:, : PAIR // 2], i, slice(PAIR, cols))
+        else:
+            advance(total(0, 0), 0, slice(0, cols))
+
+    in_specs, args = [], []
+    for a in arrays:
+        in_specs.append(pl.BlockSpec((step, rows, a.shape[2]), lambda k, o: (k, 0, 0)))
+        args.append(a)
+        if packed:
+            in_specs.append(pl.BlockSpec((1, rows, PAIR), lambda k, o: (count + k, 0, 0)))
+            args.append(a)
+    spec = pl.BlockSpec((step, rows, cols), lambda k, o: (k, 0, 0))
+    return pl.pallas_call(
+        kernel,
+        grid_spec=pltpu.PrefetchScalarGridSpec(
+            num_scalar_prefetch=1,
+            grid=(count // step,),
+            in_specs=[pl.BlockSpec(memory_space=pltpu.SMEM)] + in_specs + [spec] * 3,
+            out_specs=[spec] * 5,
+        ),
+        out_shape=[jax.ShapeDtypeStruct(master.shape, F32)] * 4
+        + [jax.ShapeDtypeStruct(master.shape, BF16)],
+        cost_estimate=pl.CostEstimate(
+            flops=12 * master.size, transcendentals=0, bytes_accessed=44 * master.size
+        ),
+        name="update_matrices",
+    )(own, inverse, *args, *state)
+
+
+def place_quarters(parts, index, cuts):
+    rows, cols = parts[0].shape
+    count = len(parts)
+
+    def kernel(idx, *refs):
+        outs = refs[count:]
+        for k in range(count):
+
+            @pl.when(pl.program_id(0) == k)
+            def _():
+                start = 0
+                for out, cut in zip(outs, cuts):
+                    out[0] = refs[k][start : start + cut]
+                    start += cut
+
+    return pl.pallas_call(
+        kernel,
+        grid_spec=pltpu.PrefetchScalarGridSpec(
+            num_scalar_prefetch=1,
+            grid=(count,),
+            in_specs=[pl.BlockSpec((rows, cols), lambda g, idx: (0, 0))] * count,
+            out_specs=[pl.BlockSpec((1, c, cols), lambda g, idx: (idx[g], 0, 0)) for c in cuts],
+        ),
+        out_shape=[jax.ShapeDtypeStruct((count, c, cols), parts[0].dtype) for c in cuts],
+        cost_estimate=pl.CostEstimate(
+            flops=0, transcendentals=0, bytes_accessed=4 * count * rows * cols
+        ),
+        name="place_quarters",
+    )(index, *parts)
+
+
 def update(master, moment, average, gradient, rate, frame_total):
     mean_grad = gradient / frame_total
     new_moment = MOMENTUM * moment + mean_grad
@@ -600,8 +739,7 @@
     return mean_grad, new_master, new_moment, new_average
 
 
-def both_cores(part):
-    low = bf(part)
+def both_cores(low):
     return wide(low) + wide(swap_core(low))
 
 
@@ -619,6 +757,11 @@
     )
 
 
+CROSS_PLANS = [
+    [(0, j) for j in range(3)],
+    [(m, j) for j in range(3) for m in (1, 2)],
+    [(3, j) for j in range(3)],
+]
 QKV_PLAN = [(m, j) for j in range(3) for m in range(3)]
 ENC_PLANS = [QKV_PLAN, [(3, j) for j in range(3)]]
 DEC_PLANS = [
@@ -671,26 +814,29 @@
     utt_count, half_len, width = frames.shape
     text_half = dec_frames.shape[1]
     full_len, text_full = 2 * half_len, 2 * text_half
-    order = jnp.arange(n_dp, dtype=jnp.int32)
-    zidx = order if n_dp > 4 else (z - order) % n_dp
-    yidx = jnp.stack([y, 1 - y]).astype(jnp.int32)
+    own = s == y
+    yidx = jnp.stack([y, 1 - y, own.astype(jnp.int32)]).astype(jnp.int32)
     root_frames = float(utt_count * full_len * n_dp) ** 0.5
 
-    attn_pieces = gather_chunk(pack_attn(bf(attn_master)))
-    ffn_pieces = gather_chunk(bf(ffn_master))
-    dec_attn_pieces = gather_chunk(pack_attn(bf(dec_attn_master)))
-    dec_ffn_pieces = gather_chunk(bf(dec_ffn_master))
-    w_qkv, w_o = assemble_attn(attn_pieces, ENC_PLANS, 4, zidx, yidx)
-    w_one, w_two = assemble_ffn(ffn_pieces, zidx, yidx)
-    d_qkv, d_o, c_q, c_kv, c_o = assemble_attn(dec_attn_pieces, DEC_PLANS, 8, zidx, yidx)
-    dw_one, dw_two = assemble_ffn(dec_ffn_pieces, zidx, yidx)
+    mine = jnp.concatenate(
+        [
+            lax.dynamic_index_in_dim(parts, m, 0, keepdims=False)
+            for parts in (frames, cotangent, dec_frames, dec_cotangent)
+        ]
+    )
+    other = swap_core(mine)
+    dffn_shard = bf(dec_ffn_master)
+    dffn_parts = gather_plane(dffn_shard)
+    attn_z = gather_dp(pack_attn(bf(attn_master)))
+    packed = jnp.concatenate([col_bias, dec_col_bias, rel_table.T.reshape(-1)])
+    groups = [jnp.where(own, packed, spread(packed, 0, 0)), spread(packed, 1, 0)]
+    ffn_z = gather_dp(after(bf(ffn_master), attn_z))
+    mine, other, dffn_parts, attn_z, groups = stage(mine, other, dffn_parts, attn_z, groups)
+    attn_pieces = gather_plane(attn_z)
 
     bucket_count, group_heads = rel_table.shape
     group_width = attn_master.shape[2]
     unit_count = ffn_master.shape[2]
-    packed = jnp.concatenate([col_bias, dec_col_bias, rel_table.T.reshape(-1)])
-    groups = [spread(packed, 0), None]
-    groups[1] = swap_mp(groups[0], 1)
     enc_cols, dec_cols = col_bias.shape[0], dec_col_bias.shape[0]
 
     def cols_at(start):
@@ -722,59 +868,76 @@
     )
     max_dist = bucket_count // 2
     blocks = full_len // BLOCK
-    before = blocks * BLOCK - max_dist + 1
-    after = blocks * BLOCK - max_dist - 1
-    line = jnp.pad(heads[:, ::-1], ((0, 0), (before, after)), mode="edge")
+    lead = blocks * BLOCK - max_dist + 1
+    tail = blocks * BLOCK - max_dist - 1
+    line = jnp.pad(heads[:, ::-1], ((0, 0), (lead, tail)), mode="edge")
     bias = bias_tiles(line[:, None, :], blocks)
 
-    def all_rows(parts):
-        mine = lax.dynamic_index_in_dim(parts, m, 0, keepdims=False)
-        other = swap_core(mine)
-        first = jnp.where(s == 0, mine, other)
-        last = jnp.where(s == 0, other, mine)
-        return jnp.concatenate([first, last], axis=0)
-
-    inputs = all_rows(frames)
-    text_in = all_rows(dec_frames)
-    upstream_in = all_rows(cotangent)
-    text_upstream = all_rows(dec_cotangent)
+    def all_rows(start, count):
+        ours, theirs = mine[start : start + count], other[start : start + count]
+        return jnp.concatenate([jnp.where(s == 0, ours, theirs), jnp.where(s == 0, theirs, ours)])
+
+    inputs = all_rows(0, half_len)
+    upstream_in = all_rows(half_len, half_len)
+    text_in = all_rows(2 * half_len, text_half)
+    text_upstream = all_rows(2 * half_len + text_half, text_half)
     limit = lax.dynamic_slice_in_dim(lengths, m, 1)
     text_limit = lax.dynamic_slice_in_dim(text_lengths, m, 1)
-    frame_total = sum_dp(jnp.broadcast_to(wide(jnp.sum(lengths)), (8, 128)))[0, 0]
-
-    def to_owners(rows):
+    own_flag = own.astype(jnp.int32).reshape(1)
+
+    def my_half(rows):
         count = rows.shape[0] // 2
-        mine = lax.dynamic_slice_in_dim(rows, s * count, count, 0)
-        cut = count // 2
-        a, b = mine[:cut], mine[cut:]
-        ax, by = swap_mp(a, 1), swap_mp(b, 2)
-        ay, axy = swap_mp(a, 2), swap_mp(ax, 2)
-        bx, byx = swap_mp(b, 1), swap_mp(by, 1)
-        out = jnp.zeros((utt_count, count, width), rows.dtype)
-        for bits, top, low in ((0, a, b), (1, ax, bx), (2, ay, by), (3, axy, byx)):
-            out = lax.dynamic_update_slice(out, top[None], (m ^ bits, 0, 0))
-            out = lax.dynamic_update_slice(out, low[None], (m ^ bits, cut, 0))
-        return out
-
+        return lax.dynamic_slice_in_dim(rows, s * count, count, 0)
+
+    def to_owners(mine):
+        return [mine] + [swap_mp(mine, bits) for bits in range(1, 4)]
+
+    owners = m ^ jnp.arange(4, dtype=jnp.int32)
+
+    attn_pieces, ffn_z, bias, bias_qkv, inputs, dattn_shard, dffn_plane = stage(
+        attn_pieces,
+        ffn_z,
+        bias,
+        bias_qkv,
+        inputs,
+        pack_attn(bf(dec_attn_master)),
+        jnp.stack([jnp.where(own, dffn_parts[0], dffn_parts[1]), *dffn_parts[2:]]),
+    )
+    ffn_pieces = gather_plane(ffn_z)
+    dattn_z = gather_dp(dattn_shard)
+    dffn_planes = gather_dp(after(dffn_plane, dattn_z).reshape((2, 2) + dffn_shard.shape))
+    w_qkv, w_o = assemble_attn(attn_pieces, ENC_PLANS, 4, yidx)
     qkv = bf(dot_nn(inputs, w_qkv) + bias_qkv)
     context, lse = attention_forward(qkv, None, limit, bias, False, True)
-    attn_sum = both_cores(dot_nt(context, w_o))
+    part = bf(dot_nt(context, w_o))
+    ffn_pieces, dattn_z, part = stage(ffn_pieces, dattn_z, part)
+    dattn_pieces = gather_plane(dattn_z)
+    attn_sum = both_cores(part)
     hidden_one, normed_one, inv_one = norm_forward(
         wide(inputs) + attn_sum + norm_vecs[4], norm_vecs[0], norm_vecs[1]
     )
     hidden_low = bf(hidden_one)
+    w_one, w_two = assemble_ffn(ffn_pieces, yidx)
     gate_in = dot_nn(hidden_low, w_one) + bias_one
     activated = bf(gelu(gate_in))
-    ffn_sum = both_cores(dot_nt(activated, w_two))
+    part = bf(dot_nt(activated, w_two))
+    dattn_pieces, part, lengths_sum = stage(
+        dattn_pieces, part, jnp.broadcast_to(wide(jnp.sum(lengths)), (8, 128))
+    )
+    ffn_sum = both_cores(part)
     result, normed_two, inv_two = norm_forward(
         hidden_one + ffn_sum + norm_vecs[5], norm_vecs[2], norm_vecs[3]
     )
     enc_low = bf(result)
-    out_enc = to_owners(enc_low)
-
+    out_enc = lax.all_gather(after(my_half(enc_low), dffn_planes), "mp", axis=0, tiled=False)
+
+    frame_total = sum_dp(lengths_sum)[0, 0]
+    inverse = (1.0 / frame_total).reshape(1)
+    d_qkv, d_o, c_q, c_kv, c_o = assemble_attn(dattn_pieces, DEC_PLANS, 8, yidx)
+    dw_one, dw_two = assemble_planes(dffn_planes, yidx)
     dqkv = bf(dot_nn(text_in, d_qkv) + bias_dqkv)
     self_context, self_lse = attention_forward(dqkv, None, text_limit, None, True, True)
-    self_sum = both_cores(dot_nt(self_context, d_o))
+    self_sum = both_cores(bf(dot_nt(self_context, d_o)))
     dec_one, normed_d1, inv_d1 = norm_forward(
         wide(text_in) + self_sum + dec_norm_vecs[6], dec_norm_vecs[0], dec_norm_vecs[1]
     )
@@ -782,30 +945,34 @@
     cross_q = bf(dot_nn(dec_one_low, c_q) + bias_cq)
     cross_kv = bf(dot_nn(enc_low, c_kv) + bias_ckv)
     cross_context, cross_lse = attention_forward(cross_q, cross_kv, limit, None, False, False)
-    cross_sum = both_cores(dot_nt(cross_context, c_o))
+    cross_sum = both_cores(bf(dot_nt(cross_context, c_o)))
     dec_two, normed_d2, inv_d2 = norm_forward(
         dec_one + cross_sum + dec_norm_vecs[7], dec_norm_vecs[2], dec_norm_vecs[3]
     )
     dec_two_low = bf(dec_two)
     dec_gate = dot_nn(dec_two_low, dw_one) + bias_done
     dec_act = bf(gelu(dec_gate))
-    dec_ffn_sum = both_cores(dot_nt(dec_act, dw_two))
+    dec_ffn_sum = both_cores(bf(dot_nt(dec_act, dw_two)))
     dec_result, normed_d3, inv_d3 = norm_forward(
         dec_two + dec_ffn_sum + dec_norm_vecs[8], dec_norm_vecs[4], dec_norm_vecs[5]
     )
-    out_dec = to_owners(bf(dec_result))
 
     text_places = lax.broadcasted_iota(jnp.int32, (text_full, 1), 0)
     dec_up = jnp.where(text_places < text_limit[0], wide(text_upstream), 0.0)
     grad_d3, gain_d3, shift_d3 = norm_backward(dec_up, normed_d3, inv_d3, dec_norm_vecs[4])
     dec_ffn_back = bf(grad_d3)
     dec_gate_grad = bf(dot_nn(dec_ffn_back, dw_two) * gelu_slope(dec_gate))
-    grad_h2 = grad_d3 + both_cores(dot_nt(dec_gate_grad, dw_one))
+    part = bf(dot_nt(dec_gate_grad, dw_one))
     dec_ffn_grads = [
         bf(dot_tn(dec_two_low, dec_gate_grad)),
         bf(dot_tn(dec_ffn_back, dec_act)),
     ]
-    dec_ffn_total = scatter_chunk(split_ffn(dec_ffn_grads, zidx, yidx))
+    dec_ffn_planes, part, sent, inverse = stage(
+        split_planes(dec_ffn_grads, n_dp, yidx), part, my_half(bf(dec_result)), inverse
+    )
+    dec_ffn_plane = scatter_dp(dec_ffn_planes)
+    out_dec = to_owners(sent)
+    grad_h2 = grad_d3 + both_cores(part)
 
     grad_d2, gain_d2, shift_d2 = norm_backward(grad_h2, normed_d2, inv_d2, dec_norm_vecs[2])
     cross_back = bf(grad_d2)
@@ -820,8 +987,21 @@
         cross_lse,
         bf(dot_nn(cross_back, c_o)),
     )
-    memory_back = both_cores(dot_nt(cross_kvg, c_kv))
-    grad_h1 = grad_d2 + both_cores(dot_nt(cross_qg, c_q))
+    cross_grads = [
+        bf(dot_tn(dec_one_low, cross_qg)),
+        bf(dot_tn(enc_low, cross_kvg)),
+        bf(dot_tn(cross_back, cross_context)),
+    ]
+    query_part, memory_part, cross_parts, out_dec = stage(
+        bf(dot_nt(cross_qg, c_q)),
+        bf(dot_nt(cross_kvg, c_kv)),
+        split_attn(cross_grads, CROSS_PLANS, 4, n_dp, yidx),
+        out_dec,
+    )
+    (out_dec,) = place_quarters(out_dec, owners, [text_half])
+    cross_plane_back = scatter_plane(cross_parts)
+    memory_back = both_cores(memory_part)
+    grad_h1 = grad_d2 + both_cores(query_part)
     grad_d1, gain_d1, shift_d1 = norm_backward(grad_h1, normed_d1, inv_d1, dec_norm_vecs[0])
     self_back = bf(grad_d1)
     (self_g,) = attention_backward(
@@ -835,39 +1015,49 @@
         self_lse,
         bf(dot_nn(self_back, d_o)),
     )
-    text_grad = grad_d1 + both_cores(dot_nt(self_g, d_qkv))
-    dec_attn_grads = [
-        bf(dot_tn(text_in, self_g)),
-        bf(dot_tn(self_back, self_context)),
-        bf(dot_tn(dec_one_low, cross_qg)),
-        bf(dot_tn(enc_low, cross_kvg)),
-        bf(dot_tn(cross_back, cross_context)),
-    ]
-    dec_attn_total = unpack_attn(
-        scatter_chunk(split_attn(dec_attn_grads, DEC_PLANS, 8, zidx, yidx)), 8
-    )
-    out_text_grad = to_owners(bf(text_grad))
+    text_part = bf(dot_nt(self_g, d_qkv))
+    self_grads = [bf(dot_tn(text_in, self_g)), bf(dot_tn(self_back, self_context))]
+    self_parts = split_attn(self_grads, ENC_PLANS, 4, n_dp, yidx)
 
     places = lax.broadcasted_iota(jnp.int32, (full_len, 1), 0)
     upstream = jnp.where(places < limit[0], wide(upstream_in), 0.0) + memory_back
     grad_two, gain_two, shift_two = norm_backward(upstream, normed_two, inv_two, norm_vecs[2])
     ffn_back = bf(grad_two)
     gate_grad = bf(dot_nn(ffn_back, w_two) * gelu_slope(gate_in))
-    hidden_grad = grad_two + both_cores(dot_nt(gate_grad, w_one))
     ffn_grads = [bf(dot_tn(hidden_low, gate_grad)), bf(dot_tn(ffn_back, activated))]
-    ffn_total = scatter_chunk(split_ffn(ffn_grads, zidx, yidx))
+    part, text_part, self_parts, cross_parts, cross_plane_back, ffn_parts = stage(
+        bf(dot_nt(gate_grad, w_one)),
+        text_part,
+        self_parts,
+        cross_parts,
+        cross_plane_back,
+        split_ffn(ffn_grads, n_dp, yidx),
+    )
+    cross_total = scatter_dp(sum_plane(cross_parts, cross_plane_back, own))
+    ffn_plane_back = scatter_plane(ffn_parts)
+    hidden_grad = grad_two + both_cores(part)
     grad_one, gain_one, shift_one = norm_backward(hidden_grad, normed_one, inv_one, norm_vecs[0])
     attn_back = bf(grad_one)
     enc_g, diag = attention_backward(
         qkv, None, limit, bias, False, True, context, lse, bf(dot_nn(attn_back, w_o))
     )
-    input_grad = grad_one + both_cores(dot_nt(enc_g, w_qkv))
+    self_parts, ffn_parts, ffn_plane_back, part, enc_g, diag, text_part, dec_ffn_plane = stage(
+        self_parts,
+        ffn_parts,
+        ffn_plane_back,
+        bf(dot_nt(enc_g, w_qkv)),
+        enc_g,
+        diag,
+        text_part,
+        dec_ffn_plane,
+    )
+    ffn_total = scatter_dp(sum_plane(ffn_parts, ffn_plane_back, own))
+    self_plane_back = scatter_plane(self_parts)
+    plane_parts = [dec_ffn_plane[dx, a] for dx, a in ROUTES]
+    dec_ffn_sums = scatter_plane(plane_parts)
+    input_grad = grad_one + both_cores(part)
     attn_grads = [bf(dot_tn(inputs, enc_g)), bf(dot_tn(attn_back, context))]
-    attn_total = unpack_attn(
-        scatter_chunk(split_attn(attn_grads, ENC_PLANS, 4, zidx, yidx)), 4
-    )
-    out_input_grad = to_owners(bf(input_grad))
-
+    attn_parts = split_attn(attn_grads, ENC_PLANS, 4, n_dp, yidx)
     def col_sum(a):
         return jnp.sum(a, axis=0, dtype=F32)
 
@@ -896,9 +1086,9 @@
         )
         for d in range(span_count)
     )
-    first_bucket = jnp.sum(line_grad[:, before + bucket_count :], axis=1, keepdims=True)
-    last_bucket = jnp.sum(line_grad[:, :before], axis=1, keepdims=True)
-    head_grad = line_grad[:, before : before + bucket_count][:, ::-1]
+    first_bucket = jnp.sum(line_grad[:, lead + bucket_count :], axis=1, keepdims=True)
+    last_bucket = jnp.sum(line_grad[:, :lead], axis=1, keepdims=True)
+    head_grad = line_grad[:, lead : lead + bucket_count][:, ::-1]
     head_grad = jnp.concatenate(
         [
             head_grad[:, :1] + first_bucket,
@@ -929,8 +1119,25 @@
         jnp.concatenate([p[dx] for p in col_parts] + [table_parts[dx].reshape(-1), shared])
         for dx in range(2)
     ]
-    small = unspread(vectors[0] + swap_mp(vectors[1], 1), 0)
-    small = sum_dp(small + swap_core(small))
+    self_parts, self_plane_back, attn_parts, input_grad, vectors, text_part, dec_ffn_sums = stage(
+        self_parts, self_plane_back, attn_parts, input_grad, vectors, text_part, dec_ffn_sums
+    )
+    self_total = scatter_dp(sum_plane(self_parts, self_plane_back, own))
+    attn_plane_back = scatter_plane(attn_parts)
+    text_grad = grad_d1 + both_cores(text_part)
+    small = vectors[0] + swap_mp(vectors[1], 1)
+    small = jnp.where(own, small, unspread(small, 0, 0))
+    small = small + swap_core(small)
+    attn_parts, attn_plane_back, small, input_grad, text_grad = stage(
+        attn_parts, attn_plane_back, small, input_grad, text_grad
+    )
+    attn_total = scatter_dp(sum_plane(attn_parts, attn_plane_back, own))
+    held_back = to_owners(jnp.concatenate([my_half(bf(input_grad)), my_half(bf(text_grad))]))
+    out_input_grad, out_text_grad = place_quarters(held_back, owners, [half_len, text_half])
+    dec_attn_total = jnp.concatenate(
+        [self_total[:4], cross_total[:4], self_total[4:], cross_total[4:]]
+    )
+    small = sum_dp(small)
     cut = [enc_cols, dec_cols, group_heads * bucket_count, norm_vecs.size, dec_norm_vecs.size]
     ends = [sum(cut[: i + 1]) for i in range(len(cut))]
     col_total, dec_col_total, table_total, norm_total, dec_norm_total, _ = jnp.split(small, ends)
@@ -940,17 +1147,45 @@
 
     matrix_rate = MATRIX_RATE * root_frames
     vector_rate = VECTOR_RATE * root_frames
-    attn_new = update(attn_master, attn_moment, attn_average, attn_total, matrix_rate, frame_total)
-    ffn_new = update(ffn_master, ffn_moment, ffn_average, ffn_total, matrix_rate, frame_total)
+    attn_new = update_matrices(
+        [attn_total],
+        None,
+        own_flag,
+        (attn_master, attn_moment, attn_average),
+        matrix_rate,
+        inverse,
+        True,
+    )
+    ffn_new = update_matrices(
+        [ffn_total],
+        None,
+        own_flag,
+        (ffn_master, ffn_moment, ffn_average),
+        matrix_rate,
+        inverse,
+        False,
+    )
+    dattn_new = update_matrices(
+        [dec_attn_total],
+        None,
+        own_flag,
+        (dec_attn_master, dec_attn_moment, dec_attn_average),
+        matrix_rate,
+        inverse,
+        True,
+    )
+    dffn_new = update_matrices(
+        dec_ffn_sums,
+        plane_parts[0],
+        own_flag,
+        (dec_ffn_master, dec_ffn_moment, dec_ffn_average),
+        matrix_rate,
+        inverse,
+        False,
+    )
     norm_new = update(norm_vecs, norm_moment, norm_average, norm_total, vector_rate, frame_total)
     col_new = update(col_bias, col_moment, col_average, col_total, vector_rate, frame_total)
     rel_new = update(rel_table, rel_moment, rel_average, table_total, vector_rate, frame_total)
-    dattn_new = update(
-        dec_attn_master, dec_attn_moment, dec_attn_average, dec_attn_total, matrix_rate, frame_total
-    )
-    dffn_new = update(
-        dec_ffn_master, dec_ffn_moment, dec_ffn_average, dec_ffn_total, matrix_rate, frame_total
-    )
     dnorm_new = update(
         dec_norm_vecs, dec_norm_moment, dec_norm_average, dec_norm_total, vector_rate, frame_total
     )
@@ -963,9 +1198,7 @@
         attn_new[0],
         ffn_new[0],
         *attn_new[1:],
-        bf(attn_new[1]),
         *ffn_new[1:],
-        bf(ffn_new[1]),
         *norm_new[1:],
         *col_new[1:],
         *rel_new[1:],
@@ -974,9 +1207,7 @@
         dattn_new[0],
         dffn_new[0],
         *dattn_new[1:],
-        bf(dattn_new[1]),
         *dffn_new[1:],
-        bf(dffn_new[1]),
         *dnorm_new[1:],
         *dcol_new[1:],
     )

time: 803 us -> 601 us (0.75)
  starting transfers between devices: 233 us -> 72.8 us
  waiting for transfers between devices: 221 us -> 161 us
  other arithmetic: 107 us -> 72.2 us
  blocking collectives: 0 us -> 16.1 us
  Pallas kernels: 104 us -> 120 us
  between operations: 4.91 us -> 18.2 us
    ppermute x80 -> x43, starting transfers between devices: 170 us -> 57.5 us  [the longest x18 28.9 us: spread(): return lax.ppermute(v, ('seq', 'mp'), spread_perm(dx, flip))]
    ppermute x50 -> x7, waiting for transfers between devices: 126 us -> 14 us  [swap_mp(): return lax.ppermute(v, 'mp', [(m, m ^ bits) for m in range(4)])]
    ppermute x50 -> x7, starting transfers between devices: 51.2 us -> 8.95 us  [swap_mp(): return lax.ppermute(v, 'mp', [(m, m ^ bits) for m in range(4)])]
    ppermute x80 -> x43, waiting for transfers between devices: 94.6 us -> 135 us  [the longest x21 66.2 us: unspread(): lax.ppermute(v, ('seq', 'mp'), [(d, s) for s, d in spread_perm(dx, flip)])]
    pallas_call x0 -> x8, Pallas kernels: none -> 24.3 us  [the longest x4 12.7 us: update_matrices(): pl.pallas_call(kernel, grid_spec=pltpu.PrefetchScalarGridSpec(num_scalar_...]
    all_gather x0 -> x1, blocking collectives: none -> 16.1 us  [gather_dp(): return lax.all_gather(shard, 'dp', axis=0, tiled=False)]
    unnamed x353 -> x334, local copies, waits for them, and re-layouts: 17.3 us -> 28.7 us
    convert_element_type x12 -> x0, other arithmetic: 10.9 us -> none  [wide(): return a.astype(F32)]
  transfers between devices with their start and end apart: 146 -> 72, of which waited for: 39 -> 24; matrix products, arithmetic and copies ran while one was open for 24% -> 27% of each run, Pallas kernels for 13% -> 19%
where the time goes in v2:
time: 601 us; the launch traced here: 592 us
  waiting for transfers between devices  161 us (27%)
  Pallas kernels  120 us (20%)
  starting transfers between devices  72.8 us (12%)
  other arithmetic  72.2 us (12%)
  matrix products  69.4 us (12%)
  local copies, waits for them, and re-layouts  61.8 us (10%)
  between operations  18.2 us (3%)
  blocking collectives  16.1 us (3%)
    ppermute x21, waiting for transfers between devices, unspread(): lax.ppermute(v, ('seq', 'mp'), [(d, s) for s, d in spread_perm(dx, flip)])  66.2 us
    ppermute x18, waiting for transfers between devices, spread(): return lax.ppermute(v, ('seq', 'mp'), spread_perm(dx, flip))  59.5 us
    pallas_call x3, Pallas kernels, attention_backward(): pl.pallas_call(kernel, grid_spec=pltpu.PrefetchScalarGridSpec(num_scalar_...  32 us
    ppermute x18, starting transfers between devices, spread(): return lax.ppermute(v, ('seq', 'mp'), spread_perm(dx, flip))  28.9 us
    unnamed x334, local copies, waits for them, and re-layouts  28.7 us
    ppermute x21, starting transfers between devices, unspread(): lax.ppermute(v, ('seq', 'mp'), [(d, s) for s, d in spread_perm(dx, flip)])  27.5 us
    dot_general x11, matrix products, dot_nt(): lax.dot_general(left, right, (((1,), (1,)), ((), ())), preferred_element_...  25.1 us
    dot_general x11, matrix products, dot_tn(): lax.dot_general(left, right, (((0,), (0,)), ((), ())), preferred_element_...  23.1 us
  transfers between devices with their start and end apart: 72, of which 24 were waited for; matrix products, arithmetic and copies ran while one was open for 27% of the time, Pallas kernels for 19%

profile of v2, /device:TPU:0, one launch (start us, length us, event | category | flops | bytes accessed | tf_op | source)
XLA Modules:
  0.0 591.8 jit_solution(2774050278054919788)
XLA Ops:
  27.6 16.1 %all-gather = bf16[24,96,128]{2,1,0:T(8,128)(2,1)} all-gather(bf16[6,96,128]{2,1,0:T(8,128)(2,1)S(1)} %maximum_maximum_fusion.1), channel_id=2, replica_groups=mesh['dp'=4,'seq'=2,'mp'=4] {'dp'}, dimensions={0}, use_global_device_ids=true | all-gather | bytes 737280 | tf_op jit(solution)/shard_map/all_gather | solution.py:91
  46.0 4.7 collective-permute-done.2
  50.8 4.3 collective-permute-start.10
  67.6 6.7 %bias_tiles.1.refs_0_ = f32[6,5,256,256]{3,2,1,0:T(8,128)} custom-call(f32[6,1,1536]{2,1,0:T(1,128)} %broadcast_in_dim.36.line_ref), custom_call_target="tpu_custom_call" | custom-call | flops 15728640 | bytes 7864320 | tf_op jit(solution)/shard_map/bias_tiles/pallas_call | solution.py:357
  89.4 5.1 assemble_attn.2
  101.0 12.8 %attend_enc.1 = (bf16[768,384]{1,0:T(8,128)(2,1)S(1)}, f32[3,8,768]{2,1,0:T(8,128)S(1)}) custom-call(s32[1]{0:T(128)} %dynamic_slice.36.limit_ref, bf16[768,1152]{1,0:T(8,128)(2,1)S(1)} %fusion.6.q_ref, f32[6,5,256,256]{3,2,1,0:T(8,128)S(1)} %copy-done), custom_call_target="tpu_custom_call" | custom-call | flops 1811939328 | bytes 2359296 | tf_op jit(solution)/shard_map/attend_enc/pallas_call | solution.py:471
  115.7 19.9 %collective-permute-done.13.refs_3_ = bf16[4,2,96,768]{3,2,1,0:T(8,128)(2,1)} collective-permute-done((bf16[4,2,96,768]{3,2,1,0:T(8,128)(2,1)}, bf16[4,2,96,768]{3,2,1,0:T(8,128)(2,1)}, u32[]{:S(2)}, u32[]{:S(2)}) %collective-permute-start.13) | collective-permute-done | bytes 1179680 | tf_op jit(solution)/shard_map/ppermute | solution.py:66
  148.4 5.9 assemble_ffn.1
  159.6 4.3 multiply_convert_fusion
  166.9 5.2 collective-permute-done.19.refs_4_
  172.2 24.3 %collective-permute-done.18.refs_3_ = bf16[4,12,96,128]{3,2,1,0:T(8,128)(2,1)} collective-permute-done((bf16[4,12,96,128]{3,2,1,0:T(8,128)(2,1)}, bf16[4,12,96,128]{3,2,1,0:T(8,128)(2,1)}, u32[]{:S(2)}, u32[]{:S(2)}) %collective-permute-start.18) | collective-permute-done | bytes 1179680 | tf_op jit(solution)/shard_map/ppermute | solution.py:66
  197.2 6.1 %assemble_attn.3 = (bf16[4,2,96,1152]{3,2,1,0:T(8,128)(2,1)}, bf16[4,2,96,384]{3,2,1,0:T(8,128)(2,1)}, bf16[4,2,96,384]{3,2,1,0:T(8,128)(2,1)}, bf16[4,2,96,768]{3,2,1,0:T(8,128)(2,1)}, bf16[4,2,96,384]{3,2,1,0:T(8,128)(2,1)}) custom-call(s32[3]{0:T(128)} %pad_add_fusion.1.yi, bf16[4,12,96,128]{3,2,1,0:T(8,128)(2,1)} %bitcast.176, ...), custom_call_target="tpu_custom_call" | custom-call | bytes 10616832 | tf_op jit(solution)/shard_map/assemble_attn/pallas_call | solution.py:149
  221.6 4.6 attend_cross.1
  230.0 9.7 %all-gather.9.cloned.1.call-done.src = bf16[4,2,2,2,96,768]{5,4,3,2,1,0:T(8,128)(2,1)} async-done(((bf16[1,2,2,2,96,768]{5,4,3,2,1,0:T(8,128)(2,1)}), bf16[4,2,2,2,96,768]{5,4,3,2,1,0:T(8,128)(2,1)}) %all-gather.9.cloned.1.call-update) | async-done | bytes 4718608 | tf_op jit(solution)/shard_map/all_gather | solution.py:91
  279.7 5.9 attend_back_cross.1
  290.4 4.7 split_attn.3
  313.7 4.6 split_attn.4
  337.7 5.7 split_ffn.1
  343.4 5.4 convolution_convert_fusion.10
  368.3 4.7 multiply_reduce_fusion.1
  383.3 22.8 %attend_back_enc.1 = (bf16[768,1152]{1,0:T(8,128)(2,1)S(1)}, f32[6,8,512]{2,1,0:T(8,128)S(1)}) custom-call(s32[1]{0:T(128)} %dynamic_slice.36.limit_ref, bf16[768,1152]{1,0:T(8,128)(2,1)S(1)} %fusion.6.q_ref, f32[6,5,256,256]{3,2,1,0:T(8,128)S(1)} %copy-done.1, bf16[768,384]{1,0:T(8,128)(2,1)S(1)} %get-tuple-element.226.refs_1_, ...), custom_call_target="tpu_custom_call" | custom-call | flops 4529848320 | bytes 4718592 | tf_op jit(solution)/shard_map/attend_back_enc/pallas_call | solution.py:590
  408.9 17.9 %collective-permute-done.37 = bf16[4,2,96,768]{3,2,1,0:T(8,128)(2,1)} collective-permute-done((bf16[4,2,96,768]{3,2,1,0:T(8,128)(2,1)}, bf16[4,2,96,768]{3,2,1,0:T(8,128)(2,1)}, u32[]{:S(2)}, u32[]{:S(2)}) %collective-permute-start.37) | collective-permute-done | bytes 1179680 | tf_op jit(solution)/shard_map/ppermute | solution.py:70
  426.9 8.5 %collective-permute-done.39 = bf16[4,2,96,768]{3,2,1,0:T(8,128)(2,1)} collective-permute-done((bf16[4,2,96,768]{3,2,1,0:T(8,128)(2,1)}, bf16[4,2,96,768]{3,2,1,0:T(8,128)(2,1)}, u32[]{:S(2)}, u32[]{:S(2)}) %collective-permute-start.39) | collective-permute-done | bytes 1179680 | tf_op jit(solution)/shard_map/ppermute | solution.py:70
  441.7 4.3 add_convert_fusion
  458.4 4.6 split_attn.5
  475.2 12.1 %collective-permute-done.42 = bf16[4,6,96,128]{3,2,1,0:T(8,128)(2,1)} collective-permute-done((bf16[4,6,96,128]{3,2,1,0:T(8,128)(2,1)}, bf16[4,6,96,128]{3,2,1,0:T(8,128)(2,1)}, u32[]{:S(2)}, u32[]{:S(2)}) %collective-permute-start.42) | collective-permute-done | bytes 589856 | tf_op jit(solution)/shard_map/ppermute | solution.py:70
  487.4 6.9 %collective-permute-done.44 = bf16[4,6,96,128]{3,2,1,0:T(8,128)(2,1)} collective-permute-done((bf16[4,6,96,128]{3,2,1,0:T(8,128)(2,1)}, bf16[4,6,96,128]{3,2,1,0:T(8,128)(2,1)}, u32[]{:S(2)}, u32[]{:S(2)}) %collective-permute-start.44) | collective-permute-done | bytes 589856 | tf_op jit(solution)/shard_map/ppermute | solution.py:70
  520.8 13.9 %collective-permute-done.51 = bf16[4,6,96,128]{3,2,1,0:T(8,128)(2,1)} collective-permute-done((bf16[4,6,96,128]{3,2,1,0:T(8,128)(2,1)}, bf16[4,6,96,128]{3,2,1,0:T(8,128)(2,1)}, u32[]{:S(2)}, u32[]{:S(2)}) %collective-permute-start.51) | collective-permute-done | bytes 589856 | tf_op jit(solution)/shard_map/ppermute | solution.py:70
  534.7 4.2 collective-permute-done.53
  560.4 4.3 update_matrices.6
  564.6 11.7 %collective-permute-done.59.refs_2_ = bf16[512,768]{1,0:T(8,128)(2,1)} collective-permute-done((bf16[512,768]{1,0:T(8,128)(2,1)S(1)}, bf16[512,768]{1,0:T(8,128)(2,1)}, u32[]{:S(2)}, u32[]{:S(2)}) %collective-permute-start.59) | collective-permute-done | bytes 786464 | tf_op jit(solution)/shard_map/ppermute | solution.py:49
  576.3 4.7 place_quarters.2
  (701 shorter events, 296.9 us)
Async XLA Ops:
  7.2 71.5 %all-gather.11.cloned.1.call-start = ((), (), s32[]{:S(2)}) async-start(), calls=%async_computation.11 | async-start | bytes 1474560 | tf_op jit(solution)/shard_map/all_gather | solution.py:91
  9.9 40.9 %collective-permute-start = (bf16[1024,768]{1,0:T(8,128)(2,1)S(1)}, bf16[1024,768]{1,0:T(8,128)(2,1)}, u32[]{:S(2)}, u32[]{:S(2)}) collective-permute-start(bf16[1024,768]{1,0:T(8,128)(2,1)S(1)} %pad_maximum_fusion), channel_id=1, source_target_pairs={{0,4},{4,0},{1,5},{5,1},{2,6},{6,2},{3,7},{7,3},{8,12},{12,8},{9,1... | collective-permute-start | bytes 4718600 | tf_op jit(solution)/shard_map/ppermute | solution.py:45
  16.0 27.9 %collective-permute-start.6 = (f32[3648]{0:T(1024)}, f32[3648]{0:T(1024)S(1)}, u32[]{:S(2)}, u32[]{:S(2)}) collective-permute-start(f32[3648]{0:T(1024)} %constant_dynamic-update-slice_fusion), channel_id=1, source_target_pairs={{0,1},{1,0},{2,5},{3,4},{4,3},{5,2},{6,7},{7,6},{8,9},{9,8},{10,13... | collective-permute-start | bytes 43784 | tf_op jit(solution)/shard_map/ppermute | solution.py:66
  43.7 93.7 %all-gather.13.cloned.1.call-start = ((), (), s32[]{:S(2)}) async-start(), calls=%async_computation.12 | async-start | bytes 1474560 | tf_op jit(solution)/shard_map/all_gather | solution.py:91
  50.8 28.0 %collective-permute-start.10 = (bf16[4,6,96,128]{3,2,1,0:T(8,128)(2,1)}, bf16[4,6,96,128]{3,2,1,0:T(8,128)(2,1)}, u32[]{:S(2)}, u32[]{:S(2)}) collective-permute-start(bf16[4,6,96,128]{3,2,1,0:T(8,128)(2,1)} %bitcast.4.refs_0_), channel_id=1, source_target_pairs={{0,3},{1,2},{2,7},{3,6},{4,1},{5,0},{6,5},{7,4},{8,11},{9,10},{10,... | collective-permute-start | bytes 1769480 | tf_op jit(solution)/shard_map/ppermute | solution.py:66
  81.6 158.1 %all-gather.9.cloned.1.call-start = ((), (), s32[]{:S(2)}) async-start(), calls=%async_computation.5 | async-start | bytes 5898240 | tf_op jit(solution)/shard_map/all_gather | solution.py:91
  81.7 34.1 %collective-permute-start.14 = (bf16[4,2,96,768]{3,2,1,0:T(8,128)(2,1)}, bf16[4,2,96,768]{3,2,1,0:T(8,128)(2,1)}, u32[]{:S(2)}, u32[]{:S(2)}) collective-permute-start(bf16[4,2,96,768]{3,2,1,0:T(8,128)(2,1)} %bitcast.167), channel_id=1, source_target_pairs={{0,3},{1,2},{2,7},{3,6},{4,1},{5,0},{6,5},{7,4},{8,11},{9,10},{10,... | collective-permute-start | bytes 3538952 | tf_op jit(solution)/shard_map/ppermute | solution.py:66
  85.6 50.1 %collective-permute-start.13 = (bf16[4,2,96,768]{3,2,1,0:T(8,128)(2,1)}, bf16[4,2,96,768]{3,2,1,0:T(8,128)(2,1)}, u32[]{:S(2)}, u32[]{:S(2)}) collective-permute-start(bf16[4,2,96,768]{3,2,1,0:T(8,128)(2,1)} %bitcast.168), channel_id=1, source_target_pairs={{0,1},{1,0},{2,5},{3,4},{4,3},{5,2},{6,7},{7,6},{8,9},{9,8},{10,13... | collective-permute-start | bytes 3538952 | tf_op jit(solution)/shard_map/ppermute | solution.py:66
  86.6 50.8 %collective-permute-start.12 = (bf16[4,2,96,768]{3,2,1,0:T(8,128)(2,1)}, bf16[4,2,96,768]{3,2,1,0:T(8,128)(2,1)}, u32[]{:S(2)}, u32[]{:S(2)}) collective-permute-start(bf16[4,2,96,768]{3,2,1,0:T(8,128)(2,1)} %bitcast.169), channel_id=1, source_target_pairs={{0,2},{1,3},{2,6},{3,7},{4,0},{5,1},{6,4},{7,5},{8,10},{9,11},{10,... | collective-permute-start | bytes 3538952 | tf_op jit(solution)/shard_map/ppermute | solution.py:66
  86.6 50.8 %collective-permute-start.11 = (bf16[4,2,96,768]{3,2,1,0:T(8,128)(2,1)}, bf16[4,2,96,768]{3,2,1,0:T(8,128)(2,1)}, u32[]{:S(2)}, u32[]{:S(2)}) collective-permute-start(bf16[4,2,96,768]{3,2,1,0:T(8,128)(2,1)} %bitcast.170), channel_id=1, source_target_pairs={{2,4},{3,5},{4,2},{5,3},{10,12},{11,13},{12,10},{13,11},{18,20},{1... | collective-permute-start | bytes 3538952 | tf_op jit(solution)/shard_map/ppermute | solution.py:66
  142.6 29.6 %collective-permute-start.19 = (bf16[4,12,96,128]{3,2,1,0:T(8,128)(2,1)}, bf16[4,12,96,128]{3,2,1,0:T(8,128)(2,1)}, u32[]{:S(2)}, u32[]{:S(2)}) collective-permute-start(bf16[4,12,96,128]{3,2,1,0:T(8,128)(2,1)} %bitcast.172), channel_id=1, source_target_pairs={{0,3},{1,2},{2,7},{3,6},{4,1},{5,0},{6,5},{7,4},{8,11},{9,10},{10,... | collective-permute-start | bytes 3538952 | tf_op jit(solution)/shard_map/ppermute | solution.py:66
  145.4 51.1 %collective-permute-start.18 = (bf16[4,12,96,128]{3,2,1,0:T(8,128)(2,1)}, bf16[4,12,96,128]{3,2,1,0:T(8,128)(2,1)}, u32[]{:S(2)}, u32[]{:S(2)}) collective-permute-start(bf16[4,12,96,128]{3,2,1,0:T(8,128)(2,1)} %bitcast.173), channel_id=1, source_target_pairs={{0,1},{1,0},{2,5},{3,4},{4,3},{5,2},{6,7},{7,6},{8,9},{9,8},{10,13... | collective-permute-start | bytes 3538952 | tf_op jit(solution)/shard_map/ppermute | solution.py:66
  146.4 50.8 %collective-permute-start.17 = (bf16[4,12,96,128]{3,2,1,0:T(8,128)(2,1)}, bf16[4,12,96,128]{3,2,1,0:T(8,128)(2,1)}, u32[]{:S(2)}, u32[]{:S(2)}) collective-permute-start(bf16[4,12,96,128]{3,2,1,0:T(8,128)(2,1)} %bitcast.174), channel_id=1, source_target_pairs={{0,2},{1,3},{2,6},{3,7},{4,0},{5,1},{6,4},{7,5},{8,10},{9,11},{10,... | collective-permute-start | bytes 3538952 | tf_op jit(solution)/shard_map/ppermute | solution.py:66
  146.4 50.8 %collective-permute-start.16 = (bf16[4,12,96,128]{3,2,1,0:T(8,128)(2,1)}, bf16[4,12,96,128]{3,2,1,0:T(8,128)(2,1)}, u32[]{:S(2)}, u32[]{:S(2)}) collective-permute-start(bf16[4,12,96,128]{3,2,1,0:T(8,128)(2,1)} %bitcast.175), channel_id=1, source_target_pairs={{2,4},{3,5},{4,2},{5,3},{10,12},{11,13},{12,10},{13,11},{18,20},{1... | collective-permute-start | bytes 3538952 | tf_op jit(solution)/shard_map/ppermute | solution.py:66
  148.2 287.3 %reduce-scatter.6.cloned.1.call-start = ((), (), s32[]{:S(2)}) async-start(), calls=%async_computation.6 | async-start | bytes 5898240 | tf_op jit(solution)/shard_map/reduce_scatter | solution.py:95
  276.2 229.3 %reduce-scatter.14.cloned.1.call-start = ((), (), s32[]{:S(2)}) async-start(), calls=%async_computation.10 | async-start | bytes 737280 | tf_op jit(solution)/shard_map/reduce_scatter | solution.py:95
  300.2 48.7 %collective-permute-start.32 = (bf16[4,6,96,128]{3,2,1,0:T(8,128)(2,1)}, bf16[4,6,96,128]{3,2,1,0:T(8,128)(2,1)}, u32[]{:S(2)}, u32[]{:S(2)}) collective-permute-start(bf16[4,6,96,128]{3,2,1,0:T(8,128)(2,1)} %get-tuple-element.350), channel_id=1, source_target_pairs={{4,2},{5,3},{2,4},{3,5},{12,10},{13,11},{10,12},{11,13},{20,18},{2... | collective-permute-start | bytes 1769480 | tf_op jit(solution)/shard_map/ppermute | solution.py:70
  301.8 47.1 %collective-permute-start.33 = (bf16[4,6,96,128]{3,2,1,0:T(8,128)(2,1)}, bf16[4,6,96,128]{3,2,1,0:T(8,128)(2,1)}, u32[]{:S(2)}, u32[]{:S(2)}) collective-permute-start(bf16[4,6,96,128]{3,2,1,0:T(8,128)(2,1)} %get-tuple-element.273), channel_id=1, source_target_pairs={{2,0},{3,1},{6,2},{7,3},{0,4},{1,5},{4,6},{5,7},{10,8},{11,9},{14,... | collective-permute-start | bytes 1769480 | tf_op jit(solution)/shard_map/ppermute | solution.py:70
  303.8 45.0 %collective-permute-start.34 = (bf16[4,6,96,128]{3,2,1,0:T(8,128)(2,1)}, bf16[4,6,96,128]{3,2,1,0:T(8,128)(2,1)}, u32[]{:S(2)}, u32[]{:S(2)}) collective-permute-start(bf16[4,6,96,128]{3,2,1,0:T(8,128)(2,1)} %get-tuple-element.274), channel_id=1, source_target_pairs={{1,0},{0,1},{5,2},{4,3},{3,4},{2,5},{7,6},{6,7},{9,8},{8,9},{13,10... | collective-permute-start | bytes 1769480 | tf_op jit(solution)/shard_map/ppermute | solution.py:70
  305.3 43.6 %collective-permute-start.35 = (bf16[4,6,96,128]{3,2,1,0:T(8,128)(2,1)}, bf16[4,6,96,128]{3,2,1,0:T(8,128)(2,1)}, u32[]{:S(2)}, u32[]{:S(2)}) collective-permute-start(bf16[4,6,96,128]{3,2,1,0:T(8,128)(2,1)} %get-tuple-element.275), channel_id=1, source_target_pairs={{3,0},{2,1},{7,2},{6,3},{1,4},{0,5},{5,6},{4,7},{11,8},{10,9},{15,... | collective-permute-start | bytes 1769480 | tf_op jit(solution)/shard_map/ppermute | solution.py:70
  351.9 164.5 %all-gather.15.cloned.1.call-start = ((), (), s32[]{:S(2)}) async-start(), calls=%async_computation.13 | async-start | bytes 2949120 | tf_op jit(solution)/shard_map/all_gather | solution.py:932
  355.1 200.0 %reduce-scatter.10.cloned.1.call-start = ((), (), s32[]{:S(2)}) async-start(), calls=%async_computation.8 | async-start | bytes 1474560 | tf_op jit(solution)/shard_map/reduce_scatter | solution.py:95
  362.3 46.7 %collective-permute-start.36 = (bf16[4,2,96,768]{3,2,1,0:T(8,128)(2,1)}, bf16[4,2,96,768]{3,2,1,0:T(8,128)(2,1)}, u32[]{:S(2)}, u32[]{:S(2)}) collective-permute-start(bf16[4,2,96,768]{3,2,1,0:T(8,128)(2,1)} %get-tuple-element.325), channel_id=1, source_target_pairs={{4,2},{5,3},{2,4},{3,5},{12,10},{13,11},{10,12},{11,13},{20,18},{2... | collective-permute-start | bytes 3538952 | tf_op jit(solution)/shard_map/ppermute | solution.py:70
  364.0 62.9 %collective-permute-start.37 = (bf16[4,2,96,768]{3,2,1,0:T(8,128)(2,1)}, bf16[4,2,96,768]{3,2,1,0:T(8,128)(2,1)}, u32[]{:S(2)}, u32[]{:S(2)}) collective-permute-start(bf16[4,2,96,768]{3,2,1,0:T(8,128)(2,1)} %get-tuple-element.285), channel_id=1, source_target_pairs={{2,0},{3,1},{6,2},{7,3},{0,4},{1,5},{4,6},{5,7},{10,8},{11,9},{14,... | collective-permute-start | bytes 3538952 | tf_op jit(solution)/shard_map/ppermute | solution.py:70
  366.0 60.9 %collective-permute-start.38 = (bf16[4,2,96,768]{3,2,1,0:T(8,128)(2,1)}, bf16[4,2,96,768]{3,2,1,0:T(8,128)(2,1)}, u32[]{:S(2)}, u32[]{:S(2)}) collective-permute-start(bf16[4,2,96,768]{3,2,1,0:T(8,128)(2,1)} %get-tuple-element.286), channel_id=1, source_target_pairs={{1,0},{0,1},{5,2},{4,3},{3,4},{2,5},{7,6},{6,7},{9,8},{8,9},{13,10... | collective-permute-start | bytes 3538952 | tf_op jit(solution)/shard_map/ppermute | solution.py:70
  367.5 67.9 %collective-permute-start.39 = (bf16[4,2,96,768]{3,2,1,0:T(8,128)(2,1)}, bf16[4,2,96,768]{3,2,1,0:T(8,128)(2,1)}, u32[]{:S(2)}, u32[]{:S(2)}) collective-permute-start(bf16[4,2,96,768]{3,2,1,0:T(8,128)(2,1)} %get-tuple-element.287), channel_id=1, source_target_pairs={{3,0},{2,1},{7,2},{6,3},{1,4},{0,5},{5,6},{4,7},{11,8},{10,9},{15,... | collective-permute-start | bytes 3538952 | tf_op jit(solution)/shard_map/ppermute | solution.py:70
  435.6 35.8 %collective-permute-start.45 = (bf16[768,768]{1,0:T(8,128)(2,1)}, bf16[768,768]{1,0:T(8,128)(2,1)}, u32[]{:S(2)}, u32[]{:S(2)}) collective-permute-start(bf16[768,768]{1,0:T(8,128)(2,1)} %convolution_convert_fusion.6), channel_id=1, source_target_pairs={{0,4},{4,0},{1,5},{5,1},{2,6},{6,2},{3,7},{7,3},{8,12},{12,8},{9,1... | collective-permute-start | bytes 3538952 | tf_op jit(solution)/shard_map/ppermute | solution.py:45
  447.4 110.5 %reduce-scatter.12.cloned.1.call-start = ((), (), s32[]{:S(2)}) async-start(), calls=%async_computation.9 | async-start | bytes 737280 | tf_op jit(solution)/shard_map/reduce_scatter | solution.py:95
  512.0 26.9 %collective-permute-start.53 = (bf16[4,6,96,128]{3,2,1,0:T(8,128)(2,1)}, bf16[4,6,96,128]{3,2,1,0:T(8,128)(2,1)}, u32[]{:S(2)}, u32[]{:S(2)}) collective-permute-start(bf16[4,6,96,128]{3,2,1,0:T(8,128)(2,1)} %get-tuple-element.310), channel_id=1, source_target_pairs={{3,0},{2,1},{7,2},{6,3},{1,4},{0,5},{5,6},{4,7},{11,8},{10,9},{15,... | collective-permute-start | bytes 1769480 | tf_op jit(solution)/shard_map/ppermute | solution.py:70
  514.9 66.1 %reduce-scatter.8.cloned.1.call-start = ((), (), s32[]{:S(2)}) async-start(), calls=%async_computation.7 | async-start | bytes 737280 | tf_op jit(solution)/shard_map/reduce_scatter | solution.py:95
  539.9 36.4 %collective-permute-start.59 = (bf16[512,768]{1,0:T(8,128)(2,1)S(1)}, bf16[512,768]{1,0:T(8,128)(2,1)}, u32[]{:S(2)}, u32[]{:S(2)}) collective-permute-start(bf16[512,768]{1,0:T(8,128)(2,1)S(1)} %pad_maximum_fusion.3.refs_0_), channel_id=1, source_target_pairs={{0,2},{1,3},{2,0},{3,1},{4,6},{5,7},{6,4},{7,5},{8,10},{9,11},{10,... | collective-permute-start | bytes 2359304 | tf_op jit(solution)/shard_map/ppermute | solution.py:49
  542.4 33.9 %collective-permute-start.58 = (bf16[512,768]{1,0:T(8,128)(2,1)S(1)}, bf16[512,768]{1,0:T(8,128)(2,1)}, u32[]{:S(2)}, u32[]{:S(2)}) collective-permute-start(bf16[512,768]{1,0:T(8,128)(2,1)S(1)} %pad_maximum_fusion.3.refs_0_), channel_id=1, source_target_pairs={{0,1},{1,0},{2,3},{3,2},{4,5},{5,4},{6,7},{7,6},{8,9},{9,8},{10,11... | collective-permute-start | bytes 2359304 | tf_op jit(solution)/shard_map/ppermute | solution.py:49
  (201 other events, 2567.5 us)
Sparse Core Ops, SparseCore 0:
  43.8 31.0 all-gather.10
  81.7 33.4 all-gather.12
  148.3 91.3 all-gather.8
  276.3 83.6 reduce-scatter.5
  362.8 22.4 reduce-scatter.13
  387.6 50.9 all-gather.14
  447.5 27.6 reduce-scatter.9
  515.0 20.6 reduce-scatter.11
  546.4 22.7 reduce-scatter.7

commit v3 on v2

--- a/solution.py
+++ b/solution.py
@@ -19,6 +19,8 @@
 PAIR = 128
 BF16 = jnp.bfloat16
 F32 = jnp.float32
+ON_CHIP = pl.BlockSpec(memory_space=pltpu.VMEM)
+SCALARS = pl.BlockSpec(memory_space=pltpu.SMEM)
 
 
 def bf(a):
@@ -127,36 +129,30 @@
     def kernel(yi, *refs):
         ins, outs = refs[:5], refs[5:]
         low = half_lanes((rows, PAIR))
-        for a in range(2):
-            side = yi[a]
-
-            def tile(t, dx):
-                val = ins[1 + dx * 2 + a][0, t]
-                return jnp.where(yi[2] == 1, ins[0][0, t], val) if dx + a == 0 else val
-
-            for out, plan in zip(outs, plans):
-                for place, (mat, j) in enumerate(plan):
-                    if j < 2:
-                        val = tile(mat, j)
-                    else:
-                        t0, t1 = tile(count + mat // 2, 0), tile(count + mat // 2, 1)
-                        if mat % 2 == 0:
-                            val = jnp.where(low, t0, half_roll(t1))
+        for k in range(n):
+            for a in range(2):
+                side = yi[a]
+
+                def tile(t, dx):
+                    val = ins[1 + dx * 2 + a][k, t]
+                    return jnp.where(yi[2] == 1, ins[0][k, t], val) if dx + a == 0 else val
+
+                for out, plan in zip(outs, plans):
+                    for place, (mat, j) in enumerate(plan):
+                        if j < 2:
+                            val = tile(mat, j)
                         else:
-                            val = jnp.where(low, half_roll(t0), t1)
-                    out[0, side, :, place * PAIR : (place + 1) * PAIR] = val
+                            t0, t1 = tile(count + mat // 2, 0), tile(count + mat // 2, 1)
+                            if mat % 2 == 0:
+                                val = jnp.where(low, t0, half_roll(t1))
+                            else:
+                                val = jnp.where(low, half_roll(t0), t1)
+                        out[k, side, :, place * PAIR : (place + 1) * PAIR] = val
 
     outs = pl.pallas_call(
         kernel,
-        grid_spec=pltpu.PrefetchScalarGridSpec(
-            num_scalar_prefetch=1,
-            grid=(n,),
-            in_specs=[pl.BlockSpec((1, tiles, rows, PAIR), lambda k, yi: (k, 0, 0, 0))] * 5,
-            out_specs=[
-                pl.BlockSpec((1, 2, rows, PAIR * len(p)), lambda k, yi: (k, 0, 0, 0))
-                for p in plans
-            ],
-        ),
+        in_specs=[SCALARS] + [ON_CHIP] * 5,
+        out_specs=[ON_CHIP] * len(plans),
         out_shape=[jax.ShapeDtypeStruct((n, 2, rows, PAIR * len(p)), BF16) for p in plans],
         cost_estimate=pl.CostEstimate(
             flops=0, transcendentals=0, bytes_accessed=9 * n * tiles * rows * PAIR * 2
@@ -178,44 +174,37 @@
     def kernel(yi, *refs):
         srcs, outs = refs[: len(mats)], refs[len(mats) :]
         low = half_lanes((rows, PAIR))
-        for a in range(2):
-            side = yi[a]
-
-            def get(mat, j):
-                i, place = where[(mat, j)]
-                return srcs[i][0, side, :, place * PAIR : (place + 1) * PAIR]
-
-            for dx in range(2):
-                for t in range(tiles):
-                    if t < count:
-                        val = get(t, dx)
-                    else:
-                        p = t - count
-                        t0, t1 = get(2 * p, 2), get(2 * p + 1, 2)
-                        if dx == 0:
-                            val = jnp.where(low, t0, half_roll(t1))
+        for k in range(n):
+            for a in range(2):
+                side = yi[a]
+
+                def get(mat, j):
+                    i, place = where[(mat, j)]
+                    return srcs[i][k, side, :, place * PAIR : (place + 1) * PAIR]
+
+                for dx in range(2):
+                    for t in range(tiles):
+                        if t < count:
+                            val = get(t, dx)
                         else:
-                            val = jnp.where(low, half_roll(t0), t1)
-                    outs[dx * 2 + a][0, t] = val
-
-    outs = pl.pallas_call(
+                            p = t - count
+                            t0, t1 = get(2 * p, 2), get(2 * p + 1, 2)
+                            if dx == 0:
+                                val = jnp.where(low, t0, half_roll(t1))
+                            else:
+                                val = jnp.where(low, half_roll(t0), t1)
+                        outs[dx * 2 + a][k, t] = val
+
+    return pl.pallas_call(
         kernel,
-        grid_spec=pltpu.PrefetchScalarGridSpec(
-            num_scalar_prefetch=1,
-            grid=(n,),
-            in_specs=[
-                pl.BlockSpec((1, 2, rows, m.shape[-1]), lambda k, yi: (k, 0, 0, 0))
-                for m in ins
-            ],
-            out_specs=[pl.BlockSpec((1, tiles, rows, PAIR), lambda k, yi: (k, 0, 0, 0))] * 4,
-        ),
+        in_specs=[SCALARS] + [ON_CHIP] * len(ins),
+        out_specs=[ON_CHIP] * 4,
         out_shape=[jax.ShapeDtypeStruct((n, tiles, rows, PAIR), BF16)] * 4,
         cost_estimate=pl.CostEstimate(
             flops=0, transcendentals=0, bytes_accessed=8 * n * tiles * rows * PAIR * 2
         ),
         name="split_attn",
     )(yidx, *ins)
-    return outs
 
 
 def assemble_ffn(pieces, yidx):
@@ -223,24 +212,18 @@
 
     def kernel(yi, *refs):
         ins, outs = refs[:5], refs[5:]
-        for a in range(2):
-            for h in range(2):
-                for dx in range(2):
-                    val = ins[1 + dx * 2 + a][0, h]
-                    val = jnp.where(yi[2] == 1, ins[0][0, h], val) if dx + a == 0 else val
-                    outs[h][0, yi[a], :, dx * cols : (dx + 1) * cols] = val
+        for k in range(n):
+            for a in range(2):
+                for h in range(2):
+                    for dx in range(2):
+                        val = ins[1 + dx * 2 + a][k, h]
+                        val = jnp.where(yi[2] == 1, ins[0][k, h], val) if dx + a == 0 else val
+                        outs[h][k, yi[a], :, dx * cols : (dx + 1) * cols] = val
 
     outs = pl.pallas_call(
         kernel,
-        grid_spec=pltpu.PrefetchScalarGridSpec(
-            num_scalar_prefetch=1,
-            grid=(n,),
-            in_specs=[pl.BlockSpec((1, 2, rows, cols), lambda k, yi: (k, 0, 0, 0))] * 5,
-            out_specs=[
-                pl.BlockSpec((1, 2, rows, 2 * cols), lambda k, yi: (k, 0, 0, 0))
-            ]
-            * 2,
-        ),
+        in_specs=[SCALARS] + [ON_CHIP] * 5,
+        out_specs=[ON_CHIP] * 2,
         out_shape=[jax.ShapeDtypeStruct((n, 2, rows, 2 * cols), BF16)] * 2,
         cost_estimate=pl.CostEstimate(
             flops=0, transcendentals=0, bytes_accessed=2 * 9 * n * rows * cols * 2
@@ -257,19 +240,18 @@
 
     def kernel(yi, *refs):
         srcs, outs = refs[:2], refs[2:]
-        for a in range(2):
-            for h in range(2):
-                for dx in range(2):
-                    outs[dx * 2 + a][0, h] = srcs[h][0, yi[a], :, dx * cols : (dx + 1) * cols]
+        for k in range(n):
+            for a in range(2):
+                for h in range(2):
+                    for dx in range(2):
+                        outs[dx * 2 + a][k, h] = srcs[h][
+                            k, yi[a], :, dx * cols : (dx + 1) * cols
+                        ]
 
     return pl.pallas_call(
         kernel,
-        grid_spec=pltpu.PrefetchScalarGridSpec(
-            num_scalar_prefetch=1,
-            grid=(n,),
-            in_specs=[pl.BlockSpec((1, 2, rows, 2 * cols), lambda k, yi: (k, 0, 0, 0))] * 2,
-            out_specs=[pl.BlockSpec((1, 2, rows, cols), lambda k, yi: (k, 0, 0, 0))] * 4,
-        ),
+        in_specs=[SCALARS] + [ON_CHIP] * 2,
+        out_specs=[ON_CHIP] * 4,
         out_shape=[jax.ShapeDtypeStruct((n, 2, rows, cols), BF16)] * 4,
         cost_estimate=pl.CostEstimate(
             flops=0, transcendentals=0, bytes_accessed=2 * 8 * n * rows * cols * 2
@@ -467,7 +449,7 @@
         args.append(memory)
     if bias is not None:
         in_specs.append(pl.BlockSpec((2,) + bias.shape[1:], lambda j, n: (j, 0, 0, 0)))
-        args.append(bias)
+        args.append(pltpu.with_memory_space_constraint(bias, pltpu.HBM))
     return pl.pallas_call(
         kernel,
         grid_spec=pltpu.PrefetchScalarGridSpec(
@@ -509,6 +491,8 @@
         refs = refs[3:]
         dq_ref = refs.pop(0)
         dkv_ref = dq_ref if fused else refs.pop(0)
+        dq_sum = refs.pop(0)
+        dkv_sum = dq_sum if fused else refs.pop(0)
         diag_ref = refs.pop(0) if bias is not None else None
         dk_acc, dv_acc = refs[:2]
         tile_acc = refs[2] if bias is not None else None
@@ -518,6 +502,7 @@
         key_a = [head_keys(keys, limit_ref[0], a) for a in range(2)]
         pure_key_a = [only_head(keys, a) for a in range(2)]
         value_a = [only_head(values, a) for a in range(2)]
+        dq_sum[...] = jnp.zeros_like(dq_sum)
         dk_acc[...] = jnp.zeros_like(dk_acc)
         dv_acc[...] = jnp.zeros_like(dv_acc)
         if bias is not None:
@@ -550,14 +535,18 @@
                     dqt = dqt + dot_tn(pure_key_a[a][span], dsb)
                     if bias is not None:
                         tile_acc[a, kb - qb + key_blocks - 1] += ds
-            dq_ref[rows, 0:PAIR] = bf(jnp.transpose(dqt) * scale)
+            dq = bf(jnp.transpose(dqt) * scale)
+            dq_ref[rows, 0:PAIR] = dq
+            dq_sum[0:1, 0:PAIR] += jnp.sum(wide(dq), axis=0, keepdims=True)
 
         if query_blocks == 1:
             visit(0)
         else:
             pl.loop(0, query_blocks)(visit)
         dkv_ref[:, k0 : k0 + PAIR] = bf(dk_acc[...])
-        dkv_ref[:, k0 + PAIR : k0 + 2 * PAIR] = bf(dv_acc[...])
+        dv = bf(dv_acc[...])
+        dkv_ref[:, k0 + PAIR : k0 + 2 * PAIR] = dv
+        dkv_sum[0:1, k0 + PAIR : k0 + 2 * PAIR] = jnp.sum(wide(dv), axis=0, keepdims=True)
         if bias is not None:
             for a in range(2):
                 for d in range(spans):
@@ -570,7 +559,7 @@
         args.append(memory)
     if bias is not None:
         in_specs.append(pl.BlockSpec((2,) + bias.shape[1:], lambda j, n: (j, 0, 0, 0)))
-        args.append(bias)
+        args.append(pltpu.with_memory_space_constraint(bias, pltpu.HBM))
     in_specs += [
         pl.BlockSpec((query_len, PAIR), lambda j, n: (0, j)),
         pl.BlockSpec((1, 8, query_len), lambda j, n: (j, 0, 0)),
@@ -583,6 +572,10 @@
     if not fused:
         out_specs.append(pl.BlockSpec((key_len, 2 * PAIR), lambda j, n: (0, j)))
         out_shape.append(jax.ShapeDtypeStruct(memory.shape, BF16))
+    for array, tiles in ((queries, 3 if fused else 1), (memory, 2)):
+        if array is not None:
+            out_specs.append(pl.BlockSpec((8, tiles * PAIR), lambda j, n: (0, j)))
+            out_shape.append(jax.ShapeDtypeStruct((8, array.shape[1]), F32))
     if bias is not None:
         out_specs.append(pl.BlockSpec((2, 8, 2 * BLOCK), lambda j, n: (j, 0, 0)))
         out_shape.append(jax.ShapeDtypeStruct((2 * pairs, 8, 2 * BLOCK), F32))
@@ -615,21 +608,156 @@
     return 0.5 * (1.0 + lax.erf(z * ROOT_HALF)) + z * jnp.exp(-0.5 * z * z) * INV_ROOT_TAU
 
 
-def norm_forward(values, gain, offset):
-    center = values - jnp.mean(values, axis=-1, keepdims=True)
-    inv = lax.rsqrt(jnp.mean(center * center, axis=-1, keepdims=True) + EPSILON)
-    normed = center * inv
-    return normed * gain + offset, normed, inv
-
-
-def norm_backward(upstream, normed, inv, gain):
-    scaled = upstream * gain
-    inner = (
-        scaled
-        - jnp.mean(scaled, axis=-1, keepdims=True)
-        - normed * jnp.mean(scaled * normed, axis=-1, keepdims=True)
-    )
-    return inv * inner, jnp.sum(upstream * normed, axis=0), jnp.sum(upstream, axis=0)
+ROWS = 128
+
+
+def row_steps(count, body):
+    @pl.loop(0, count // ROWS)
+    def _(step):
+        body(pl.ds(pl.multiple_of(step * ROWS, ROWS), ROWS), step)
+
+
+def add_norm(residual, own_part, other_part, vecs, bias, gain, shift):
+    source, affine = residual if isinstance(residual, tuple) else (residual, None)
+    count, width = source.shape
+
+    def kernel(x_ref, p_ref, q_ref, v_ref, low_ref, normed_ref, inv_ref):
+        def body(rows, step):
+            base = wide(x_ref[rows])
+            if affine is not None:
+                base = base * v_ref[affine[0] : affine[0] + 1] + v_ref[affine[1] : affine[1] + 1]
+            values = base + (wide(p_ref[rows]) + wide(q_ref[rows])) + v_ref[bias : bias + 1]
+            center = values - jnp.sum(values, axis=-1, keepdims=True) * (1.0 / width)
+            square = jnp.sum(center * center, axis=-1, keepdims=True)
+            inv = lax.rsqrt(square * (1.0 / width) + EPSILON)
+            normed = center * inv
+            low_ref[rows] = bf(normed * v_ref[gain : gain + 1] + v_ref[shift : shift + 1])
+            normed_ref[rows] = normed
+            inv_ref[rows] = jnp.broadcast_to(inv, (ROWS, PAIR))
+
+        row_steps(count, body)
+
+    return pl.pallas_call(
+        kernel,
+        in_specs=[ON_CHIP] * 4,
+        out_specs=[ON_CHIP] * 3,
+        out_shape=[
+            jax.ShapeDtypeStruct((count, width), BF16),
+            jax.ShapeDtypeStruct((count, width), F32),
+            jax.ShapeDtypeStruct((count, PAIR), F32),
+        ],
+        cost_estimate=pl.CostEstimate(
+            flops=12 * count * width, transcendentals=count, bytes_accessed=14 * count * width
+        ),
+        name="add_norm",
+    )(source, own_part, other_part, vecs)
+
+
+def norm_back(terms, limit, normed, inv, vecs, gain):
+    count, width = normed.shape
+    use = limit is not None
+
+    def kernel(*refs):
+        refs = list(refs)
+        limit_ref = refs.pop(0) if use else None
+        ins, (n_ref, inv_ref, v_ref, grad_ref, low_ref, sum_ref) = refs[:-6], refs[-6:]
+        sum_ref[...] = jnp.zeros_like(sum_ref)
+
+        def body(rows, step):
+            up = wide(ins[0][rows])
+            if use:
+                place = step * ROWS + lax.broadcasted_iota(jnp.int32, up.shape, 0)
+                up = jnp.where(place < limit_ref[0], up, 0.0)
+            rest = [wide(r[rows]) for r in ins[1:]]
+            if rest:
+                up = up + (rest[0] + rest[1])
+            values = n_ref[rows]
+            scaled = up * v_ref[gain : gain + 1]
+            mean = jnp.sum(scaled, axis=-1, keepdims=True) * (1.0 / width)
+            along = jnp.sum(scaled * values, axis=-1, keepdims=True) * (1.0 / width)
+            grad = inv_ref[rows, :1] * (scaled - mean - values * along)
+            grad_ref[rows] = grad
+            low_ref[rows] = bf(grad)
+            sum_ref[0:1] += jnp.sum(up * values, axis=0, keepdims=True)
+            sum_ref[1:2] += jnp.sum(up, axis=0, keepdims=True)
+            sum_ref[2:3] += jnp.sum(grad, axis=0, keepdims=True)
+
+        row_steps(count, body)
+
+    smem = [pl.BlockSpec(memory_space=pltpu.SMEM)] if use else []
+    return pl.pallas_call(
+        kernel,
+        in_specs=smem + [ON_CHIP] * (len(terms) + 3),
+        out_specs=[ON_CHIP] * 3,
+        out_shape=[
+            jax.ShapeDtypeStruct((count, width), F32),
+            jax.ShapeDtypeStruct((count, width), BF16),
+            jax.ShapeDtypeStruct((8, width), F32),
+        ],
+        cost_estimate=pl.CostEstimate(
+            flops=16 * count * width, transcendentals=0, bytes_accessed=20 * count * width
+        ),
+        name="norm_back",
+    )(*([limit] if use else []), *terms, normed, inv, vecs)
+
+
+NORM_ROWS = 15
+
+
+def pack_small(norm_sums, enc_sum, dec_sum, query_sum, memory_sum, unit_sums, diag, buckets):
+    width = norm_sums[0].shape[1]
+    heads, _, span = diag.shape
+    spans = 2 * (span // BLOCK) + 1
+    length = (spans + 1) * BLOCK
+
+    def kernel(*refs):
+        one, two, d_one, d_two, d_three = refs[:5]
+        enc_ref, dec_ref, query_ref, memory_ref, unit_ref, dec_unit_ref, diag_ref = refs[5:12]
+        outs, line = refs[12:14], refs[14]
+        norms = [(one, 0), (one, 1), (two, 0), (two, 1), (one, 2), (two, 2)]
+        norms += [(r, i) for r in (d_one, d_two, d_three) for i in range(2)]
+        norms += [(r, 2) for r in (d_one, d_two, d_three)]
+        tiles = [(enc_ref, 3, 0), (enc_ref, 3, 2), (dec_ref, 3, 0)]
+        tiles += [(dec_ref, 3, 2), (query_ref, 1, 0), (memory_ref, 2, 1)]
+        line[...] = jnp.zeros_like(line)
+        for h in range(heads):
+            for d in range(spans):
+                row = diag_ref[h, d : d + 1, :]
+                start = (spans - 1 - d) * BLOCK
+                line[h : h + 1, start : start + BLOCK] += row[:, BLOCK:]
+                line[h : h + 1, start + BLOCK : start + 2 * BLOCK] += row[:, :BLOCK]
+        wide_table = -(-buckets // PAIR) * PAIR
+        dist = length // 2 - lax.broadcasted_iota(jnp.int32, (length, wide_table), 0)
+        bucket = jnp.clip(dist, -(buckets // 2), buckets // 2 - 1) + buckets // 2
+        hot = jnp.where(
+            bucket == lax.broadcasted_iota(jnp.int32, (length, wide_table), 1), 1.0, 0.0
+        )
+        table = jnp.dot(
+            line[...], hot, precision=lax.Precision.HIGHEST, preferred_element_type=F32
+        )
+        for dx, out in enumerate(outs):
+            out[...] = jnp.zeros_like(out)
+            for i, (ref, r) in enumerate(norms):
+                out[i : i + 1, :] = ref[r : r + 1, :]
+            for i, (ref, stride, at) in enumerate(tiles):
+                row, lane = NORM_ROWS + i // 3, (i % 3) * 2 * PAIR
+                part = [ref[0:1, (j * stride + at) * PAIR : (j * stride + at + 1) * PAIR] for j in range(3)]
+                out[row : row + 1, lane : lane + PAIR] = part[dx]
+                both = jnp.broadcast_to(part[2], (8, PAIR))
+                both = pltpu.roll(both, PAIR // 2, 1) if dx else both
+                out[row : row + 1, lane + PAIR : lane + 2 * PAIR] = both[0:1]
+            for i, ref in enumerate((unit_ref, dec_unit_ref)):
+                out[NORM_ROWS + 2 + i : NORM_ROWS + 3 + i, :] = ref[0:1, dx * width : (dx + 1) * width]
+            for i, h in enumerate(((0, 1, 4), (2, 3, 5))[dx]):
+                out[NORM_ROWS + 4 + i : NORM_ROWS + 5 + i, 0:wide_table] = table[h : h + 1]
+
+    return pl.pallas_call(
+        kernel,
+        out_shape=[jax.ShapeDtypeStruct((24, width), F32)] * 2,
+        scratch_shapes=[pltpu.VMEM((8, length), F32)],
+        compiler_params=pltpu.CompilerParams(vmem_limit_bytes=32 << 20),
+        name="pack_small",
+    )(*norm_sums, enc_sum, dec_sum, query_sum, memory_sum, *unit_sums, diag)
 
 
 def update_matrices(sums, alternative, own, state, rate, inverse, packed):
@@ -700,32 +828,27 @@
     )(own, inverse, *args, *state)
 
 
-def place_quarters(parts, index, cuts):
-    rows, cols = parts[0].shape
+def place_quarters(parts, index):
     count = len(parts)
 
     def kernel(idx, *refs):
-        outs = refs[count:]
-        for k in range(count):
-
-            @pl.when(pl.program_id(0) == k)
-            def _():
-                start = 0
-                for out, cut in zip(outs, cuts):
-                    out[0] = refs[k][start : start + cut]
-                    start += cut
+        out, sem = refs[count], refs[count + 1]
+        copies = [
+            pltpu.make_async_copy(refs[k], out.at[idx[k]], sem.at[k]) for k in range(count)
+        ]
+        for copy in copies:
+            copy.start()
+        for copy in copies:
+            copy.wait()
 
     return pl.pallas_call(
         kernel,
-        grid_spec=pltpu.PrefetchScalarGridSpec(
-            num_scalar_prefetch=1,
-            grid=(count,),
-            in_specs=[pl.BlockSpec((rows, cols), lambda g, idx: (0, 0))] * count,
-            out_specs=[pl.BlockSpec((1, c, cols), lambda g, idx: (idx[g], 0, 0)) for c in cuts],
-        ),
-        out_shape=[jax.ShapeDtypeStruct((count, c, cols), parts[0].dtype) for c in cuts],
+        in_specs=[pl.BlockSpec(memory_space=pltpu.SMEM)] + [ON_CHIP] * count,
+        out_specs=pl.BlockSpec(memory_space=pl.ANY),
+        out_shape=jax.ShapeDtypeStruct((count,) + parts[0].shape, parts[0].dtype),
+        scratch_shapes=[pltpu.SemaphoreType.DMA((count,))],
         cost_estimate=pl.CostEstimate(
-            flops=0, transcendentals=0, bytes_accessed=4 * count * rows * cols
+            flops=0, transcendentals=0, bytes_accessed=4 * count * parts[0].size
         ),
         name="place_quarters",
     )(index, *parts)
@@ -739,21 +862,9 @@
     return mean_grad, new_master, new_moment, new_average
 
 
-def both_cores(low):
-    return wide(low) + wide(swap_core(low))
-
-
 def order_cols(v0, v1):
     return jnp.concatenate(
         [v0[..., :PAIR], v1[..., :PAIR], v0[..., PAIR:], v1[..., PAIR:]], axis=-1
-    )
-
-
-def group_cols(v):
-    half = PAIR // 2
-    return (
-        jnp.concatenate([v[..., :PAIR], v[..., 2 * PAIR : 2 * PAIR + half]], axis=-1),
-        jnp.concatenate([v[..., PAIR : 2 * PAIR], v[..., 2 * PAIR + half :]], axis=-1),
     )
 
 
@@ -764,14 +875,6 @@
 ]
 QKV_PLAN = [(m, j) for j in range(3) for m in range(3)]
 ENC_PLANS = [QKV_PLAN, [(3, j) for j in range(3)]]
-DEC_PLANS = [
-    QKV_PLAN,
-    [(3, j) for j in range(3)],
-    [(4, j) for j in range(3)],
-    [(m, j) for j in range(3) for m in (5, 6)],
-    [(7, j) for j in range(3)],
-]
-
 
 def local(
     frames,
@@ -831,7 +934,10 @@
     packed = jnp.concatenate([col_bias, dec_col_bias, rel_table.T.reshape(-1)])
     groups = [jnp.where(own, packed, spread(packed, 0, 0)), spread(packed, 1, 0)]
     ffn_z = gather_dp(after(bf(ffn_master), attn_z))
-    mine, other, dffn_parts, attn_z, groups = stage(mine, other, dffn_parts, attn_z, groups)
+    mine, other, dffn_parts, attn_z, groups, dattn_low, lengths = stage(
+        mine, other, dffn_parts, attn_z, groups, dec_attn_master, lengths
+    )
+    dattn_low = bf(dattn_low)
     attn_pieces = gather_plane(attn_z)
 
     bucket_count, group_heads = rel_table.shape
@@ -894,89 +1000,91 @@
 
     owners = m ^ jnp.arange(4, dtype=jnp.int32)
 
+    frame_count = jnp.sum(lengths)
+    digit_row = lax.broadcasted_iota(jnp.int32, (1,) + dec_attn_master.shape[1:2] + (PAIR,), 1)
+    digits = bf(jnp.where(digit_row == 0, frame_count // 256, frame_count % 256))
+
     attn_pieces, ffn_z, bias, bias_qkv, inputs, dattn_shard, dffn_plane = stage(
         attn_pieces,
         ffn_z,
         bias,
         bias_qkv,
         inputs,
-        pack_attn(bf(dec_attn_master)),
+        jnp.concatenate(
+            [pack_attn(dattn_low[:4]), pack_attn(dattn_low[4:]), digits]
+        ),
         jnp.stack([jnp.where(own, dffn_parts[0], dffn_parts[1]), *dffn_parts[2:]]),
     )
     ffn_pieces = gather_plane(ffn_z)
     dattn_z = gather_dp(dattn_shard)
-    dffn_planes = gather_dp(after(dffn_plane, dattn_z).reshape((2, 2) + dffn_shard.shape))
     w_qkv, w_o = assemble_attn(attn_pieces, ENC_PLANS, 4, yidx)
     qkv = bf(dot_nn(inputs, w_qkv) + bias_qkv)
     context, lse = attention_forward(qkv, None, limit, bias, False, True)
     part = bf(dot_nt(context, w_o))
-    ffn_pieces, dattn_z, part = stage(ffn_pieces, dattn_z, part)
-    dattn_pieces = gather_plane(dattn_z)
-    attn_sum = both_cores(part)
-    hidden_one, normed_one, inv_one = norm_forward(
-        wide(inputs) + attn_sum + norm_vecs[4], norm_vecs[0], norm_vecs[1]
-    )
-    hidden_low = bf(hidden_one)
+    ffn_pieces, dattn_z, part, dffn_plane = stage(ffn_pieces, dattn_z, part, dffn_plane)
+    tiles = dattn_z.shape[1] // 2
+    frame_total = jnp.sum(wide(dattn_z[:, -1, 0, 0]) * 256.0 + wide(dattn_z[:, -1, 1, 0]))
+    inverse = (1.0 / frame_total).reshape(1)
+    cross_z = dattn_z[:, tiles : 2 * tiles]
+    self_pieces = gather_plane(dattn_z[:, :tiles])
+    dffn_planes = gather_dp(dffn_plane.reshape((2, 2) + dffn_shard.shape))
+    hidden_low, normed_one, inv_one = add_norm(
+        inputs, part, swap_core(part), norm_vecs, 4, 0, 1
+    )
     w_one, w_two = assemble_ffn(ffn_pieces, yidx)
     gate_in = dot_nn(hidden_low, w_one) + bias_one
-    activated = bf(gelu(gate_in))
+    activated, slope = bf(gelu(gate_in)), bf(gelu_slope(gate_in))
     part = bf(dot_nt(activated, w_two))
-    dattn_pieces, part, lengths_sum = stage(
-        dattn_pieces, part, jnp.broadcast_to(wide(jnp.sum(lengths)), (8, 128))
-    )
-    ffn_sum = both_cores(part)
-    result, normed_two, inv_two = norm_forward(
-        hidden_one + ffn_sum + norm_vecs[5], norm_vecs[2], norm_vecs[3]
-    )
-    enc_low = bf(result)
+    self_pieces, cross_z, part, activated, slope = stage(
+        self_pieces, cross_z, part, activated, slope
+    )
+    cross_pieces = gather_plane(cross_z)
+    enc_low, normed_two, inv_two = add_norm(
+        (normed_one, (0, 1)), part, swap_core(part), norm_vecs, 5, 2, 3
+    )
     out_enc = lax.all_gather(after(my_half(enc_low), dffn_planes), "mp", axis=0, tiled=False)
 
-    frame_total = sum_dp(lengths_sum)[0, 0]
-    inverse = (1.0 / frame_total).reshape(1)
-    d_qkv, d_o, c_q, c_kv, c_o = assemble_attn(dattn_pieces, DEC_PLANS, 8, yidx)
-    dw_one, dw_two = assemble_planes(dffn_planes, yidx)
+    d_qkv, d_o = assemble_attn(self_pieces, ENC_PLANS, 4, yidx)
     dqkv = bf(dot_nn(text_in, d_qkv) + bias_dqkv)
     self_context, self_lse = attention_forward(dqkv, None, text_limit, None, True, True)
-    self_sum = both_cores(bf(dot_nt(self_context, d_o)))
-    dec_one, normed_d1, inv_d1 = norm_forward(
-        wide(text_in) + self_sum + dec_norm_vecs[6], dec_norm_vecs[0], dec_norm_vecs[1]
-    )
-    dec_one_low = bf(dec_one)
+    part, cross_pieces = stage(bf(dot_nt(self_context, d_o)), cross_pieces)
+    c_q, c_kv, c_o = assemble_attn(cross_pieces, CROSS_PLANS, 4, yidx)
+    dw_one, dw_two = assemble_planes(dffn_planes, yidx)
+    dec_one_low, normed_d1, inv_d1 = add_norm(
+        text_in, part, swap_core(part), dec_norm_vecs, 6, 0, 1
+    )
     cross_q = bf(dot_nn(dec_one_low, c_q) + bias_cq)
     cross_kv = bf(dot_nn(enc_low, c_kv) + bias_ckv)
     cross_context, cross_lse = attention_forward(cross_q, cross_kv, limit, None, False, False)
-    cross_sum = both_cores(bf(dot_nt(cross_context, c_o)))
-    dec_two, normed_d2, inv_d2 = norm_forward(
-        dec_one + cross_sum + dec_norm_vecs[7], dec_norm_vecs[2], dec_norm_vecs[3]
-    )
-    dec_two_low = bf(dec_two)
+    part = bf(dot_nt(cross_context, c_o))
+    dec_two_low, normed_d2, inv_d2 = add_norm(
+        (normed_d1, (0, 1)), part, swap_core(part), dec_norm_vecs, 7, 2, 3
+    )
     dec_gate = dot_nn(dec_two_low, dw_one) + bias_done
-    dec_act = bf(gelu(dec_gate))
-    dec_ffn_sum = both_cores(bf(dot_nt(dec_act, dw_two)))
-    dec_result, normed_d3, inv_d3 = norm_forward(
-        dec_two + dec_ffn_sum + dec_norm_vecs[8], dec_norm_vecs[4], dec_norm_vecs[5]
-    )
-
-    text_places = lax.broadcasted_iota(jnp.int32, (text_full, 1), 0)
-    dec_up = jnp.where(text_places < text_limit[0], wide(text_upstream), 0.0)
-    grad_d3, gain_d3, shift_d3 = norm_backward(dec_up, normed_d3, inv_d3, dec_norm_vecs[4])
-    dec_ffn_back = bf(grad_d3)
-    dec_gate_grad = bf(dot_nn(dec_ffn_back, dw_two) * gelu_slope(dec_gate))
+    dec_act, dec_slope = bf(gelu(dec_gate)), bf(gelu_slope(dec_gate))
+    part, dec_act, dec_slope = stage(bf(dot_nt(dec_act, dw_two)), dec_act, dec_slope)
+    dec_low, normed_d3, inv_d3 = add_norm(
+        (normed_d2, (2, 3)), part, swap_core(part), dec_norm_vecs, 8, 4, 5
+    )
+    grad_d3, dec_ffn_back, sums_d3 = norm_back(
+        [text_upstream], text_limit, normed_d3, inv_d3, dec_norm_vecs, 4
+    )
+    dec_gate_grad = bf(dot_nn(dec_ffn_back, dw_two) * wide(dec_slope))
     part = bf(dot_nt(dec_gate_grad, dw_one))
     dec_ffn_grads = [
         bf(dot_tn(dec_two_low, dec_gate_grad)),
         bf(dot_tn(dec_ffn_back, dec_act)),
     ]
-    dec_ffn_planes, part, sent, inverse = stage(
-        split_planes(dec_ffn_grads, n_dp, yidx), part, my_half(bf(dec_result)), inverse
+    dec_ffn_planes, part, sent, out_enc = stage(
+        split_planes(dec_ffn_grads, n_dp, yidx), part, my_half(dec_low), out_enc
     )
     dec_ffn_plane = scatter_dp(dec_ffn_planes)
     out_dec = to_owners(sent)
-    grad_h2 = grad_d3 + both_cores(part)
-
-    grad_d2, gain_d2, shift_d2 = norm_backward(grad_h2, normed_d2, inv_d2, dec_norm_vecs[2])
-    cross_back = bf(grad_d2)
-    cross_qg, cross_kvg = attention_backward(
+
+    grad_d2, cross_back, sums_d2 = norm_back(
+        [grad_d3, part, swap_core(part)], None, normed_d2, inv_d2, dec_norm_vecs, 2
+    )
+    cross_qg, cross_kvg, query_sum, memory_sum = attention_backward(
         cross_q,
         cross_kv,
         limit,
@@ -998,13 +1106,13 @@
         split_attn(cross_grads, CROSS_PLANS, 4, n_dp, yidx),
         out_dec,
     )
-    (out_dec,) = place_quarters(out_dec, owners, [text_half])
+    out_dec = place_quarters(out_dec, owners)
     cross_plane_back = scatter_plane(cross_parts)
-    memory_back = both_cores(memory_part)
-    grad_h1 = grad_d2 + both_cores(query_part)
-    grad_d1, gain_d1, shift_d1 = norm_backward(grad_h1, normed_d1, inv_d1, dec_norm_vecs[0])
-    self_back = bf(grad_d1)
-    (self_g,) = attention_backward(
+    memory_other = swap_core(memory_part)
+    grad_d1, self_back, sums_d1 = norm_back(
+        [grad_d2, query_part, swap_core(query_part)], None, normed_d1, inv_d1, dec_norm_vecs, 0
+    )
+    self_g, dec_sum = attention_backward(
         dqkv,
         None,
         text_limit,
@@ -1019,134 +1127,121 @@
     self_grads = [bf(dot_tn(text_in, self_g)), bf(dot_tn(self_back, self_context))]
     self_parts = split_attn(self_grads, ENC_PLANS, 4, n_dp, yidx)
 
-    places = lax.broadcasted_iota(jnp.int32, (full_len, 1), 0)
-    upstream = jnp.where(places < limit[0], wide(upstream_in), 0.0) + memory_back
-    grad_two, gain_two, shift_two = norm_backward(upstream, normed_two, inv_two, norm_vecs[2])
-    ffn_back = bf(grad_two)
-    gate_grad = bf(dot_nn(ffn_back, w_two) * gelu_slope(gate_in))
+    self_parts, memory_part, memory_other, cross_parts, cross_plane_back, text_part = stage(
+        self_parts, memory_part, memory_other, cross_parts, cross_plane_back, text_part
+    )
+    self_plane_back = scatter_plane(self_parts)
+    text_other = swap_core(text_part)
+    cross_total = scatter_dp(sum_plane(cross_parts, cross_plane_back, own))
+    grad_two, ffn_back, sums_two = norm_back(
+        [upstream_in, memory_part, memory_other], limit, normed_two, inv_two, norm_vecs, 2
+    )
+    gate_grad = bf(dot_nn(ffn_back, w_two) * wide(slope))
     ffn_grads = [bf(dot_tn(hidden_low, gate_grad)), bf(dot_tn(ffn_back, activated))]
-    part, text_part, self_parts, cross_parts, cross_plane_back, ffn_parts = stage(
+    part, self_parts, self_plane_back, ffn_parts, text_other = stage(
         bf(dot_nt(gate_grad, w_one)),
-        text_part,
         self_parts,
-        cross_parts,
-        cross_plane_back,
+        self_plane_back,
         split_ffn(ffn_grads, n_dp, yidx),
-    )
-    cross_total = scatter_dp(sum_plane(cross_parts, cross_plane_back, own))
+        text_other,
+    )
+    text_grad = my_half(grad_d1) + (wide(my_half(text_part)) + wide(my_half(text_other)))
+    self_total = scatter_dp(sum_plane(self_parts, self_plane_back, own))
     ffn_plane_back = scatter_plane(ffn_parts)
-    hidden_grad = grad_two + both_cores(part)
-    grad_one, gain_one, shift_one = norm_backward(hidden_grad, normed_one, inv_one, norm_vecs[0])
-    attn_back = bf(grad_one)
-    enc_g, diag = attention_backward(
+    grad_one, attn_back, sums_one = norm_back(
+        [grad_two, part, swap_core(part)], None, normed_one, inv_one, norm_vecs, 0
+    )
+    enc_g, enc_sum, diag = attention_backward(
         qkv, None, limit, bias, False, True, context, lse, bf(dot_nn(attn_back, w_o))
     )
-    self_parts, ffn_parts, ffn_plane_back, part, enc_g, diag, text_part, dec_ffn_plane = stage(
-        self_parts,
+    ffn_parts, ffn_plane_back, part, enc_g, diag, text_low, dec_ffn_plane = stage(
         ffn_parts,
         ffn_plane_back,
         bf(dot_nt(enc_g, w_qkv)),
         enc_g,
         diag,
-        text_part,
+        bf(text_grad),
         dec_ffn_plane,
     )
+    out_text_grad = to_owners(text_low)
     ffn_total = scatter_dp(sum_plane(ffn_parts, ffn_plane_back, own))
-    self_plane_back = scatter_plane(self_parts)
     plane_parts = [dec_ffn_plane[dx, a] for dx, a in ROUTES]
     dec_ffn_sums = scatter_plane(plane_parts)
-    input_grad = grad_one + both_cores(part)
+    input_grad = my_half(grad_one) + (wide(my_half(part)) + wide(my_half(swap_core(part))))
     attn_grads = [bf(dot_tn(inputs, enc_g)), bf(dot_tn(attn_back, context))]
     attn_parts = split_attn(attn_grads, ENC_PLANS, 4, n_dp, yidx)
     def col_sum(a):
-        return jnp.sum(a, axis=0, dtype=F32)
-
-    def pick(v, stride, at):
-        return jnp.concatenate(
-            [v[(j * stride + at) * PAIR : (j * stride + at + 1) * PAIR] for j in range(3)]
-        )
-
-    enc_sum, dec_sum, kv_sum = col_sum(enc_g), col_sum(self_g), col_sum(cross_kvg)
-    col_parts = [
-        group_cols(pick(enc_sum, 3, 0)),
-        group_cols(pick(enc_sum, 3, 2)),
-        jnp.split(col_sum(gate_grad), 2),
-        group_cols(pick(dec_sum, 3, 0)),
-        group_cols(pick(dec_sum, 3, 2)),
-        group_cols(col_sum(cross_qg)),
-        group_cols(pick(kv_sum, 2, 1)),
-        jnp.split(col_sum(dec_gate_grad), 2),
-    ]
-    turned = jnp.concatenate([diag[:, :, BLOCK:], diag[:, :, :BLOCK]], axis=-1)
-    span_count = 2 * blocks - 1
-    line_grad = sum(
-        jnp.pad(
-            turned[:, d],
-            ((0, 0), ((span_count - 1 - d) * BLOCK, d * BLOCK)),
-        )
-        for d in range(span_count)
-    )
-    first_bucket = jnp.sum(line_grad[:, lead + bucket_count :], axis=1, keepdims=True)
-    last_bucket = jnp.sum(line_grad[:, :lead], axis=1, keepdims=True)
-    head_grad = line_grad[:, lead : lead + bucket_count][:, ::-1]
-    head_grad = jnp.concatenate(
-        [
-            head_grad[:, :1] + first_bucket,
-            head_grad[:, 1:-1],
-            head_grad[:, -1:] + last_bucket,
-        ],
-        axis=1,
-    )
-    table_parts = (head_grad[jnp.array([0, 1, 4])], head_grad[jnp.array([2, 3, 5])])
-    norm_local = jnp.stack(
-        [gain_one, shift_one, gain_two, shift_two, jnp.sum(grad_one, 0), jnp.sum(grad_two, 0)]
-    )
-    dec_norm_local = jnp.stack(
-        [
-            gain_d1,
-            shift_d1,
-            gain_d2,
-            shift_d2,
-            gain_d3,
-            shift_d3,
-            jnp.sum(grad_d1, 0),
-            jnp.sum(grad_d2, 0),
-            jnp.sum(grad_d3, 0),
-        ]
-    )
-    shared = jnp.concatenate([norm_local.reshape(-1), dec_norm_local.reshape(-1)])
-    vectors = [
-        jnp.concatenate([p[dx] for p in col_parts] + [table_parts[dx].reshape(-1), shared])
-        for dx in range(2)
-    ]
-    self_parts, self_plane_back, attn_parts, input_grad, vectors, text_part, dec_ffn_sums = stage(
-        self_parts, self_plane_back, attn_parts, input_grad, vectors, text_part, dec_ffn_sums
-    )
-    self_total = scatter_dp(sum_plane(self_parts, self_plane_back, own))
+        return dot_nn(jnp.ones((8, a.shape[0]), BF16), a)
+
+    vectors = pack_small(
+        [sums_one, sums_two, sums_d1, sums_d2, sums_d3],
+        enc_sum,
+        dec_sum,
+        query_sum,
+        memory_sum,
+        [col_sum(gate_grad), col_sum(dec_gate_grad)],
+        diag,
+        bucket_count,
+    )
+    attn_parts, input_grad, vectors, out_text_grad, dec_ffn_sums = stage(
+        attn_parts, input_grad, vectors, out_text_grad, dec_ffn_sums
+    )
+    out_text_grad = place_quarters(out_text_grad, owners)
     attn_plane_back = scatter_plane(attn_parts)
-    text_grad = grad_d1 + both_cores(text_part)
     small = vectors[0] + swap_mp(vectors[1], 1)
     small = jnp.where(own, small, unspread(small, 0, 0))
-    small = small + swap_core(small)
-    attn_parts, attn_plane_back, small, input_grad, text_grad = stage(
-        attn_parts, attn_plane_back, small, input_grad, text_grad
-    )
-    attn_total = scatter_dp(sum_plane(attn_parts, attn_plane_back, own))
-    held_back = to_owners(jnp.concatenate([my_half(bf(input_grad)), my_half(bf(text_grad))]))
-    out_input_grad, out_text_grad = place_quarters(held_back, owners, [half_len, text_half])
     dec_attn_total = jnp.concatenate(
         [self_total[:4], cross_total[:4], self_total[4:], cross_total[4:]]
     )
-    small = sum_dp(small)
-    cut = [enc_cols, dec_cols, group_heads * bucket_count, norm_vecs.size, dec_norm_vecs.size]
-    ends = [sum(cut[: i + 1]) for i in range(len(cut))]
-    col_total, dec_col_total, table_total, norm_total, dec_norm_total, _ = jnp.split(small, ends)
-    table_total = table_total.reshape(group_heads, bucket_count).T
-    norm_total = norm_total.reshape(norm_vecs.shape)
-    dec_norm_total = dec_norm_total.reshape(dec_norm_vecs.shape)
-
     matrix_rate = MATRIX_RATE * root_frames
     vector_rate = VECTOR_RATE * root_frames
+    ffn_new = update_matrices(
+        [ffn_total],
+        None,
+        own_flag,
+        (ffn_master, ffn_moment, ffn_average),
+        matrix_rate,
+        inverse,
+        False,
+    )
+    dattn_new = update_matrices(
+        [dec_attn_total],
+        None,
+        own_flag,
+        (dec_attn_master, dec_attn_moment, dec_attn_average),
+        matrix_rate,
+        inverse,
+        True,
+    )
+    dffn_new = update_matrices(
+        dec_ffn_sums,
+        plane_parts[0],
+        own_flag,
+        (dec_ffn_master, dec_ffn_moment, dec_ffn_average),
+        matrix_rate,
+        inverse,
+        False,
+    )
+    small, out_dec, out_text_grad, *_ = stage(
+        small, out_dec, out_text_grad, ffn_new[4], dattn_new[4], dffn_new[4]
+    )
+    small = small + swap_core(small)
+    attn_parts, attn_plane_back, small, input_grad = stage(
+        attn_parts, attn_plane_back, small, input_grad
+    )
+    attn_total = scatter_dp(sum_plane(attn_parts, attn_plane_back, own))
+    out_input_grad = place_quarters(to_owners(bf(input_grad)), owners)
+    small = sum_dp(small)
+    def head_bias(i):
+        row, lane = NORM_ROWS + i // 3, (i % 3) * 2 * PAIR
+        return small[row, lane : lane + group_width]
+
+    norm_total = small[: norm_vecs.shape[0]]
+    dec_norm_total = small[norm_vecs.shape[0] : NORM_ROWS]
+    col_total = jnp.concatenate([head_bias(0), head_bias(1), small[NORM_ROWS + 2]])
+    dec_col_total = jnp.concatenate([head_bias(i) for i in range(2, 6)] + [small[NORM_ROWS + 3]])
+    table_total = small[NORM_ROWS + 4 : NORM_ROWS + 4 + group_heads, :bucket_count].T
+
     attn_new = update_matrices(
         [attn_total],
         None,
@@ -1155,33 +1250,6 @@
         matrix_rate,
         inverse,
         True,
-    )
-    ffn_new = update_matrices(
-        [ffn_total],
-        None,
-        own_flag,
-        (ffn_master, ffn_moment, ffn_average),
-        matrix_rate,
-        inverse,
-        False,
-    )
-    dattn_new = update_matrices(
-        [dec_attn_total],
-        None,
-        own_flag,
-        (dec_attn_master, dec_attn_moment, dec_attn_average),
-        matrix_rate,
-        inverse,
-        True,
-    )
-    dffn_new = update_matrices(
-        dec_ffn_sums,
-        plane_parts[0],
-        own_flag,
-        (dec_ffn_master, dec_ffn_moment, dec_ffn_average),
-        matrix_rate,
-        inverse,
-        False,
     )
     norm_new = update(norm_vecs, norm_moment, norm_average, norm_total, vector_rate, frame_total)
     col_new = update(col_bias, col_moment, col_average, col_total, vector_rate, frame_total)

time: 601 us -> 558 us (0.928)
  waiting for transfers between devices: 161 us -> 97 us
  Pallas kernels: 120 us -> 163 us
  other arithmetic: 72.2 us -> 41.5 us
  local copies, waits for them, and re-layouts: 61.8 us -> 38 us
  starting transfers between devices: 72.8 us -> 93.8 us
  matrix products: 69.4 us -> 76.6 us
    ppermute x21, waiting for transfers between devices: 66.2 us -> 19.8 us  [unspread(): lax.ppermute(v, ('seq', 'mp'), [(d, s) for s, d in spread_perm(dx, flip)])]
    pallas_call x9 -> x22, Pallas kernels: 44.8 us -> 84.9 us  [the longest x5 24.2 us: norm_back(): pl.pallas_call(kernel, in_specs=smem + [ON_CHIP] * (len(terms) + 3), out_...]
    reduce_sum x27 -> x2, other arithmetic: 30.8 us -> 2.07 us  [the longest x1 1.44 us: local(): jnp.sum(wide(dattn_z[:, -1, 0, 0]) * 256.0 + wide(dattn_z[:, -1, 1, 0]))]
    ppermute x18 -> x22, waiting for transfers between devices: 59.5 us -> 43.6 us  [spread(): return lax.ppermute(v, ('seq', 'mp'), spread_perm(dx, flip))]
    ppermute x13, starting transfers between devices: 5.77 us -> 18.5 us  [swap_core(): return lax.ppermute(v, 'seq', [(0, 1), (1, 0)])]
    unnamed x334 -> x269, local copies, waits for them, and re-layouts: 28.7 us -> 16.7 us
    dot_general x11 -> x13, matrix products: 21.2 us -> 28 us  [dot_nn(): return jnp.dot(left, right, preferred_element_type=F32)]
    ppermute x18 -> x22, starting transfers between devices: 28.9 us -> 33.6 us  [spread(): return lax.ppermute(v, ('seq', 'mp'), spread_perm(dx, flip))]
  transfers between devices with their start and end apart: 72 -> 77, of which waited for: 24 -> 22; matrix products, arithmetic and copies ran while one was open for 27% -> 25% of each run, Pallas kernels for 19% -> 29%
where the time goes in v3:
time: 558 us; the launch traced here: 547 us
  Pallas kernels  163 us (29%)
  waiting for transfers between devices  97 us (17%)
  starting transfers between devices  93.8 us (17%)
  matrix products  76.6 us (14%)
  other arithmetic  41.5 us (7%)
  local copies, waits for them, and re-layouts  38 us (7%)
  between operations  19.2 us (3%)
  blocking collectives  17.7 us (3%)
    ppermute x22, waiting for transfers between devices, spread(): return lax.ppermute(v, ('seq', 'mp'), spread_perm(dx, flip))  43.6 us
    ppermute x22, starting transfers between devices, spread(): return lax.ppermute(v, ('seq', 'mp'), spread_perm(dx, flip))  33.6 us
    pallas_call x3, Pallas kernels, attention_backward(): pl.pallas_call(kernel, grid_spec=pltpu.PrefetchScalarGridSpec(num_scalar_...  33.5 us
    dot_general x13, matrix products, dot_nn(): return jnp.dot(left, right, preferred_element_type=F32)  28 us
    ppermute x21, starting transfers between devices, unspread(): lax.ppermute(v, ('seq', 'mp'), [(d, s) for s, d in spread_perm(dx, flip)])  27.7 us
    dot_general x11, matrix products, dot_tn(): lax.dot_general(left, right, (((0,), (0,)), ((), ())), preferred_element_...  25.6 us
    pallas_call x5, Pallas kernels, norm_back(): pl.pallas_call(kernel, in_specs=smem + [ON_CHIP] * (len(terms) + 3), out_...  24.2 us
    dot_general x11, matrix products, dot_nt(): lax.dot_general(left, right, (((1,), (1,)), ((), ())), preferred_element_...  23 us
  transfers between devices with their start and end apart: 77, of which 22 were waited for; matrix products, arithmetic and copies ran while one was open for 25% of the time, Pallas kernels for 29%

profile of v3, /device:TPU:0, one launch (start us, length us, event | category | flops | bytes accessed | tf_op | source)
XLA Modules:
  0.0 547.0 jit_solution(5357893061340501121)
XLA Ops:
  14.9 3.9 collective-permute-start.4
  22.1 17.7 %all-gather = bf16[24,96,128]{2,1,0:T(8,128)(2,1)S(1)} all-gather(bf16[6,96,128]{2,1,0:T(8,128)(2,1)S(1)} %maximum_maximum_fusion), channel_id=2, replica_groups=mesh['dp'=4,'seq'=2,'mp'=4] {'dp'}, dimensions={0}, use_global_device_ids=true | all-gather | bytes 737280 | tf_op jit(solution)/shard_map/all_gather | solution.py:93
  53.5 6.6 %bias_tiles.1.refs_0_ = f32[6,5,256,256]{3,2,1,0:T(8,128)} custom-call(f32[6,1,1536]{2,1,0:T(1,128)} %broadcast_in_dim.27.line_ref), custom_call_target="tpu_custom_call" | custom-call | flops 15728640 | bytes 7864320 | tf_op jit(solution)/shard_map/bias_tiles/pallas_call | solution.py:339
  70.9 4.8 collective-permute-done.9.refs_3_
  83.4 3.8 assemble_attn.3
  90.4 14.5 %attend_enc.1 = (bf16[768,384]{1,0:T(8,128)(2,1)S(1)}, f32[3,8,768]{2,1,0:T(8,128)S(1)}) custom-call(s32[1]{0:T(128)} %dynamic_slice.49.limit_ref.refs_0_, bf16[768,1152]{1,0:T(8,128)(2,1)S(1)} %fusion.5.q_ref, f32[6,5,256,256]{3,2,1,0:T(8,128)} %bias_tiles.1.refs_0_), custom_call_target="tpu_custom_call" | custom-call | flops 1811939328 | bytes 2359296 | tf_op jit(solution)/shard_map/attend_enc/pallas_call | solution.py:453
  106.3 23.4 %collective-permute-done.13.refs_3_ = bf16[4,2,96,768]{3,2,1,0:T(8,128)(2,1)} collective-permute-done((bf16[4,2,96,768]{3,2,1,0:T(8,128)(2,1)}, bf16[4,2,96,768]{3,2,1,0:T(8,128)(2,1)}, u32[]{:S(2)}, u32[]{:S(2)}) %collective-permute-start.13) | collective-permute-done | bytes 1179680 | tf_op jit(solution)/shard_map/ppermute | solution.py:68
  141.3 5.6 %assemble_ffn.1 = (bf16[4,2,96,1536]{3,2,1,0:T(8,128)(2,1)}, bf16[4,2,96,1536]{3,2,1,0:T(8,128)(2,1)}) custom-call(s32[3]{0:T(128)} %pad_add_fusion.yi, bf16[4,2,96,768]{3,2,1,0:T(8,128)(2,1)} %bitcast.177, bf16[4,2,96,768]{3,2,1,0:T(8,128)(2,1)} %collective-permute-done.11.refs_1_, bf16[4,2,96,768]{3,2,1,0:T(8,128)(2,1)} %collective-permute-done.12.refs_2_, ...), custom_call_target="tpu_custom_call" | custom-call | bytes 10616832 | tf_op jit(solution)/shard_map/assemble_ffn/pallas_call | solution.py:223
  147.0 5.5 %add_norm.5 = (bf16[768,768]{1,0:T(8,128)(2,1)}, f32[768,768]{1,0:T(8,128)}, f32[768,128]{1,0:T(8,128)}) custom-call(bf16[768,768]{1,0:T(8,128)(2,1)} %copy-done.26, bf16[768,768]{1,0:T(8,128)(2,1)} %copy-done.28, bf16[768,768]{1,0:T(8,128)(2,1)} %collective-permute-done.19.q_ref, f32[6,768]{1,0:T(8,128)} %refs_5_.6), custom_call_target="tpu_custom_call" | custom-call | flops 7077888 | bytes 8257536 | tf_op jit(solution)/shard_map/add_norm/pallas_call | solution.py:640
  152.5 6.3 %fusion.4 = (bf16[768,1536]{1,0:T(8,128)(2,1)}, bf16[768,1536]{1,0:T(8,128)(2,1)S(1)}) fusion(f32[1536]{0:T(1024)S(1)} %pad_maximum_fusion.7, bf16[768,768]{1,0:T(8,128)(2,1)} %get-tuple-element.285, bf16[768,1536]{1,0:T(8,128)(2,1)} %bitcast.194), kind=kOutput, calls=%fused_computation.5 | convolution fusion | flops 1826095104 | bytes 8263680 | tf_op jit(solution)/shard_map/dot_general | solution.py:35
  174.8 3.7 assemble_attn.4
  185.2 8.8 %collective-permute-done.22.refs_3_ = bf16[4,6,96,128]{3,2,1,0:T(8,128)(2,1)} collective-permute-done((bf16[4,6,96,128]{3,2,1,0:T(8,128)(2,1)S(1)}, bf16[4,6,96,128]{3,2,1,0:T(8,128)(2,1)}, u32[]{:S(2)}, u32[]{:S(2)}) %collective-permute-start.22) | collective-permute-done | bytes 589856 | tf_op jit(solution)/shard_map/ppermute | solution.py:68
  197.6 3.7 assemble_attn.5
  204.8 6.0 %add_norm.7 = (bf16[768,768]{1,0:T(8,128)(2,1)}, f32[768,768]{1,0:T(8,128)}, f32[768,128]{1,0:T(8,128)}) custom-call(f32[768,768]{1,0:T(8,128)} %get-tuple-element.311.x_ref.refs_3_, bf16[768,768]{1,0:T(8,128)(2,1)} %convolution_convert_fusion.11.p_ref, bf16[768,768]{1,0:T(8,128)(2,1)} %collective-permute-done.25.q_ref, f32[6,768]{1,0:T(8,128)} %refs_5_.6), custom_call_target="tpu_custom_call" | custom-call | flops 7077888 | bytes 8257536 | tf_op jit(solution)/shard_map/add_norm/pallas_call | solution.py:640
  212.9 9.7 %all-gather.9.cloned.1.call-done.src = bf16[4,2,2,2,96,768]{5,4,3,2,1,0:T(8,128)(2,1)} async-done(((bf16[1,2,2,2,96,768]{5,4,3,2,1,0:T(8,128)(2,1)}), bf16[4,2,2,2,96,768]{5,4,3,2,1,0:T(8,128)(2,1)}) %all-gather.9.cloned.1.call-update) | async-done | bytes 4718608 | tf_op jit(solution)/shard_map/all_gather | solution.py:93
  225.4 4.6 attend_cross.1
  275.1 5.9 %attend_back_cross.1 = (bf16[256,384]{1,0:T(8,128)(2,1)S(1)}, bf16[768,768]{1,0:T(8,128)(2,1)S(1)}, f32[8,384]{1,0:T(8,128)S(1)}, f32[8,768]{1,0:T(8,128)S(1)}) custom-call(s32[1]{0:T(128)} %dynamic_slice.49.limit_ref.refs_0_, bf16[256,384]{1,0:T(8,128)(2,1)S(1)} %fusion.13.q_ref, bf16[768,768]{1,0:T(8,128)(2,1)S(1)} %copy-done.17, ...), custom_call_target="tpu_custom_call" | custom-call | flops 1509949440 | bytes 3145728 | tf_op jit(solution)/shard_map/attend_back_cross/pallas_call | solution.py:583
  285.7 3.5 split_attn.3
  322.9 4.0 collective-permute-done.37
  332.6 7.4 %norm_back.8 = (f32[768,768]{1,0:T(8,128)}, bf16[768,768]{1,0:T(8,128)(2,1)}, f32[8,768]{1,0:T(8,128)}) custom-call(s32[1]{0:T(128)} %dynamic_slice.49.limit_ref.refs_0_, bf16[768,768]{1,0:T(8,128)(2,1)} %pad_maximum_fusion.3.refs_1_, bf16[768,768]{1,0:T(8,128)(2,1)} %convolution_convert_fusion.8.refs_2_, bf16[768,768]{1,0:T(8,128)(2,1)} %collective-permute-done.33.refs_3_, ...), custom_call_target="tpu_custom_call" | custom-call | flops 9437184 | bytes 11796480 | tf_op jit(solution)/shard_map/norm_back/pallas_call | solution.py:688
  340.0 5.6 %convolution_convert_fusion = bf16[768,1536]{1,0:T(8,128)(2,1)} fusion(bf16[768,768]{1,0:T(8,128)(2,1)} %get-tuple-element.362, bf16[768,1536]{1,0:T(8,128)(2,1)} %copy-done.130), kind=kOutput, calls=%fused_computation.11 | convolution fusion | flops 1813118976 | bytes 5898240 | tf_op jit(solution)/shard_map/dot_general | solution.py:43
  347.6 3.5 convolution_convert_fusion.1
  353.8 4.9 split_ffn.1
  358.8 4.5 convolution_convert_fusion.10.refs_1_
  378.4 6.8 %norm_back.9 = (f32[768,768]{1,0:T(8,128)}, bf16[768,768]{1,0:T(8,128)(2,1)}, f32[8,768]{1,0:T(8,128)}) custom-call(f32[768,768]{1,0:T(8,128)} %get-tuple-element.379.refs_0_, bf16[768,768]{1,0:T(8,128)(2,1)} %copy-done.59, bf16[768,768]{1,0:T(8,128)(2,1)} %collective-permute-done.47.refs_2_, f32[768,768]{1,0:T(8,128)} %get-tuple-element.311.x_ref.refs_3_, ...), custom_call_target="tpu_custom_call" | custom-call | flops 9437184 | bytes 11796480 | tf_op jit(solution)/shard_map/norm_back/pallas_call | solution.py:688
  387.4 24.5 %attend_back_enc.1 = (bf16[768,1152]{1,0:T(8,128)(2,1)S(1)}, f32[8,1152]{1,0:T(8,128)S(1)}, f32[6,8,512]{2,1,0:T(8,128)S(1)}) custom-call(s32[1]{0:T(128)} %dynamic_slice.49.limit_ref.refs_0_, bf16[768,1152]{1,0:T(8,128)(2,1)S(1)} %copy-done.3, f32[6,5,256,256]{3,2,1,0:T(8,128)} %bias_tiles.1.refs_0_, bf16[768,384]{1,0:T(8,128)(2,1)S(1)} %get-tuple-element.280.refs_1_, ...), custom_call_target="tpu_custom_call" | custom-call | flops 4529848320 | bytes 4718592 | tf_op jit(solution)/shard_map/attend_back_enc/pallas_call | solution.py:583
  414.8 9.0 %collective-permute-done.44 = bf16[4,2,96,768]{3,2,1,0:T(8,128)(2,1)} collective-permute-done((bf16[4,2,96,768]{3,2,1,0:T(8,128)(2,1)}, bf16[4,2,96,768]{3,2,1,0:T(8,128)(2,1)}, u32[]{:S(2)}, u32[]{:S(2)}) %collective-permute-start.44) | collective-permute-done | bytes 1179680 | tf_op jit(solution)/shard_map/ppermute | solution.py:72
  426.2 4.5 add_convert_fusion
  466.7 4.2 collective-permute-start.57
  475.7 4.3 update_matrices.5
  488.1 13.3 %collective-permute-start.62 = (f32[24,768]{1,0:T(8,128)S(1)}, f32[24,768]{1,0:T(8,128)S(1)}, u32[]{:S(2)}, u32[]{:S(2)}) collective-permute-start(f32[24,768]{1,0:T(8,128)S(1)} %broadcast_select_fusion.8), channel_id=1, source_target_pairs={{0,4},{4,0},{1,5},{5,1},{2,6},{6,2},{3,7},{7,3},{8,12},{12,8},{9,1... | collective-permute-start | bytes 221192 | tf_op jit(solution)/shard_map/ppermute | solution.py:47
  520.9 11.4 %collective-permute-done.64.refs_2_ = bf16[384,768]{1,0:T(8,128)(2,1)S(1)} collective-permute-done((bf16[384,768]{1,0:T(8,128)(2,1)S(1)}, bf16[384,768]{1,0:T(8,128)(2,1)S(1)}, u32[]{:S(2)}, u32[]{:S(2)}) %collective-permute-start.64) | collective-permute-done | bytes 589856 | tf_op jit(solution)/shard_map/ppermute | solution.py:51
  (563 shorter events, 282.0 us)
Async XLA Ops:
  7.2 63.7 %all-gather.11.cloned.1.call-start = ((), (), s32[]{:S(2)}) async-start(), calls=%async_computation.11 | async-start | bytes 1474560 | tf_op jit(solution)/shard_map/all_gather | solution.py:93
  9.8 30.9 %collective-permute-start = (bf16[1024,768]{1,0:T(8,128)(2,1)S(1)}, bf16[1024,768]{1,0:T(8,128)(2,1)}, u32[]{:S(2)}, u32[]{:S(2)}) collective-permute-start(bf16[1024,768]{1,0:T(8,128)(2,1)S(1)} %pad_maximum_fusion), channel_id=1, source_target_pairs={{0,4},{4,0},{1,5},{5,1},{2,6},{6,2},{3,7},{7,3},{8,12},{12,8},{9,1... | collective-permute-start | bytes 4718600 | tf_op jit(solution)/shard_map/ppermute | solution.py:47
  40.6 90.6 %all-gather.13.cloned.1.call-start = ((), (), s32[]{:S(2)}) async-start(), calls=%async_computation.12 | async-start | bytes 1597440 | tf_op jit(solution)/shard_map/all_gather | solution.py:93
  47.8 27.9 %collective-permute-start.9 = (bf16[4,6,96,128]{3,2,1,0:T(8,128)(2,1)S(1)}, bf16[4,6,96,128]{3,2,1,0:T(8,128)(2,1)}, u32[]{:S(2)}, u32[]{:S(2)}) collective-permute-start(bf16[4,6,96,128]{3,2,1,0:T(8,128)(2,1)S(1)} %bitcast.166), channel_id=1, source_target_pairs={{0,1},{1,0},{2,5},{3,4},{4,3},{5,2},{6,7},{7,6},{8,9},{9,8},{10,13... | collective-permute-start | bytes 1769480 | tf_op jit(solution)/shard_map/ppermute | solution.py:68
  75.7 146.8 %all-gather.9.cloned.1.call-start = ((), (), s32[]{:S(2)}) async-start(), calls=%async_computation.5 | async-start | bytes 5898240 | tf_op jit(solution)/shard_map/all_gather | solution.py:93
  75.8 30.6 %collective-permute-start.14 = (bf16[4,2,96,768]{3,2,1,0:T(8,128)(2,1)}, bf16[4,2,96,768]{3,2,1,0:T(8,128)(2,1)}, u32[]{:S(2)}, u32[]{:S(2)}) collective-permute-start(bf16[4,2,96,768]{3,2,1,0:T(8,128)(2,1)} %bitcast.173), channel_id=1, source_target_pairs={{0,3},{1,2},{2,7},{3,6},{4,1},{5,0},{6,5},{7,4},{8,11},{9,10},{10,... | collective-permute-start | bytes 3538952 | tf_op jit(solution)/shard_map/ppermute | solution.py:68
  78.6 51.1 %collective-permute-start.13 = (bf16[4,2,96,768]{3,2,1,0:T(8,128)(2,1)}, bf16[4,2,96,768]{3,2,1,0:T(8,128)(2,1)}, u32[]{:S(2)}, u32[]{:S(2)}) collective-permute-start(bf16[4,2,96,768]{3,2,1,0:T(8,128)(2,1)} %bitcast.174), channel_id=1, source_target_pairs={{0,1},{1,0},{2,5},{3,4},{4,3},{5,2},{6,7},{7,6},{8,9},{9,8},{10,13... | collective-permute-start | bytes 3538952 | tf_op jit(solution)/shard_map/ppermute | solution.py:68
  80.5 50.8 %collective-permute-start.12 = (bf16[4,2,96,768]{3,2,1,0:T(8,128)(2,1)}, bf16[4,2,96,768]{3,2,1,0:T(8,128)(2,1)}, u32[]{:S(2)}, u32[]{:S(2)}) collective-permute-start(bf16[4,2,96,768]{3,2,1,0:T(8,128)(2,1)} %bitcast.175), channel_id=1, source_target_pairs={{0,2},{1,3},{2,6},{3,7},{4,0},{5,1},{6,4},{7,5},{8,10},{9,11},{10,... | collective-permute-start | bytes 3538952 | tf_op jit(solution)/shard_map/ppermute | solution.py:68
  80.5 50.8 %collective-permute-start.11 = (bf16[4,2,96,768]{3,2,1,0:T(8,128)(2,1)}, bf16[4,2,96,768]{3,2,1,0:T(8,128)(2,1)}, u32[]{:S(2)}, u32[]{:S(2)}) collective-permute-start(bf16[4,2,96,768]{3,2,1,0:T(8,128)(2,1)} %bitcast.176), channel_id=1, source_target_pairs={{2,4},{3,5},{4,2},{5,3},{10,12},{11,13},{12,10},{13,11},{18,20},{1... | collective-permute-start | bytes 3538952 | tf_op jit(solution)/shard_map/ppermute | solution.py:68
  131.3 133.3 %all-gather.15.cloned.1.call-start = ((), (), s32[]{:S(2)}) async-start(), calls=%async_computation.13 | async-start | bytes 2949120 | tf_op jit(solution)/shard_map/all_gather | solution.py:1045
  171.8 33.0 %collective-permute-start.25 = (bf16[768,768]{1,0:T(8,128)(2,1)}, bf16[768,768]{1,0:T(8,128)(2,1)}, u32[]{:S(2)}, u32[]{:S(2)}) collective-permute-start(bf16[768,768]{1,0:T(8,128)(2,1)} %convolution_convert_fusion.11.p_ref), channel_id=1, source_target_pairs={{0,4},{4,0},{1,5},{5,1},{2,6},{6,2},{3,7},{7,3},{8,12},{12,8},{9,1... | collective-permute-start | bytes 3538952 | tf_op jit(solution)/shard_map/ppermute | solution.py:47
  222.6 203.7 %reduce-scatter.6.cloned.1.call-start = ((), (), s32[]{:S(2)}) async-start(), calls=%async_computation.6 | async-start | bytes 5898240 | tf_op jit(solution)/shard_map/reduce_scatter | solution.py:97
  264.6 168.2 %reduce-scatter.12.cloned.1.call-start = ((), (), s32[]{:S(2)}) async-start(), calls=%async_computation.9 | async-start | bytes 737280 | tf_op jit(solution)/shard_map/reduce_scatter | solution.py:97
  265.9 27.2 %collective-permute-start.31 = (bf16[128,768]{1,0:T(8,128)(2,1)}, bf16[128,768]{1,0:T(8,128)(2,1)}, u32[]{:S(2)}, u32[]{:S(2)}) collective-permute-start(bf16[128,768]{1,0:T(8,128)(2,1)} %constant_dynamic-slice_fusion.1.refs_0_), channel_id=1, source_target_pairs={{0,3},{1,2},{2,1},{3,0},{4,7},{5,6},{6,5},{7,4},{8,11},{9,10},{10,... | collective-permute-start | bytes 589832 | tf_op jit(solution)/shard_map/ppermute | solution.py:51
  293.2 33.7 %collective-permute-start.33 = (bf16[768,768]{1,0:T(8,128)(2,1)}, bf16[768,768]{1,0:T(8,128)(2,1)}, u32[]{:S(2)}, u32[]{:S(2)}) collective-permute-start(bf16[768,768]{1,0:T(8,128)(2,1)} %convolution_convert_fusion.8.refs_2_), channel_id=1, source_target_pairs={{0,4},{4,0},{1,5},{5,1},{2,6},{6,2},{3,7},{7,3},{8,12},{12,8},{9,1... | collective-permute-start | bytes 3538952 | tf_op jit(solution)/shard_map/ppermute | solution.py:47
  326.9 36.4 %collective-permute-start.42 = (bf16[256,768]{1,0:T(8,128)(2,1)}, bf16[256,768]{1,0:T(8,128)(2,1)}, u32[]{:S(2)}, u32[]{:S(2)}) collective-permute-start(bf16[256,768]{1,0:T(8,128)(2,1)} %convolution_convert_fusion.17), channel_id=1, source_target_pairs={{0,4},{4,0},{1,5},{5,1},{2,6},{6,2},{3,7},{7,3},{8,12},{12,8},{9,1... | collective-permute-start | bytes 1179656 | tf_op jit(solution)/shard_map/ppermute | solution.py:47
  327.0 36.2 %collective-permute-start.38 = (bf16[4,6,96,128]{3,2,1,0:T(8,128)(2,1)}, bf16[4,6,96,128]{3,2,1,0:T(8,128)(2,1)S(1)}, u32[]{:S(2)}, u32[]{:S(2)}) collective-permute-start(bf16[4,6,96,128]{3,2,1,0:T(8,128)(2,1)} %get-tuple-element.429), channel_id=1, source_target_pairs={{4,2},{5,3},{2,4},{3,5},{12,10},{13,11},{10,12},{11,13},{20,18},{2... | collective-permute-start | bytes 1769480 | tf_op jit(solution)/shard_map/ppermute | solution.py:72
  327.7 35.6 %collective-permute-start.39 = (bf16[4,6,96,128]{3,2,1,0:T(8,128)(2,1)}, bf16[4,6,96,128]{3,2,1,0:T(8,128)(2,1)}, u32[]{:S(2)}, u32[]{:S(2)}) collective-permute-start(bf16[4,6,96,128]{3,2,1,0:T(8,128)(2,1)} %get-tuple-element.365), channel_id=1, source_target_pairs={{2,0},{3,1},{6,2},{7,3},{0,4},{1,5},{4,6},{5,7},{10,8},{11,9},{14,... | collective-permute-start | bytes 1769480 | tf_op jit(solution)/shard_map/ppermute | solution.py:72
  329.5 33.8 %collective-permute-start.40 = (bf16[4,6,96,128]{3,2,1,0:T(8,128)(2,1)}, bf16[4,6,96,128]{3,2,1,0:T(8,128)(2,1)}, u32[]{:S(2)}, u32[]{:S(2)}) collective-permute-start(bf16[4,6,96,128]{3,2,1,0:T(8,128)(2,1)} %get-tuple-element.366), channel_id=1, source_target_pairs={{1,0},{0,1},{5,2},{4,3},{3,4},{2,5},{7,6},{6,7},{9,8},{8,9},{13,10... | collective-permute-start | bytes 1769480 | tf_op jit(solution)/shard_map/ppermute | solution.py:72
  331.0 32.4 %collective-permute-start.41 = (bf16[4,6,96,128]{3,2,1,0:T(8,128)(2,1)}, bf16[4,6,96,128]{3,2,1,0:T(8,128)(2,1)}, u32[]{:S(2)}, u32[]{:S(2)}) collective-permute-start(bf16[4,6,96,128]{3,2,1,0:T(8,128)(2,1)} %get-tuple-element.367), channel_id=1, source_target_pairs={{3,0},{2,1},{7,2},{6,3},{1,4},{0,5},{5,6},{4,7},{11,8},{10,9},{15,... | collective-permute-start | bytes 1769480 | tf_op jit(solution)/shard_map/ppermute | solution.py:72
  358.7 77.1 %reduce-scatter.10.cloned.1.call-start = ((), (), s32[]{:S(2)}) async-start(), calls=%async_computation.8 | async-start | bytes 737280 | tf_op jit(solution)/shard_map/reduce_scatter | solution.py:97
  369.0 45.8 %collective-permute-start.43 = (bf16[4,2,96,768]{3,2,1,0:T(8,128)(2,1)}, bf16[4,2,96,768]{3,2,1,0:T(8,128)(2,1)}, u32[]{:S(2)}, u32[]{:S(2)}) collective-permute-start(bf16[4,2,96,768]{3,2,1,0:T(8,128)(2,1)} %get-tuple-element.423), channel_id=1, source_target_pairs={{4,2},{5,3},{2,4},{3,5},{12,10},{13,11},{10,12},{11,13},{20,18},{2... | collective-permute-start | bytes 3538952 | tf_op jit(solution)/shard_map/ppermute | solution.py:72
  370.7 53.1 %collective-permute-start.44 = (bf16[4,2,96,768]{3,2,1,0:T(8,128)(2,1)}, bf16[4,2,96,768]{3,2,1,0:T(8,128)(2,1)}, u32[]{:S(2)}, u32[]{:S(2)}) collective-permute-start(bf16[4,2,96,768]{3,2,1,0:T(8,128)(2,1)} %get-tuple-element.375), channel_id=1, source_target_pairs={{2,0},{3,1},{6,2},{7,3},{0,4},{1,5},{4,6},{5,7},{10,8},{11,9},{14,... | collective-permute-start | bytes 3538952 | tf_op jit(solution)/shard_map/ppermute | solution.py:72
  371.5 52.3 %collective-permute-start.45 = (bf16[4,2,96,768]{3,2,1,0:T(8,128)(2,1)}, bf16[4,2,96,768]{3,2,1,0:T(8,128)(2,1)}, u32[]{:S(2)}, u32[]{:S(2)}) collective-permute-start(bf16[4,2,96,768]{3,2,1,0:T(8,128)(2,1)} %get-tuple-element.376), channel_id=1, source_target_pairs={{1,0},{0,1},{5,2},{4,3},{3,4},{2,5},{7,6},{6,7},{9,8},{8,9},{13,10... | collective-permute-start | bytes 3538952 | tf_op jit(solution)/shard_map/ppermute | solution.py:72
  372.9 53.3 %collective-permute-start.46 = (bf16[4,2,96,768]{3,2,1,0:T(8,128)(2,1)}, bf16[4,2,96,768]{3,2,1,0:T(8,128)(2,1)}, u32[]{:S(2)}, u32[]{:S(2)}) collective-permute-start(bf16[4,2,96,768]{3,2,1,0:T(8,128)(2,1)} %get-tuple-element.377), channel_id=1, source_target_pairs={{3,0},{2,1},{7,2},{6,3},{1,4},{0,5},{5,6},{4,7},{11,8},{10,9},{15,... | collective-permute-start | bytes 3538952 | tf_op jit(solution)/shard_map/ppermute | solution.py:72
  378.1 107.2 %reduce-scatter.8.cloned.1.call-start = ((), (), s32[]{:S(2)}) async-start(), calls=%async_computation.7 | async-start | bytes 1474560 | tf_op jit(solution)/shard_map/reduce_scatter | solution.py:97
  430.7 105.6 %reduce-scatter.14.cloned.1.call-start = ((), (), s32[]{:S(2)}) async-start(), calls=%async_computation.10 | async-start | bytes 737280 | tf_op jit(solution)/shard_map/reduce_scatter | solution.py:97
  466.0 36.3 %collective-permute-start.56 = (bf16[4,6,96,128]{3,2,1,0:T(8,128)(2,1)S(1)}, bf16[4,6,96,128]{3,2,1,0:T(8,128)(2,1)S(1)}, u32[]{:S(2)}, u32[]{:S(2)}) collective-permute-start(bf16[4,6,96,128]{3,2,1,0:T(8,128)(2,1)S(1)} %copy-done.68), channel_id=1, source_target_pairs={{4,2},{5,3},{2,4},{3,5},{12,10},{13,11},{10,12},{11,13},{20,18},{2... | collective-permute-start | bytes 1769480 | tf_op jit(solution)/shard_map/ppermute | solution.py:72
  466.7 35.6 %collective-permute-start.57 = (bf16[4,6,96,128]{3,2,1,0:T(8,128)(2,1)}, bf16[4,6,96,128]{3,2,1,0:T(8,128)(2,1)S(1)}, u32[]{:S(2)}, u32[]{:S(2)}) collective-permute-start(bf16[4,6,96,128]{3,2,1,0:T(8,128)(2,1)} %get-tuple-element.410), channel_id=1, source_target_pairs={{2,0},{3,1},{6,2},{7,3},{0,4},{1,5},{4,6},{5,7},{10,8},{11,9},{14,... | collective-permute-start | bytes 1769480 | tf_op jit(solution)/shard_map/ppermute | solution.py:72
  471.0 31.4 %collective-permute-start.58 = (bf16[4,6,96,128]{3,2,1,0:T(8,128)(2,1)}, bf16[4,6,96,128]{3,2,1,0:T(8,128)(2,1)S(1)}, u32[]{:S(2)}, u32[]{:S(2)}) collective-permute-start(bf16[4,6,96,128]{3,2,1,0:T(8,128)(2,1)} %get-tuple-element.411), channel_id=1, source_target_pairs={{1,0},{0,1},{5,2},{4,3},{3,4},{2,5},{7,6},{6,7},{9,8},{8,9},{13,10... | collective-permute-start | bytes 1769480 | tf_op jit(solution)/shard_map/ppermute | solution.py:72
  471.6 30.9 %collective-permute-start.59 = (bf16[4,6,96,128]{3,2,1,0:T(8,128)(2,1)}, bf16[4,6,96,128]{3,2,1,0:T(8,128)(2,1)}, u32[]{:S(2)}, u32[]{:S(2)}) collective-permute-start(bf16[4,6,96,128]{3,2,1,0:T(8,128)(2,1)} %get-tuple-element.412), channel_id=1, source_target_pairs={{3,0},{2,1},{7,2},{6,3},{1,4},{0,5},{5,6},{4,7},{11,8},{10,9},{15,... | collective-permute-start | bytes 1769480 | tf_op jit(solution)/shard_map/ppermute | solution.py:72
  503.6 28.7 %collective-permute-start.64 = (bf16[384,768]{1,0:T(8,128)(2,1)S(1)}, bf16[384,768]{1,0:T(8,128)(2,1)S(1)}, u32[]{:S(2)}, u32[]{:S(2)}) collective-permute-start(bf16[384,768]{1,0:T(8,128)(2,1)S(1)} %add_add_fusion.refs_0_), channel_id=1, source_target_pairs={{0,2},{1,3},{2,0},{3,1},{4,6},{5,7},{6,4},{7,5},{8,10},{9,11},{10,... | collective-permute-start | bytes 1769480 | tf_op jit(solution)/shard_map/ppermute | solution.py:51
  (176 other events, 1940.8 us)
Sparse Core Ops, SparseCore 0:
  40.8 30.0 all-gather.10
  75.8 33.5 all-gather.12
  131.4 91.0 all-gather.8
  224.8 36.1 all-gather.14
  264.8 83.7 reduce-scatter.5
  358.8 20.3 reduce-scatter.11
  382.1 20.4 reduce-scatter.9
  430.9 27.4 reduce-scatter.7
  512.3 20.3 reduce-scatter.13
